TPU v7x, 128 devices: a whole 4x4x4 slice. The times are simulated.
128 devices in a mesh: row: 16 (over x_hi, y, core), col: 8 (over x_lo, z).
Axes of the slice: x: 4 (x_hi: 2, x_lo: 2; x = x_hi * 2 + x_lo), y: 4, z: 4, core: 2. Of those that a mesh axis runs over, the one named last changes fastest.
Arguments:
- points: bfloat16 [65536, 128], P(('row', 'col')), may hold values from -6 to 6
- probes: bfloat16 [65536, 128], P(('row', 'col')), may hold values from -6 to 6
Outputs:
- sketch: float32 [65536, 128], P(('row', 'col'))
- basis: float32 [65536, 128], P(('row', 'col'))
All inputs are finite; a program needn't handle non-finite values.
Results may differ from a plain program's by a relative error of at most 0.0044.
Values may be sent and summed in bfloat16 or wider, within the bound.
No kernel may reach another device: no remote copies, remote signals or barrier semaphores. Data moves between devices by JAX's collectives and lax.ppermute only.
A program may use at most 64 MiB of HBM per device.

v0:
```python
import math

import jax
import jax.numpy as jnp
from jax import lax
from jax.experimental import pallas as pl
from jax.experimental.pallas import tpu as pltpu
from jax.sharding import PartitionSpec as P

AXES = ("row", "col")
SIDE = 4
BLK = 512
DIM = 128
NPTS = BLK * 2 * SIDE ** 3
TI = 256
TJ = 1024
SCALE = -3.0 / DIM * math.log2(math.e)
VMEM = pl.BlockSpec(memory_space=pltpu.VMEM)
PARAMS = pltpu.CompilerParams(vmem_limit_bytes=56 << 20)


def index(x, y, z, k):
    x, y, z = x % SIDE, y % SIDE, z % SIDE
    return ((x // 2) * 8 + y * 2 + k) * 8 + (x % 2) * 4 + z


def fetch(value, source):
    pairs = []
    for x in range(SIDE):
        for y in range(SIDE):
            for z in range(SIDE):
                for k in range(2):
                    pairs.append((index(*source(x, y, z, k)), index(x, y, z, k)))
    return lax.ppermute(value, AXES, sorted(pairs))


def swap(value):
    return fetch(value, lambda x, y, z, k: (x, y, z, 1 - k))


def from_x(value, step):
    return fetch(value, lambda x, y, z, k: (x + step, y, z, k))


def from_y(value, step):
    return fetch(value, lambda x, y, z, k: (x, y + step, z, k))


def from_z(value, step):
    return fetch(value, lambda x, y, z, k: (x, y, z + step, k))


def first_leg(value, step):
    return fetch(value, lambda x, y, z, k: (x + step * (1 - k), y + step * k, z, k))


def second_leg(value, step):
    return fetch(value, lambda x, y, z, k: (x + step * k, y + step * (1 - k), z, k))


def pack_body(pts_ref, prb_ref, out_ref):
    out_ref[:, :DIM] = pts_ref[...]
    for c in range(BLK // DIM):
        rows = slice(c * DIM, (c + 1) * DIM)
        out_ref[rows, DIM:] = prb_ref[rows, :].astype(jnp.float32).T.astype(jnp.bfloat16)


def pack(points, probes):
    return pl.pallas_call(
        pack_body,
        out_shape=jax.ShapeDtypeStruct((BLK, 2 * DIM), jnp.bfloat16),
        in_specs=[VMEM, VMEM],
        out_specs=VMEM,
        compiler_params=PARAMS,
        name="pack",
    )(points, probes)


def norm_columns(pts, ones_first):
    total = jnp.sum(pts * pts, axis=1, keepdims=True)
    high = total.astype(jnp.bfloat16).astype(jnp.float32)
    rest = total - high
    mid = rest.astype(jnp.bfloat16).astype(jnp.float32)
    low = rest - mid
    lane = lax.broadcasted_iota(jnp.int32, pts.shape, 1)
    at = 3 if ones_first else 0
    ones = (lane < 3) if ones_first else ((lane >= 3) & (lane < 6))
    cols = jnp.where(ones, 1.0, 0.0)
    cols = jnp.where(lane == at + 2, low, cols)
    cols = jnp.where(lane == at + 1, mid, cols)
    cols = jnp.where(lane == at, high, cols)
    return cols.astype(jnp.bfloat16)


def sketch_part(islots, jblocks, acc, last, unroll, name):
    m, n = len(islots), len(jblocks)
    first = acc is None
    irows = sum(v.shape[0] for v in islots)
    jrows = sum(v.shape[0] for v in jblocks)
    half = irows // 2

    def body(*refs):
        irefs, jrefs = refs[:m], refs[m:m + n]
        pos = m + n
        acc_ref = None
        if not first:
            acc_ref = refs[pos]
            pos += 1
        nout = 2 if last else 1
        outs = refs[pos:pos + nout]
        ia, ja, pt = refs[pos + nout:]
        at = 0
        for ref in irefs:
            for lo in range(0, ref.shape[0], BLK):
                pts = ref[lo:lo + BLK, :]
                ia[at:at + BLK, :DIM] = pts
                ia[at:at + BLK, DIM:] = norm_columns(pts.astype(jnp.float32), True)
                at += BLK
        at = 0
        for ref in jrefs:
            for lo in range(0, ref.shape[0], BLK):
                pts = ref[lo:lo + BLK, :DIM].astype(jnp.float32)
                ja[at:at + BLK, :DIM] = (pts * -2.0).astype(jnp.bfloat16)
                ja[at:at + BLK, DIM:] = norm_columns(pts, False)
                for c in range(0, BLK, DIM):
                    pt[:, at + c:at + c + DIM] = ref[lo + c:lo + c + DIM, DIM:]
                at += BLK
        spans = [(lo, min(lo + TJ, jrows)) for lo in range(0, jrows, TJ)]

        def tile(t, total):
            a = ia[pl.ds(pl.multiple_of(t * TI, TI), TI), :]

            def dist(span):
                return lax.dot_general(
                    ja[span[0]:span[1], :], a, (((1,), (1,)), ((), ())),
                    preferred_element_type=jnp.float32)

            now = dist(spans[0])
            for q, span in enumerate(spans):
                ahead = dist(spans[q + 1]) if q + 1 < len(spans) else None
                kern = jnp.exp2(now * SCALE).astype(jnp.bfloat16)
                total = total + jnp.dot(pt[:, span[0]:span[1]], kern, preferred_element_type=jnp.float32)
                now = ahead
            return total

        def start(t):
            return jnp.zeros((DIM, TI), jnp.float32) if first else acc_ref[t]

        if not last:
            def step(t, carry):
                outs[0][t] = tile(t, start(t))
                return carry
            lax.fori_loop(0, irows // TI, step, 0, unroll=unroll)
        else:
            for part in range(2):
                base = part * (half // TI)

                def step(t, carry, part=part, base=base):
                    done = tile(t + base, start(t + base))
                    outs[part][pl.ds(pl.multiple_of(t * TI, TI), TI), :] = done.T
                    return carry
                lax.fori_loop(0, half // TI, step, 0, unroll=unroll)

    if last:
        shape = [jax.ShapeDtypeStruct((half, DIM), jnp.float32)] * 2
        specs = [VMEM, VMEM]
    else:
        shape = jax.ShapeDtypeStruct((irows // TI, DIM, TI), jnp.float32)
        specs = VMEM
    ops = list(islots) + list(jblocks) + ([] if first else [acc])
    return pl.pallas_call(
        body,
        out_shape=shape,
        in_specs=[VMEM] * len(ops),
        out_specs=specs,
        scratch_shapes=[
            pltpu.VMEM((irows, 2 * DIM), jnp.bfloat16),
            pltpu.VMEM((jrows, 2 * DIM), jnp.bfloat16),
            pltpu.VMEM((DIM, jrows), jnp.bfloat16),
        ],
        compiler_params=PARAMS,
        cost_estimate=pl.CostEstimate(
            flops=irows * jrows * DIM * 6, transcendentals=irows * jrows,
            bytes_accessed=(irows + jrows) * DIM * 8),
        name=name,
    )(*ops)


def gram_body(keep_ref, got_ref, back_ref, out_ref, gram_ref):
    rows = (keep_ref[...] + got_ref[...]) + back_ref[...]
    out_ref[...] = rows
    gram_ref[...] = lax.dot_general(
        rows, rows, (((0,), (0,)), ((), ())),
        precision=lax.Precision.HIGHEST, preferred_element_type=jnp.float32)


def finish_rows(*parts):
    return pl.pallas_call(
        gram_body,
        out_shape=[
            jax.ShapeDtypeStruct((BLK, DIM), jnp.float32),
            jax.ShapeDtypeStruct((DIM, DIM), jnp.float32),
        ],
        in_specs=[VMEM] * 3,
        out_specs=[VMEM, VMEM],
        compiler_params=PARAMS,
        name="finish_rows",
    )(*parts)


def basis_body(gram_ref, rows_ref, out_ref, work):
    work[:, :DIM] = gram_ref[...]
    at_row = lax.broadcasted_iota(jnp.int32, (DIM, DIM), 0)
    at_col = lax.broadcasted_iota(jnp.int32, (DIM, DIM), 1)
    work[:, DIM:] = (at_row == at_col).astype(jnp.float32)
    sub = lax.broadcasted_iota(jnp.int32, (8, DIM), 0)

    def row(v, i):
        return jnp.broadcast_to(v[i:i + 1, :], (8, DIM))

    inverse = []
    for lo in range(0, DIM, 8):
        left, right = work[lo:lo + 8, :DIM], work[lo:lo + 8, DIM:]
        cols = [jnp.broadcast_to(left[:, lo + i:lo + i + 1], (8, DIM)) for i in range(8)]
        for i in range(8):
            scale = lax.rsqrt(row(cols[i], i))
            c = cols[i] * scale
            for q in range(i + 1, 8):
                cols[q] = cols[q] - c * row(c, q)
            below = jnp.where(sub > i, c, 0.0)
            pivot = row(left, i) * scale
            left = jnp.where(sub == i, pivot, left - below * pivot)
            pivot = row(right, i) * scale
            right = jnp.where(sub == i, pivot, right - below * pivot)
        inverse.append(right)
        turned = left.T
        for r in range(lo + 8, DIM, 8):
            a, b = work[r:r + 8, :DIM], work[r:r + 8, DIM:]
            for i in range(8):
                c = jnp.broadcast_to(turned[r:r + 8, i:i + 1], (8, DIM))
                a = a - c * left[i:i + 1, :]
                b = b - c * right[i:i + 1, :]
            work[r:r + 8, :DIM] = a
            work[r:r + 8, DIM:] = b
    inv = jnp.concatenate(inverse, axis=0) * math.sqrt(NPTS)
    out_ref[...] = lax.dot_general(
        rows_ref[...], inv, (((1,), (1,)), ((), ())),
        precision=lax.Precision.HIGHEST, preferred_element_type=jnp.float32)


def make_basis(gram, rows):
    return pl.pallas_call(
        basis_body,
        out_shape=jax.ShapeDtypeStruct((BLK, DIM), jnp.float32),
        in_specs=[VMEM, VMEM],
        out_specs=VMEM,
        scratch_shapes=[pltpu.VMEM((DIM, 2 * DIM), jnp.float32)],
        compiler_params=PARAMS,
        name="make_basis",
    )(gram, rows)


def ring_sum(value, move):
    return (value + move(value, 2)) + (move(value, 1) + move(value, -1))


def shards(points, probes):
    order = (1, -1, 2)
    near = jnp.concatenate([from_z(points, d) for d in order])
    block = pack(points, probes)
    leg = jnp.concatenate([first_leg(block, d) for d in order])
    side = [second_leg(block, d) for d in order]
    far = swap(near)
    home = [points, swap(points)]
    rest = [second_leg(leg, d) for d in order]

    early = [block, leg] + side
    acc = sketch_part([near, far], early, None, False, 2, "early")
    keep, give = sketch_part([near, far], rest, acc, True, 2, "away")
    summed = keep + swap(give)
    pieces = [summed[i * BLK:(i + 1) * BLK] for i in range(3)]
    held = lax.optimization_barrier(pieces + home)
    pieces, home = held[:3], held[3:]
    back = [from_z(v, -d) for v, d in zip(pieces, order)]
    keep, give = sketch_part(home, early + rest, None, True, 2, "home")
    rows, gram = finish_rows(keep, swap(give), back[0] + (back[1] + back[2]))
    gram = gram + swap(gram)
    for move in (from_z, from_y, from_x):
        gram = ring_sum(gram, move)
    return rows, make_basis(gram, rows)


def solution(mesh):
    spec = P(AXES, None)
    return jax.shard_map(shards, mesh=mesh, in_specs=(spec, spec), out_specs=(spec, spec), check_vma=False)
```

profile of v0, /device:TPU:0, one launch (start us, length us, event | category | flops | bytes accessed | tf_op | source)
XLA Modules:
  0.0 136.9 jit_solution(12171928027678339373)
XLA Ops:
  0.6 4.2 %collective-permute-start = (bf16[512,128]{1,0:T(8,128)(2,1)}, bf16[512,128]{1,0:T(8,128)(2,1)S(1)}, u32[]{:S(2)}, u32[]{:S(2)}) collective-permute-start(bf16[512,128]{1,0:T(8,128)(2,1)} %refs_0_), channel_id=1, source_target_pairs={{0,3},{1,0},{2,1},{3,2},{4,7},{5,4},{6,5},{7,6},{8,11},{9,8},{10,9... | collective-permute-start | bytes 393224 | tf_op jit(solution)/shard_map/ppermute | solution.py:34
  4.8 1.8 %pack.1.refs_2_ = bf16[512,256]{1,0:T(8,128)(2,1)} custom-call(bf16[512,128]{1,0:T(8,128)(2,1)} %refs_0_, bf16[512,128]{1,0:T(8,128)(2,1)} %prb_ref.1), custom_call_target="tpu_custom_call" | custom-call | tf_op jit(solution)/shard_map/pack/pallas_call | solution.py:69
  6.6 2.8 %collective-permute-start.4 = (bf16[512,256]{1,0:T(8,128)(2,1)}, bf16[512,256]{1,0:T(8,128)(2,1)S(1)}, u32[]{:S(2)}, u32[]{:S(2)}) collective-permute-start(bf16[512,256]{1,0:T(8,128)(2,1)} %pack.1.refs_2_), channel_id=1, source_target_pairs={{0,68},{1,69},{2,70},{3,71},{4,0},{5,1},{6,2},{7,3},{8,56},{9,57},... | collective-permute-start | bytes 786440 | tf_op jit(solution)/shard_map/ppermute | solution.py:34
  9.4 1.9 %collective-permute-start.2 = (bf16[512,128]{1,0:T(8,128)(2,1)}, bf16[512,128]{1,0:T(8,128)(2,1)S(1)}, u32[]{:S(2)}, u32[]{:S(2)}) collective-permute-start(bf16[512,128]{1,0:T(8,128)(2,1)} %refs_0_), channel_id=1, source_target_pairs={{0,2},{1,3},{2,0},{3,1},{4,6},{5,7},{6,4},{7,5},{8,10},{9,11},{10,... | collective-permute-start | bytes 393224 | tf_op jit(solution)/shard_map/ppermute | solution.py:34
  11.3 4.8 %collective-permute-done.2 = bf16[512,128]{1,0:T(8,128)(2,1)S(1)} collective-permute-done((bf16[512,128]{1,0:T(8,128)(2,1)}, bf16[512,128]{1,0:T(8,128)(2,1)S(1)}, u32[]{:S(2)}, u32[]{:S(2)}) %collective-permute-start.2) | collective-permute-done | bytes 131104 | tf_op jit(solution)/shard_map/ppermute | solution.py:34
  16.2 3.1 %collective-permute-start.6 = (bf16[512,256]{1,0:T(8,128)(2,1)}, bf16[512,256]{1,0:T(8,128)(2,1)S(1)}, u32[]{:S(2)}, u32[]{:S(2)}) collective-permute-start(bf16[512,256]{1,0:T(8,128)(2,1)} %pack.1.refs_2_), channel_id=1, source_target_pairs={{0,64},{1,65},{2,66},{3,67},{4,68},{5,69},{6,70},{7,71},{8,40},{9,... | collective-permute-start | bytes 786440 | tf_op jit(solution)/shard_map/ppermute | solution.py:34
  19.2 3.0 %collective-permute-start.10 = (bf16[512,256]{1,0:T(8,128)(2,1)}, bf16[512,256]{1,0:T(8,128)(2,1)S(1)}, u32[]{:S(2)}, u32[]{:S(2)}) collective-permute-start(bf16[512,256]{1,0:T(8,128)(2,1)} %pack.1.refs_2_), channel_id=1, source_target_pairs={{0,48},{1,49},{2,50},{3,51},{4,52},{5,53},{6,54},{7,55},{8,76},{9,... | collective-permute-start | bytes 786440 | tf_op jit(solution)/shard_map/ppermute | solution.py:34
  22.2 1.6 %collective-permute-start.12 = (bf16[512,256]{1,0:T(8,128)(2,1)}, bf16[512,256]{1,0:T(8,128)(2,1)S(1)}, u32[]{:S(2)}, u32[]{:S(2)}) collective-permute-start(bf16[512,256]{1,0:T(8,128)(2,1)} %pack.1.refs_2_), channel_id=1, source_target_pairs={{0,32},{1,33},{2,34},{3,35},{4,36},{5,37},{6,38},{7,39},{8,72},{9,... | collective-permute-start | bytes 786440 | tf_op jit(solution)/shard_map/ppermute | solution.py:34
  23.8 0.5 collective-permute-done.6
  24.4 4.2 %collective-permute-start.7 = (bf16[1536,256]{1,0:T(8,128)(2,1)S(1)}, bf16[1536,256]{1,0:T(8,128)(2,1)S(1)}, u32[]{:S(2)}, u32[]{:S(2)}) collective-permute-start(bf16[1536,256]{1,0:T(8,128)(2,1)S(1)} %constant_dynamic-update-slice_fusion.3.refs_3_), channel_id=1, source_target_pairs={{0,48},{1,49},{2,50},{3,51},{4,52},{5,53},{6,54},{7,55},{8,76},{9,... | collective-permute-start | bytes 2359304 | tf_op jit(solution)/shard_map/ppermute | solution.py:34
  28.6 4.2 %collective-permute-done.11.refs_5_ = bf16[512,256]{1,0:T(8,128)(2,1)S(1)} collective-permute-done((bf16[512,256]{1,0:T(8,128)(2,1)}, bf16[512,256]{1,0:T(8,128)(2,1)S(1)}, u32[]{:S(2)}, u32[]{:S(2)}) %collective-permute-start.11) | collective-permute-done | bytes 262176 | tf_op jit(solution)/shard_map/ppermute | solution.py:34
  32.9 0.6 copy-done.9
  33.6 0.7 copy-done.7
  34.4 16.2 %early.1.refs_5_ = f32[12,128,256]{2,1,0:T(8,128)} custom-call(bf16[1536,128]{1,0:T(8,128)(2,1)} %copy-done.3, bf16[1536,128]{1,0:T(8,128)(2,1)} %copy-done.7, bf16[512,256]{1,0:T(8,128)(2,1)} %pack.1.refs_2_, bf16[1536,256]{1,0:T(8,128)(2,1)} %copy-done.2, bf16[512,256]{1,0:T(8,128)(2,1)} %copy-done.8, bf16[512,256]{1,0:T(8,128)(2,1)} %copy-done.9, ...), custom_call_target="tpu_custom_call" | custom-call | flops 8455716864 | bytes 6815744 | tf_op jit(solution)/shard_map/early/pallas_call | solution.py:171
  50.6 0.9 copy-done.4
  51.4 0.3 copy-done.5
  51.7 0.9 copy-done.6
  52.6 19.3 %away.1 = (f32[1536,128]{1,0:T(8,128)}, f32[1536,128]{1,0:T(8,128)}) custom-call(bf16[1536,128]{1,0:T(8,128)(2,1)} %copy-done.3, bf16[1536,128]{1,0:T(8,128)(2,1)} %copy-done.7, bf16[1536,256]{1,0:T(8,128)(2,1)} %copy-done.4, bf16[1536,256]{1,0:T(8,128)(2,1)} %copy-done.5, bf16[1536,256]{1,0:T(8,128)(2,1)} %copy-done.6, f32[12,128,256]{2,1,0:T(8,128)} %early.1.refs_5_), custom_call_target="tpu_custom_call" | custom-call | flops 10871635968 | bytes 7864320 | tf_op jit(solution)/shard_map/away/pallas_call | solution.py:171
  71.9 2.1 %collective-permute-start.13 = (f32[1536,128]{1,0:T(8,128)}, f32[1536,128]{1,0:T(8,128)S(1)}, u32[]{:S(2)}, u32[]{:S(2)}) collective-permute-start(f32[1536,128]{1,0:T(8,128)} %get-tuple-element.14), channel_id=1, source_target_pairs={{0,8},{1,9},{2,10},{3,11},{4,12},{5,13},{6,14},{7,15},{8,0},{9,1},... | collective-permute-start | bytes 2359304 | tf_op jit(solution)/shard_map/ppermute | solution.py:34
  74.1 2.2 %collective-permute-done.13 = f32[1536,128]{1,0:T(8,128)S(1)} collective-permute-done((f32[1536,128]{1,0:T(8,128)}, f32[1536,128]{1,0:T(8,128)S(1)}, u32[]{:S(2)}, u32[]{:S(2)}) %collective-permute-start.13) | collective-permute-done | bytes 786464 | tf_op jit(solution)/shard_map/ppermute | solution.py:34
  76.3 1.2 add.39
  77.6 0.6 collective-permute-start.16
  78.2 2.7 %collective-permute-start.17 = (f32[512,128]{1,0:T(8,128)S(1)}, f32[512,128]{1,0:T(8,128)S(1)}, u32[]{:S(2)}, u32[]{:S(2)}) collective-permute-start(f32[512,128]{1,0:T(8,128)S(1)} %get-tuple-element.20), channel_id=1, source_target_pairs={{0,3},{1,0},{2,1},{3,2},{4,7},{5,4},{6,5},{7,6},{8,11},{9,8},{10,9... | collective-permute-start | bytes 786440 | tf_op jit(solution)/shard_map/ppermute | solution.py:34
  80.9 1.3 collective-permute-start.18
  82.2 12.2 %home.1 = (f32[512,128]{1,0:T(8,128)}, f32[512,128]{1,0:T(8,128)}) custom-call(bf16[512,128]{1,0:T(8,128)(2,1)} %refs_0_, bf16[512,128]{1,0:T(8,128)(2,1)} %copy-done.11, bf16[512,256]{1,0:T(8,128)(2,1)} %pack.1.refs_2_, bf16[1536,256]{1,0:T(8,128)(2,1)} %copy-done.2, bf16[512,256]{1,0:T(8,128)(2,1)} %copy-done.8, bf16[512,256]{1,0:T(8,128)(2,1)} %copy-done.9, ...), custom_call_target="tpu_custom_call" | custom-call | flops 6442450944 | bytes 9437184 | tf_op jit(solution)/shard_map/home/pallas_call | solution.py:171
  94.4 0.8 add_add_fusion.back_ref
  95.2 1.0 collective-permute-done.15.got_ref
  96.1 0.7 copy-done
  96.8 2.2 %finish_rows.1 = (f32[512,128]{1,0:T(8,128)}, f32[128,128]{1,0:T(8,128)}) custom-call(f32[512,128]{1,0:T(8,128)} %get-tuple-element.17.keep_ref, f32[512,128]{1,0:T(8,128)} %copy-done, f32[512,128]{1,0:T(8,128)} %add_add_fusion.back_ref), custom_call_target="tpu_custom_call" | custom-call | tf_op jit(solution)/shard_map/finish_rows/pallas_call | solution.py:198
  99.1 1.3 collective-permute-done.19
  100.5 0.9 add.42
  101.3 2.3 %collective-permute-start.20 = (f32[128,128]{1,0:T(8,128)S(1)}, f32[128,128]{1,0:T(8,128)S(1)}, u32[]{:S(2)}, u32[]{:S(2)}) collective-permute-start(f32[128,128]{1,0:T(8,128)S(1)} %add.42), channel_id=1, source_target_pairs={{0,2},{1,3},{2,0},{3,1},{4,6},{5,7},{6,4},{7,5},{8,10},{9,11},{10,... | collective-permute-start | bytes 196616 | tf_op jit(solution)/shard_map/ppermute | solution.py:34
  103.6 1.9 %collective-permute-start.21 = (f32[128,128]{1,0:T(8,128)S(1)}, f32[128,128]{1,0:T(8,128)S(1)}, u32[]{:S(2)}, u32[]{:S(2)}) collective-permute-start(f32[128,128]{1,0:T(8,128)S(1)} %add.42), channel_id=1, source_target_pairs={{0,3},{1,0},{2,1},{3,2},{4,7},{5,4},{6,5},{7,6},{8,11},{9,8},{10,9... | collective-permute-start | bytes 196616 | tf_op jit(solution)/shard_map/ppermute | solution.py:34
  105.7 1.5 %collective-permute-done.20 = f32[128,128]{1,0:T(8,128)S(1)} collective-permute-done((f32[128,128]{1,0:T(8,128)S(1)}, f32[128,128]{1,0:T(8,128)S(1)}, u32[]{:S(2)}, u32[]{:S(2)}) %collective-permute-start.20) | collective-permute-done | bytes 65568 | tf_op jit(solution)/shard_map/ppermute | solution.py:34
  107.2 0.7 collective-permute-done.21
  107.9 3.1 %collective-permute-done.22 = f32[128,128]{1,0:T(8,128)S(1)} collective-permute-done((f32[128,128]{1,0:T(8,128)S(1)}, f32[128,128]{1,0:T(8,128)S(1)}, u32[]{:S(2)}, u32[]{:S(2)}) %collective-permute-start.22) | collective-permute-done | bytes 65568 | tf_op jit(solution)/shard_map/ppermute | solution.py:34
  111.0 1.6 %collective-permute-start.23 = (f32[128,128]{1,0:T(8,128)S(1)}, f32[128,128]{1,0:T(8,128)S(1)}, u32[]{:S(2)}, u32[]{:S(2)}) collective-permute-start(f32[128,128]{1,0:T(8,128)S(1)} %add_add_fusion.3), channel_id=1, source_target_pairs={{0,32},{1,33},{2,34},{3,35},{4,36},{5,37},{6,38},{7,39},{8,40},{9,... | collective-permute-start | bytes 196616 | tf_op jit(solution)/shard_map/ppermute | solution.py:34
  112.5 2.4 %collective-permute-start.24 = (f32[128,128]{1,0:T(8,128)S(1)}, f32[128,128]{1,0:T(8,128)S(1)}, u32[]{:S(2)}, u32[]{:S(2)}) collective-permute-start(f32[128,128]{1,0:T(8,128)S(1)} %add_add_fusion.3), channel_id=1, source_target_pairs={{0,48},{1,49},{2,50},{3,51},{4,52},{5,53},{6,54},{7,55},{8,56},{9,... | collective-permute-start | bytes 196616 | tf_op jit(solution)/shard_map/ppermute | solution.py:34
  115.0 1.9 %collective-permute-done.23 = f32[128,128]{1,0:T(8,128)S(1)} collective-permute-done((f32[128,128]{1,0:T(8,128)S(1)}, f32[128,128]{1,0:T(8,128)S(1)}, u32[]{:S(2)}, u32[]{:S(2)}) %collective-permute-start.23) | collective-permute-done | bytes 65568 | tf_op jit(solution)/shard_map/ppermute | solution.py:34
  116.8 0.3 collective-permute-done.24
  117.1 3.3 %collective-permute-done.25 = f32[128,128]{1,0:T(8,128)S(1)} collective-permute-done((f32[128,128]{1,0:T(8,128)S(1)}, f32[128,128]{1,0:T(8,128)S(1)}, u32[]{:S(2)}, u32[]{:S(2)}) %collective-permute-start.25) | collective-permute-done | bytes 65568 | tf_op jit(solution)/shard_map/ppermute | solution.py:34
  120.5 1.1 collective-permute-start.26
  121.6 1.6 %collective-permute-start.27 = (f32[128,128]{1,0:T(8,128)S(1)}, f32[128,128]{1,0:T(8,128)S(1)}, u32[]{:S(2)}, u32[]{:S(2)}) collective-permute-start(f32[128,128]{1,0:T(8,128)S(1)} %add_add_fusion.2), channel_id=1, source_target_pairs={{0,68},{1,69},{2,70},{3,71},{4,0},{5,1},{6,2},{7,3},{8,76},{9,77},... | collective-permute-start | bytes 196616 | tf_op jit(solution)/shard_map/ppermute | solution.py:34
  123.2 0.5 collective-permute-start.28
  123.6 2.7 %collective-permute-done.26 = f32[128,128]{1,0:T(8,128)S(1)} collective-permute-done((f32[128,128]{1,0:T(8,128)S(1)}, f32[128,128]{1,0:T(8,128)S(1)}, u32[]{:S(2)}, u32[]{:S(2)}) %collective-permute-start.26) | collective-permute-done | bytes 65568 | tf_op jit(solution)/shard_map/ppermute | solution.py:34
  126.3 2.3 %collective-permute-done.28 = f32[128,128]{1,0:T(8,128)S(1)} collective-permute-done((f32[128,128]{1,0:T(8,128)S(1)}, f32[128,128]{1,0:T(8,128)S(1)}, u32[]{:S(2)}, u32[]{:S(2)}) %collective-permute-start.28) | collective-permute-done | bytes 65568 | tf_op jit(solution)/shard_map/ppermute | solution.py:34
  128.7 0.6 add_add_fusion.1.gram_ref
  129.3 7.6 %make_basis.1 = f32[512,128]{1,0:T(8,128)} custom-call(f32[128,128]{1,0:T(8,128)} %add_add_fusion.1.gram_ref, f32[512,128]{1,0:T(8,128)} %get-tuple-element.11.rows_ref), custom_call_target="tpu_custom_call" | custom-call | tf_op jit(solution)/shard_map/make_basis/pallas_call | solution.py:252
  (53 shorter events, 0.9 us)
Async XLA Ops:
  0.6 10.6 %collective-permute-start = (bf16[512,128]{1,0:T(8,128)(2,1)}, bf16[512,128]{1,0:T(8,128)(2,1)S(1)}, u32[]{:S(2)}, u32[]{:S(2)}) collective-permute-start(bf16[512,128]{1,0:T(8,128)(2,1)} %refs_0_), channel_id=1, source_target_pairs={{0,3},{1,0},{2,1},{3,2},{4,7},{5,4},{6,5},{7,6},{8,11},{9,8},{10,9... | collective-permute-start | bytes 393224 | tf_op jit(solution)/shard_map/ppermute | solution.py:34
  4.8 6.4 %collective-permute-start.1 = (bf16[512,128]{1,0:T(8,128)(2,1)}, bf16[512,128]{1,0:T(8,128)(2,1)S(1)}, u32[]{:S(2)}, u32[]{:S(2)}) collective-permute-start(bf16[512,128]{1,0:T(8,128)(2,1)} %refs_0_), channel_id=1, source_target_pairs={{0,1},{1,2},{2,3},{3,0},{4,5},{5,6},{6,7},{7,4},{8,9},{9,10},{10,1... | collective-permute-start | bytes 393224 | tf_op jit(solution)/shard_map/ppermute | solution.py:34
  6.6 15.6 %collective-permute-start.4 = (bf16[512,256]{1,0:T(8,128)(2,1)}, bf16[512,256]{1,0:T(8,128)(2,1)S(1)}, u32[]{:S(2)}, u32[]{:S(2)}) collective-permute-start(bf16[512,256]{1,0:T(8,128)(2,1)} %pack.1.refs_2_), channel_id=1, source_target_pairs={{0,68},{1,69},{2,70},{3,71},{4,0},{5,1},{6,2},{7,3},{8,56},{9,57},... | collective-permute-start | bytes 786440 | tf_op jit(solution)/shard_map/ppermute | solution.py:34
  9.4 12.8 %collective-permute-start.5 = (bf16[512,256]{1,0:T(8,128)(2,1)}, bf16[512,256]{1,0:T(8,128)(2,1)S(1)}, u32[]{:S(2)}, u32[]{:S(2)}) collective-permute-start(bf16[512,256]{1,0:T(8,128)(2,1)} %pack.1.refs_2_), channel_id=1, source_target_pairs={{0,4},{1,5},{2,6},{3,7},{4,64},{5,65},{6,66},{7,67},{8,24},{9,25},... | collective-permute-start | bytes 786440 | tf_op jit(solution)/shard_map/ppermute | solution.py:34
  9.4 6.7 %collective-permute-start.2 = (bf16[512,128]{1,0:T(8,128)(2,1)}, bf16[512,128]{1,0:T(8,128)(2,1)S(1)}, u32[]{:S(2)}, u32[]{:S(2)}) collective-permute-start(bf16[512,128]{1,0:T(8,128)(2,1)} %refs_0_), channel_id=1, source_target_pairs={{0,2},{1,3},{2,0},{3,1},{4,6},{5,7},{6,4},{7,5},{8,10},{9,11},{10,... | collective-permute-start | bytes 393224 | tf_op jit(solution)/shard_map/ppermute | solution.py:34
  16.1 16.8 %copy-start.3 = (bf16[1536,128]{1,0:T(8,128)(2,1)}, bf16[1536,128]{1,0:T(8,128)(2,1)S(1)}, u32[]{:S(2)}) copy-start(bf16[1536,128]{1,0:T(8,128)(2,1)S(1)} %constant_dynamic-update-slice_fusion.refs_0_) | copy-start | bytes 1179652
  16.1 16.7 %collective-permute-start.3 = (bf16[1536,128]{1,0:T(8,128)(2,1)S(1)}, bf16[1536,128]{1,0:T(8,128)(2,1)S(1)}, u32[]{:S(2)}, u32[]{:S(2)}) collective-permute-start(bf16[1536,128]{1,0:T(8,128)(2,1)S(1)} %constant_dynamic-update-slice_fusion.refs_0_), channel_id=1, source_target_pairs={{0,8},{1,9},{2,10},{3,11},{4,12},{5,13},{6,14},{7,15},{8,0},{9,1},... | collective-permute-start | bytes 1179656 | tf_op jit(solution)/shard_map/ppermute | solution.py:34
  16.2 8.2 %collective-permute-start.6 = (bf16[512,256]{1,0:T(8,128)(2,1)}, bf16[512,256]{1,0:T(8,128)(2,1)S(1)}, u32[]{:S(2)}, u32[]{:S(2)}) collective-permute-start(bf16[512,256]{1,0:T(8,128)(2,1)} %pack.1.refs_2_), channel_id=1, source_target_pairs={{0,64},{1,65},{2,66},{3,67},{4,68},{5,69},{6,70},{7,71},{8,40},{9,... | collective-permute-start | bytes 786440 | tf_op jit(solution)/shard_map/ppermute | solution.py:34
  19.2 9.4 %collective-permute-start.10 = (bf16[512,256]{1,0:T(8,128)(2,1)}, bf16[512,256]{1,0:T(8,128)(2,1)S(1)}, u32[]{:S(2)}, u32[]{:S(2)}) collective-permute-start(bf16[512,256]{1,0:T(8,128)(2,1)} %pack.1.refs_2_), channel_id=1, source_target_pairs={{0,48},{1,49},{2,50},{3,51},{4,52},{5,53},{6,54},{7,55},{8,76},{9,... | collective-permute-start | bytes 786440 | tf_op jit(solution)/shard_map/ppermute | solution.py:34
  22.2 10.6 %collective-permute-start.11 = (bf16[512,256]{1,0:T(8,128)(2,1)}, bf16[512,256]{1,0:T(8,128)(2,1)S(1)}, u32[]{:S(2)}, u32[]{:S(2)}) collective-permute-start(bf16[512,256]{1,0:T(8,128)(2,1)} %pack.1.refs_2_), channel_id=1, source_target_pairs={{0,16},{1,17},{2,18},{3,19},{4,20},{5,21},{6,22},{7,23},{8,12},{9,... | collective-permute-start | bytes 786440 | tf_op jit(solution)/shard_map/ppermute | solution.py:34
  22.2 10.6 %collective-permute-start.12 = (bf16[512,256]{1,0:T(8,128)(2,1)}, bf16[512,256]{1,0:T(8,128)(2,1)S(1)}, u32[]{:S(2)}, u32[]{:S(2)}) collective-permute-start(bf16[512,256]{1,0:T(8,128)(2,1)} %pack.1.refs_2_), channel_id=1, source_target_pairs={{0,32},{1,33},{2,34},{3,35},{4,36},{5,37},{6,38},{7,39},{8,72},{9,... | collective-permute-start | bytes 786440 | tf_op jit(solution)/shard_map/ppermute | solution.py:34
  24.4 8.5 %copy-start.2 = (bf16[1536,256]{1,0:T(8,128)(2,1)}, bf16[1536,256]{1,0:T(8,128)(2,1)S(1)}, u32[]{:S(2)}) copy-start(bf16[1536,256]{1,0:T(8,128)(2,1)S(1)} %constant_dynamic-update-slice_fusion.3.refs_3_) | copy-start | bytes 2359300
  24.4 26.2 %collective-permute-start.7 = (bf16[1536,256]{1,0:T(8,128)(2,1)S(1)}, bf16[1536,256]{1,0:T(8,128)(2,1)S(1)}, u32[]{:S(2)}, u32[]{:S(2)}) collective-permute-start(bf16[1536,256]{1,0:T(8,128)(2,1)S(1)} %constant_dynamic-update-slice_fusion.3.refs_3_), channel_id=1, source_target_pairs={{0,48},{1,49},{2,50},{3,51},{4,52},{5,53},{6,54},{7,55},{8,76},{9,... | collective-permute-start | bytes 2359304 | tf_op jit(solution)/shard_map/ppermute | solution.py:34
  28.6 4.2 %copy-start.8 = (bf16[512,256]{1,0:T(8,128)(2,1)}, bf16[512,256]{1,0:T(8,128)(2,1)S(1)}, u32[]{:S(2)}) copy-start(bf16[512,256]{1,0:T(8,128)(2,1)S(1)} %collective-permute-done.10.refs_4_) | copy-start | bytes 786436
  28.6 21.9 %collective-permute-start.8 = (bf16[1536,256]{1,0:T(8,128)(2,1)S(1)}, bf16[1536,256]{1,0:T(8,128)(2,1)S(1)}, u32[]{:S(2)}, u32[]{:S(2)}) collective-permute-start(bf16[1536,256]{1,0:T(8,128)(2,1)S(1)} %constant_dynamic-update-slice_fusion.3.refs_3_), channel_id=1, source_target_pairs={{0,16},{1,17},{2,18},{3,19},{4,20},{5,21},{6,22},{7,23},{8,12},{9,... | collective-permute-start | bytes 2359304 | tf_op jit(solution)/shard_map/ppermute | solution.py:34
  32.8 0.7 copy-start.9
  32.8 17.7 %collective-permute-start.9 = (bf16[1536,256]{1,0:T(8,128)(2,1)S(1)}, bf16[1536,256]{1,0:T(8,128)(2,1)S(1)}, u32[]{:S(2)}, u32[]{:S(2)}) collective-permute-start(bf16[1536,256]{1,0:T(8,128)(2,1)S(1)} %constant_dynamic-update-slice_fusion.3.refs_3_), channel_id=1, source_target_pairs={{0,32},{1,33},{2,34},{3,35},{4,36},{5,37},{6,38},{7,39},{8,72},{9,... | collective-permute-start | bytes 2359304 | tf_op jit(solution)/shard_map/ppermute | solution.py:34
  32.8 0.8 copy-start.10
  33.6 0.7 copy-start.7
  50.5 23.5 %copy-start.1 = (bf16[512,128]{1,0:T(8,128)(2,1)S(1)}, bf16[512,128]{1,0:T(8,128)(2,1)}, u32[]{:S(2)}) copy-start(bf16[512,128]{1,0:T(8,128)(2,1)} %refs_0_) | copy-start | bytes 393220
  50.5 0.9 copy-start.4
  50.5 1.1 copy-start.5
  51.7 0.9 copy-start.6
  71.9 4.4 %collective-permute-start.13 = (f32[1536,128]{1,0:T(8,128)}, f32[1536,128]{1,0:T(8,128)S(1)}, u32[]{:S(2)}, u32[]{:S(2)}) collective-permute-start(f32[1536,128]{1,0:T(8,128)} %get-tuple-element.14), channel_id=1, source_target_pairs={{0,8},{1,9},{2,10},{3,11},{4,12},{5,13},{6,14},{7,15},{8,0},{9,1},... | collective-permute-start | bytes 2359304 | tf_op jit(solution)/shard_map/ppermute | solution.py:34
  74.0 3.6 %collective-permute-start.14 = (bf16[512,128]{1,0:T(8,128)(2,1)S(1)}, bf16[512,128]{1,0:T(8,128)(2,1)S(1)}, u32[]{:S(2)}, u32[]{:S(2)}) collective-permute-start(bf16[512,128]{1,0:T(8,128)(2,1)S(1)} %copy-done.1), channel_id=1, source_target_pairs={{0,8},{1,9},{2,10},{3,11},{4,12},{5,13},{6,14},{7,15},{8,0},{9,1},... | collective-permute-start | bytes 393224 | tf_op jit(solution)/shard_map/ppermute | solution.py:34
  77.6 4.6 %copy-start.11 = (bf16[512,128]{1,0:T(8,128)(2,1)}, bf16[512,128]{1,0:T(8,128)(2,1)S(1)}, u32[]{:S(2)}) copy-start(bf16[512,128]{1,0:T(8,128)(2,1)S(1)} %collective-permute-done.14.refs_1_) | copy-start | bytes 393220
  77.6 16.8 %collective-permute-start.16 = (f32[512,128]{1,0:T(8,128)S(1)}, f32[512,128]{1,0:T(8,128)S(1)}, u32[]{:S(2)}, u32[]{:S(2)}) collective-permute-start(f32[512,128]{1,0:T(8,128)S(1)} %get-tuple-element.19), channel_id=1, source_target_pairs={{0,1},{1,2},{2,3},{3,0},{4,5},{5,6},{6,7},{7,4},{8,9},{9,10},{10,1... | collective-permute-start | bytes 786440 | tf_op jit(solution)/shard_map/ppermute | solution.py:34
  78.2 16.2 %collective-permute-start.17 = (f32[512,128]{1,0:T(8,128)S(1)}, f32[512,128]{1,0:T(8,128)S(1)}, u32[]{:S(2)}, u32[]{:S(2)}) collective-permute-start(f32[512,128]{1,0:T(8,128)S(1)} %get-tuple-element.20), channel_id=1, source_target_pairs={{0,3},{1,0},{2,1},{3,2},{4,7},{5,4},{6,5},{7,6},{8,11},{9,8},{10,9... | collective-permute-start | bytes 786440 | tf_op jit(solution)/shard_map/ppermute | solution.py:34
  80.9 13.5 %collective-permute-start.18 = (f32[512,128]{1,0:T(8,128)S(1)}, f32[512,128]{1,0:T(8,128)S(1)}, u32[]{:S(2)}, u32[]{:S(2)}) collective-permute-start(f32[512,128]{1,0:T(8,128)S(1)} %get-tuple-element.21), channel_id=1, source_target_pairs={{0,2},{1,3},{2,0},{3,1},{4,6},{5,7},{6,4},{7,5},{8,10},{9,11},{10,... | collective-permute-start | bytes 786440 | tf_op jit(solution)/shard_map/ppermute | solution.py:34
  94.4 1.7 %collective-permute-start.15 = (f32[512,128]{1,0:T(8,128)}, f32[512,128]{1,0:T(8,128)S(1)}, u32[]{:S(2)}, u32[]{:S(2)}) collective-permute-start(f32[512,128]{1,0:T(8,128)} %get-tuple-element.18), channel_id=1, source_target_pairs={{0,8},{1,9},{2,10},{3,11},{4,12},{5,13},{6,14},{7,15},{8,0},{9,1},... | collective-permute-start | bytes 786440 | tf_op jit(solution)/shard_map/ppermute | solution.py:34
  96.1 0.7 copy-start
  99.0 1.5 %collective-permute-start.19 = (f32[128,128]{1,0:T(8,128)}, f32[128,128]{1,0:T(8,128)S(1)}, u32[]{:S(2)}, u32[]{:S(2)}) collective-permute-start(f32[128,128]{1,0:T(8,128)} %get-tuple-element.23), channel_id=1, source_target_pairs={{0,8},{1,9},{2,10},{3,11},{4,12},{5,13},{6,14},{7,15},{8,0},{9,1},... | collective-permute-start | bytes 196616 | tf_op jit(solution)/shard_map/ppermute | solution.py:34
  101.3 5.8 %collective-permute-start.20 = (f32[128,128]{1,0:T(8,128)S(1)}, f32[128,128]{1,0:T(8,128)S(1)}, u32[]{:S(2)}, u32[]{:S(2)}) collective-permute-start(f32[128,128]{1,0:T(8,128)S(1)} %add.42), channel_id=1, source_target_pairs={{0,2},{1,3},{2,0},{3,1},{4,6},{5,7},{6,4},{7,5},{8,10},{9,11},{10,... | collective-permute-start | bytes 196616 | tf_op jit(solution)/shard_map/ppermute | solution.py:34
  103.6 4.3 %collective-permute-start.21 = (f32[128,128]{1,0:T(8,128)S(1)}, f32[128,128]{1,0:T(8,128)S(1)}, u32[]{:S(2)}, u32[]{:S(2)}) collective-permute-start(f32[128,128]{1,0:T(8,128)S(1)} %add.42), channel_id=1, source_target_pairs={{0,3},{1,0},{2,1},{3,2},{4,7},{5,4},{6,5},{7,6},{8,11},{9,8},{10,9... | collective-permute-start | bytes 196616 | tf_op jit(solution)/shard_map/ppermute | solution.py:34
  105.5 5.5 %collective-permute-start.22 = (f32[128,128]{1,0:T(8,128)S(1)}, f32[128,128]{1,0:T(8,128)S(1)}, u32[]{:S(2)}, u32[]{:S(2)}) collective-permute-start(f32[128,128]{1,0:T(8,128)S(1)} %add.42), channel_id=1, source_target_pairs={{0,1},{1,2},{2,3},{3,0},{4,5},{5,6},{6,7},{7,4},{8,9},{9,10},{10,1... | collective-permute-start | bytes 196616 | tf_op jit(solution)/shard_map/ppermute | solution.py:34
  111.0 5.9 %collective-permute-start.23 = (f32[128,128]{1,0:T(8,128)S(1)}, f32[128,128]{1,0:T(8,128)S(1)}, u32[]{:S(2)}, u32[]{:S(2)}) collective-permute-start(f32[128,128]{1,0:T(8,128)S(1)} %add_add_fusion.3), channel_id=1, source_target_pairs={{0,32},{1,33},{2,34},{3,35},{4,36},{5,37},{6,38},{7,39},{8,40},{9,... | collective-permute-start | bytes 196616 | tf_op jit(solution)/shard_map/ppermute | solution.py:34
  112.5 4.6 %collective-permute-start.24 = (f32[128,128]{1,0:T(8,128)S(1)}, f32[128,128]{1,0:T(8,128)S(1)}, u32[]{:S(2)}, u32[]{:S(2)}) collective-permute-start(f32[128,128]{1,0:T(8,128)S(1)} %add_add_fusion.3), channel_id=1, source_target_pairs={{0,48},{1,49},{2,50},{3,51},{4,52},{5,53},{6,54},{7,55},{8,56},{9,... | collective-permute-start | bytes 196616 | tf_op jit(solution)/shard_map/ppermute | solution.py:34
  115.0 5.5 %collective-permute-start.25 = (f32[128,128]{1,0:T(8,128)S(1)}, f32[128,128]{1,0:T(8,128)S(1)}, u32[]{:S(2)}, u32[]{:S(2)}) collective-permute-start(f32[128,128]{1,0:T(8,128)S(1)} %add_add_fusion.3), channel_id=1, source_target_pairs={{0,16},{1,17},{2,18},{3,19},{4,20},{5,21},{6,22},{7,23},{8,24},{9,... | collective-permute-start | bytes 196616 | tf_op jit(solution)/shard_map/ppermute | solution.py:34
  120.5 5.8 %collective-permute-start.26 = (f32[128,128]{1,0:T(8,128)S(1)}, f32[128,128]{1,0:T(8,128)S(1)}, u32[]{:S(2)}, u32[]{:S(2)}) collective-permute-start(f32[128,128]{1,0:T(8,128)S(1)} %add_add_fusion.2), channel_id=1, source_target_pairs={{0,64},{1,65},{2,66},{3,67},{4,68},{5,69},{6,70},{7,71},{8,72},{9,... | collective-permute-start | bytes 196616 | tf_op jit(solution)/shard_map/ppermute | solution.py:34
  121.6 4.7 %collective-permute-start.27 = (f32[128,128]{1,0:T(8,128)S(1)}, f32[128,128]{1,0:T(8,128)S(1)}, u32[]{:S(2)}, u32[]{:S(2)}) collective-permute-start(f32[128,128]{1,0:T(8,128)S(1)} %add_add_fusion.2), channel_id=1, source_target_pairs={{0,68},{1,69},{2,70},{3,71},{4,0},{5,1},{6,2},{7,3},{8,76},{9,77},... | collective-permute-start | bytes 196616 | tf_op jit(solution)/shard_map/ppermute | solution.py:34
  123.2 5.5 %collective-permute-start.28 = (f32[128,128]{1,0:T(8,128)S(1)}, f32[128,128]{1,0:T(8,128)S(1)}, u32[]{:S(2)}, u32[]{:S(2)}) collective-permute-start(f32[128,128]{1,0:T(8,128)S(1)} %add_add_fusion.2), channel_id=1, source_target_pairs={{0,4},{1,5},{2,6},{3,7},{4,64},{5,65},{6,66},{7,67},{8,12},{9,13},... | collective-permute-start | bytes 196616 | tf_op jit(solution)/shard_map/ppermute | solution.py:34
where the time goes:
time: 137 us
  Pallas kernels  59.3 us (43%)
  starting transfers between devices  39.1 us (29%)
  waiting for transfers between devices  29.8 us (22%)
  local copies, waits for them, and re-layouts  4.38 us (3%)
  other arithmetic  3.5 us (3%)
    pallas_call x3, Pallas kernels, sketch_part(): pl.pallas_call(body, out_shape=shape, in_specs=[VMEM] * len(ops), out_spe...  47.7 us
    ppermute x29, starting transfers between devices, fetch(): return lax.ppermute(value, AXES, sorted(pairs))  39.1 us
    ppermute x29, waiting for transfers between devices, fetch(): return lax.ppermute(value, AXES, sorted(pairs))  29.8 us
    pallas_call x1, Pallas kernels, make_basis(): pl.pallas_call(basis_body, out_shape=jax.ShapeDtypeStruct((BLK, DIM), jnp...  7.65 us
    unnamed x28, local copies, waits for them, and re-layouts  4.29 us
  transfers between devices with their start and end apart: 29, of which 14 were waited for; matrix products, arithmetic and copies ran while one was open for 2% of the time, Pallas kernels for 22%

commit v1 on v0

v1 whole, which is shorter than its diff:
```python
import math

import jax
import jax.numpy as jnp
from jax import lax
from jax.experimental import pallas as pl
from jax.experimental.pallas import tpu as pltpu
from jax.sharding import PartitionSpec as P

AXES = ("row", "col")
SIDE = 4
BLK = 512
DIM = 128
NPTS = BLK * 2 * SIDE ** 3
TI = 256
GROUP = 2
COLS = BLK + 16
ROWS = BLK + 32
SCALE = -3.0 / DIM * math.log2(math.e)
VMEM = pl.BlockSpec(memory_space=pltpu.VMEM)
PARAMS = pltpu.CompilerParams(vmem_limit_bytes=20 << 20)


def local(values):
    return [pltpu.with_memory_space_constraint(v, pltpu.VMEM) for v in values]


def index(x, y, z, k):
    x, y, z = x % SIDE, y % SIDE, z % SIDE
    return ((x // 2) * 8 + y * 2 + k) * 8 + (x % 2) * 4 + z


def fetch(value, source):
    pairs = []
    for x in range(SIDE):
        for y in range(SIDE):
            for z in range(SIDE):
                for k in range(2):
                    pairs.append((index(*source(x, y, z, k)), index(x, y, z, k)))
    return lax.ppermute(value, AXES, sorted(pairs))


def swap(value):
    return fetch(value, lambda x, y, z, k: (x, y, z, 1 - k))


def from_x(value, step):
    return fetch(value, lambda x, y, z, k: (x + step, y, z, k))


def from_y(value, step):
    return fetch(value, lambda x, y, z, k: (x, y + step, z, k))


def from_z(value, step):
    return fetch(value, lambda x, y, z, k: (x, y, z + step, k))


def first_leg(value, step):
    return fetch(value, lambda x, y, z, k: (x + step * (1 - k), y + step * k, z, k))


def second_leg(value, step):
    return fetch(value, lambda x, y, z, k: (x + step * k, y + step * (1 - k), z, k))


def pack_body(pts_ref, prb_ref, block_ref, rows_ref):
    pts = pts_ref[...].astype(jnp.float32)
    square = pts * pts
    major = square.astype(jnp.bfloat16)
    minor = (square - major.astype(jnp.float32)).astype(jnp.bfloat16)
    ones = jnp.ones((8, DIM), jnp.bfloat16)

    def lanes(v):
        return lax.dot_general(ones, v, (((1,), (1,)), ((), ())), preferred_element_type=jnp.float32)

    total = lanes(major) + lanes(minor)
    high = total.astype(jnp.bfloat16).astype(jnp.float32)
    rest = total - high
    mid = rest.astype(jnp.bfloat16).astype(jnp.float32)
    low = rest - mid
    sub = lax.broadcasted_iota(jnp.int32, (8, BLK), 0)

    def place(at, one):
        v = jnp.where((sub >= one) & (sub < one + 3), 1.0, 0.0)
        v = jnp.where(sub == at, high, v)
        v = jnp.where(sub == at + 1, mid, v)
        return jnp.where(sub == at + 2, low, v)

    col = place(0, 3)
    row = place(3, 0)
    half = BLK // 2
    block_ref[BLK:, :] = jnp.concatenate([col[:, :half], col[:, half:]], axis=0).astype(jnp.bfloat16)
    rows_ref[BLK:, :] = jnp.concatenate(
        [row[:, c:c + DIM] for c in range(0, BLK, DIM)], axis=0).astype(jnp.bfloat16)
    block_ref[:BLK, :DIM] = pts_ref[...]
    rows_ref[:BLK, :] = (pts * -2.0).astype(jnp.bfloat16)
    for c in range(0, BLK, DIM):
        block_ref[c:c + DIM, DIM:] = prb_ref[c:c + DIM, :].astype(jnp.float32).T.astype(jnp.bfloat16)


def pack(points, probes):
    return pl.pallas_call(
        pack_body,
        out_shape=[
            pltpu.VMEM((COLS, 2 * DIM), jnp.bfloat16),
            pltpu.VMEM((ROWS, DIM), jnp.bfloat16),
        ],
        in_specs=[VMEM, VMEM],
        out_specs=[VMEM, VMEM],
        compiler_params=PARAMS,
        name="pack",
    )(points, probes)


def upright(v):
    return jnp.concatenate([v, jnp.zeros((DIM - 8, DIM), jnp.float32)], axis=0).T.astype(jnp.bfloat16)


def sketch_part(islots, jblocks, acc, last, carry_product, name):
    m, n = len(islots), len(jblocks)
    first = acc is None
    slots = [(r, lo) for r, v in enumerate(islots) for lo in range(0, v.shape[0], ROWS)]
    irows = len(slots) * BLK
    nout = len(slots) if last else 1
    where = [(r, lo) for r, v in enumerate(jblocks) for lo in range(0, v.shape[0], COLS)]
    count = len(where)
    ntile = irows // TI
    groups = [list(range(b, min(b + GROUP, count))) for b in range(0, count, GROUP)]

    def body(*refs):
        irefs, jrefs = refs[:m], refs[m:m + n]
        pos = m + n
        acc_ref = None
        if not first:
            acc_ref = refs[pos]
            pos += 1
        outs = refs[pos:pos + nout]
        ia, norms, ahead_ref = refs[pos + nout:]
        for s, (r, lo) in enumerate(slots):
            at = s * BLK
            ia[at:at + BLK, :DIM] = irefs[r][lo:lo + BLK, :]
            tail = irefs[r][lo + BLK:lo + ROWS, :].astype(jnp.float32)
            for c in range(BLK // DIM):
                ia[at + c * DIM:at + (c + 1) * DIM, DIM:] = upright(tail[c * 8:c * 8 + 8, :])
        for b, (r, lo) in enumerate(where):
            tail = jrefs[r][lo + BLK:lo + COLS, :].astype(jnp.float32)
            for c in range(BLK // DIM):
                at = b * BLK + c * DIM
                part = tail[(c // 2) * 8:(c // 2) * 8 + 8, (c % 2) * DIM:(c % 2 + 1) * DIM]
                norms[at:at + DIM, :] = upright(part)

        def rows_of(t):
            if isinstance(t, int):
                return ia[t * TI:(t + 1) * TI, :]
            return ia[pl.ds(pl.multiple_of(t * TI, TI), TI), :]

        def dist(group, a):
            pts = [jrefs[where[b][0]][where[b][1]:where[b][1] + BLK, :DIM] for b in group]
            lhs = jnp.concatenate(
                [jnp.concatenate(pts, axis=0), norms[group[0] * BLK:(group[-1] + 1) * BLK, :]], axis=1)
            return lax.dot_general(lhs, a, (((1,), (1,)), ((), ())), preferred_element_type=jnp.float32)

        def turned_probes(group):
            parts = []
            for b in group:
                r, lo = where[b]
                parts += [jrefs[r][lo + c:lo + c + DIM, DIM:] for c in range(0, BLK, DIM)]
            return jnp.concatenate(parts, axis=1)

        if carry_product:
            ahead_ref[...] = dist(groups[0], rows_of(0))

        def step(t, out_ref, at):
            a = rows_of(t)
            total = jnp.zeros((DIM, TI), jnp.float32) if first else acc_ref[t]
            now = ahead_ref[...] if carry_product else dist(groups[0], a)
            for q, group in enumerate(groups):
                final = q + 1 == len(groups)
                if not final:
                    ahead = dist(groups[q + 1], a)
                kern = jnp.exp2(now * SCALE).astype(jnp.bfloat16)
                if final and carry_product:
                    ahead_ref[...] = dist(groups[0], rows_of(min(t + 1, ntile - 1) if isinstance(t, int) else jnp.minimum(t + 1, ntile - 1)))
                total = total + jnp.dot(turned_probes(group), kern, preferred_element_type=jnp.float32)
                if not final:
                    now = ahead
            if last:
                out_ref[at * TI:(at + 1) * TI, :] = total.T
            else:
                out_ref[t] = total

        if last:
            for t in range(ntile):
                step(t, outs[t // 2], t % 2)
        else:
            def turn(i, carry):
                step(2 * i, outs[0], 0)
                step(2 * i + 1, outs[0], 0)
                return carry
            lax.fori_loop(0, ntile // 2, turn, 0)

    shape = (BLK, DIM) if last else (ntile, DIM, TI)
    ops = list(islots) + list(jblocks) + ([] if first else [acc])
    return pl.pallas_call(
        body,
        out_shape=[pltpu.VMEM(shape, jnp.float32)] * nout if last else pltpu.VMEM(shape, jnp.float32),
        in_specs=[VMEM] * len(ops),
        out_specs=[VMEM] * nout if last else VMEM,
        scratch_shapes=[
            pltpu.VMEM((irows, 2 * DIM), jnp.bfloat16),
            pltpu.VMEM((count * BLK, DIM), jnp.bfloat16),
            pltpu.VMEM((GROUP * BLK, TI), jnp.float32),
        ],
        compiler_params=PARAMS,
        cost_estimate=pl.CostEstimate(
            flops=irows * count * BLK * DIM * 6, transcendentals=irows * count * BLK,
            bytes_accessed=(irows + count * BLK) * DIM * 8),
        name=name,
    )(*local(ops))


def gram_body(home_ref, a_ref, b_ref, c_ref, out_ref, gram_ref):
    rows = (home_ref[...] + a_ref[...]) + (b_ref[...] + c_ref[...])
    out_ref[...] = rows
    gram_ref[...] = lax.dot_general(
        rows, rows, (((0,), (0,)), ((), ())),
        precision=lax.Precision.HIGHEST, preferred_element_type=jnp.float32)


def finish_rows(*parts):
    return pl.pallas_call(
        gram_body,
        out_shape=[
            pltpu.VMEM((BLK, DIM), jnp.float32),
            pltpu.VMEM((DIM, DIM), jnp.float32),
        ],
        in_specs=[VMEM] * 4,
        out_specs=[VMEM, VMEM],
        compiler_params=PARAMS,
        name="finish_rows",
    )(*local(parts))


def basis_body(g_ref, a_ref, b_ref, c_ref, rows_ref, out_ref, work):
    work[:, :DIM] = (g_ref[...] + a_ref[...]) + (b_ref[...] + c_ref[...])
    at_row = lax.broadcasted_iota(jnp.int32, (DIM, DIM), 0)
    at_col = lax.broadcasted_iota(jnp.int32, (DIM, DIM), 1)
    work[:, DIM:] = (at_row == at_col).astype(jnp.float32)
    sub = lax.broadcasted_iota(jnp.int32, (8, DIM), 0)

    def row(v, i):
        return jnp.broadcast_to(v[i:i + 1, :], (8, DIM))

    inverse = []
    for lo in range(0, DIM, 8):
        left, right = work[lo:lo + 8, :DIM], work[lo:lo + 8, DIM:]
        cols = [jnp.broadcast_to(left[:, lo + i:lo + i + 1], (8, DIM)) for i in range(8)]
        for i in range(8):
            scale = lax.rsqrt(row(cols[i], i))
            c = cols[i] * scale
            for q in range(i + 1, 8):
                cols[q] = cols[q] - c * row(c, q)
            below = jnp.where(sub > i, c, 0.0)
            pivot = row(left, i) * scale
            left = jnp.where(sub == i, pivot, left - below * pivot)
            pivot = row(right, i) * scale
            right = jnp.where(sub == i, pivot, right - below * pivot)
        inverse.append(right)
        turned = left.T
        for r in range(lo + 8, DIM, 8):
            a, b = work[r:r + 8, :DIM], work[r:r + 8, DIM:]
            for i in range(8):
                c = jnp.broadcast_to(turned[r:r + 8, i:i + 1], (8, DIM))
                a = a - c * left[i:i + 1, :]
                b = b - c * right[i:i + 1, :]
            work[r:r + 8, :DIM] = a
            work[r:r + 8, DIM:] = b
    inv = jnp.concatenate(inverse, axis=0) * math.sqrt(NPTS)
    out_ref[...] = lax.dot_general(
        rows_ref[...], inv, (((1,), (1,)), ((), ())),
        precision=lax.Precision.HIGHEST, preferred_element_type=jnp.float32)


def make_basis(parts, rows):
    return pl.pallas_call(
        basis_body,
        out_shape=jax.ShapeDtypeStruct((BLK, DIM), jnp.float32),
        in_specs=[VMEM] * 5,
        out_specs=VMEM,
        scratch_shapes=[pltpu.VMEM((DIM, 2 * DIM), jnp.float32)],
        compiler_params=PARAMS,
        name="make_basis",
    )(*local(parts + [rows]))


def ring_parts(value, move):
    return [value] + [move(value, d) for d in (2, 1, -1)]


def ring_sum(parts):
    return (parts[0] + parts[1]) + (parts[2] + parts[3])


def shards(points, probes):
    order = (1, -1, 2)
    block, mine = pack(points, probes)
    near = [from_z(mine, d) for d in order]
    legs = [first_leg(block, d) for d in order]
    held = lax.optimization_barrier(near + legs)
    near, legs = held[:3], held[3:]
    early = [block] + legs
    early += [swap(v) for v in early]
    leg = jnp.concatenate([block] + legs)
    rest = [second_leg(leg, d) for d in (1, -1)]

    acc = sketch_part(near, early, None, False, True, "early")
    acc, leg, *rest = lax.optimization_barrier([acc, leg] + rest)
    across = second_leg(leg, 2)
    other = [swap(v) for v in rest]
    acc = sketch_part(near, rest, acc, False, True, "away_own")
    acc, across = lax.optimization_barrier([acc, across])
    far = swap(across)
    acc = sketch_part(near, other, acc, False, True, "away_other")
    away = sketch_part(near, [across, far], acc, True, True, "away_last")
    held = lax.optimization_barrier(list(away) + [mine])
    back = [from_z(v, -d) for v, d in zip(held[:3], order)]
    home, = sketch_part(held[3:], early + rest + other + [across, far], None, True, False, "home")
    rows, gram = finish_rows(home, *back)
    gram = gram + swap(gram)
    gram = ring_sum(ring_parts(gram, from_z))
    gram = ring_sum(ring_parts(gram, from_y))
    return rows, make_basis(ring_parts(gram, from_x), rows)


def solution(mesh):
    spec = P(AXES, None)
    return jax.shard_map(shards, mesh=mesh, in_specs=(spec, spec), out_specs=(spec, spec), check_vma=False)
```

time: 137 us -> 120 us (0.88)
  Pallas kernels: 59.3 us -> 43.4 us
  waiting for transfers between devices: 29.8 us -> 34.7 us
  other arithmetic: 3.5 us -> 0.04 us
  local copies, waits for them, and re-layouts: 4.38 us -> 2.58 us
    pallas_call x5 -> x7, Pallas kernels: 51.6 us -> 36.8 us  [the longest x5 36.1 us: sketch_part(): pl.pallas_call(body, out_shape=[pltpu.VMEM(shape, jnp.float32)] * nout if...]
    ppermute x29, waiting for transfers between devices: 29.8 us -> 34.7 us  [fetch(): return lax.ppermute(value, AXES, sorted(pairs))]
    add x5 -> x2, other arithmetic: 2.65 us -> 0.03 us  [ring_sum(): return parts[0] + parts[1] + (parts[2] + parts[3])]
    unnamed x28 -> x8, local copies, waits for them, and re-layouts: 4.29 us -> 2.56 us
  transfers between devices with their start and end apart: 29 -> 29, of which waited for: 14 -> 18; matrix products, arithmetic and copies ran while one was open for 2% -> 1% of each run, Pallas kernels for 22% -> 25%
where the time goes in v1:
time: 120 us
  Pallas kernels  43.4 us (36%)
  starting transfers between devices  37.9 us (32%)
  waiting for transfers between devices  34.7 us (29%)
  local copies, waits for them, and re-layouts  2.58 us (2%)
    ppermute x29, starting transfers between devices, fetch(): return lax.ppermute(value, AXES, sorted(pairs))  37.9 us
    pallas_call x5, Pallas kernels, sketch_part(): pl.pallas_call(body, out_shape=[pltpu.VMEM(shape, jnp.float32)] * nout if...  36.1 us
    ppermute x29, waiting for transfers between devices, fetch(): return lax.ppermute(value, AXES, sorted(pairs))  34.7 us
    pallas_call x1, Pallas kernels, make_basis(): pl.pallas_call(basis_body, out_shape=jax.ShapeDtypeStruct((BLK, DIM), jnp...  6.66 us
    unnamed x8, local copies, waits for them, and re-layouts  2.56 us
  transfers between devices with their start and end apart: 29, of which 18 were waited for; matrix products, arithmetic and copies ran while one was open for 1% of the time, Pallas kernels for 25%

profile of v1, /device:TPU:0, one launch (start us, length us, event | category | flops | bytes accessed | tf_op | source)
XLA Modules:
  0.0 119.5 jit_solution(10623126732486223443)
XLA Ops:
  0.6 0.9 copy-done
  1.5 0.9 copy-done.1
  2.7 4.0 %collective-permute-start.2 = (bf16[544,128]{1,0:T(8,128)(2,1)S(1)}, bf16[544,128]{1,0:T(8,128)(2,1)S(1)}, u32[]{:S(2)}, u32[]{:S(2)}) collective-permute-start(bf16[544,128]{1,0:T(8,128)(2,1)S(1)} %get-tuple-element.42.refs_0_), channel_id=1, source_target_pairs={{0,2},{1,3},{2,0},{3,1},{4,6},{5,7},{6,4},{7,5},{8,10},{9,11},{10,... | collective-permute-start | bytes 417800 | tf_op jit(solution)/shard_map/ppermute | solution.py:40
  6.7 3.0 %collective-permute-start.5 = (bf16[528,256]{1,0:T(8,128)(2,1)S(1)}, bf16[528,256]{1,0:T(8,128)(2,1)S(1)}, u32[]{:S(2)}, u32[]{:S(2)}) collective-permute-start(bf16[528,256]{1,0:T(8,128)(2,1)S(1)} %get-tuple-element.26.refs_3_.refs_1_), channel_id=1, source_target_pairs={{0,64},{1,65},{2,66},{3,67},{4,68},{5,69},{6,70},{7,71},{8,40},{9,... | collective-permute-start | bytes 811016 | tf_op jit(solution)/shard_map/ppermute | solution.py:40
  9.7 0.6 collective-permute-start.4
  10.3 2.6 %collective-permute-start.3 = (bf16[528,256]{1,0:T(8,128)(2,1)S(1)}, bf16[528,256]{1,0:T(8,128)(2,1)S(1)}, u32[]{:S(2)}, u32[]{:S(2)}) collective-permute-start(bf16[528,256]{1,0:T(8,128)(2,1)S(1)} %get-tuple-element.26.refs_3_.refs_1_), channel_id=1, source_target_pairs={{0,68},{1,69},{2,70},{3,71},{4,0},{5,1},{6,2},{7,3},{8,56},{9,57},... | collective-permute-start | bytes 811016 | tf_op jit(solution)/shard_map/ppermute | solution.py:40
  13.0 1.0 collective-permute-start.1
  14.0 2.2 %collective-permute-start = (bf16[544,128]{1,0:T(8,128)(2,1)S(1)}, bf16[544,128]{1,0:T(8,128)(2,1)S(1)}, u32[]{:S(2)}, u32[]{:S(2)}) collective-permute-start(bf16[544,128]{1,0:T(8,128)(2,1)S(1)} %get-tuple-element.42.refs_0_), channel_id=1, source_target_pairs={{0,3},{1,0},{2,1},{3,2},{4,7},{5,4},{6,5},{7,6},{8,11},{9,8},{10,9... | collective-permute-start | bytes 417800 | tf_op jit(solution)/shard_map/ppermute | solution.py:40
  16.2 3.0 %collective-permute-done.1.refs_1_ = bf16[544,128]{1,0:T(8,128)(2,1)S(1)} collective-permute-done((bf16[544,128]{1,0:T(8,128)(2,1)S(1)}, bf16[544,128]{1,0:T(8,128)(2,1)S(1)}, u32[]{:S(2)}, u32[]{:S(2)}) %collective-permute-start.1) | collective-permute-done | bytes 139296 | tf_op jit(solution)/shard_map/ppermute | solution.py:40
  19.3 1.6 %collective-permute-start.11 = (bf16[2112,256]{1,0:T(8,128)(2,1)S(1)}, bf16[2112,256]{1,0:T(8,128)(2,1)S(1)}, u32[]{:S(2)}, u32[]{:S(2)}) collective-permute-start(bf16[2112,256]{1,0:T(8,128)(2,1)S(1)} %constant_dynamic-update-slice_fusion), channel_id=1, source_target_pairs={{0,16},{1,17},{2,18},{3,19},{4,20},{5,21},{6,22},{7,23},{8,12},{9,... | collective-permute-start | bytes 3244040 | tf_op jit(solution)/shard_map/ppermute | solution.py:40
  21.0 1.7 %collective-permute-start.10 = (bf16[2112,256]{1,0:T(8,128)(2,1)S(1)}, bf16[2112,256]{1,0:T(8,128)(2,1)S(1)}, u32[]{:S(2)}, u32[]{:S(2)}) collective-permute-start(bf16[2112,256]{1,0:T(8,128)(2,1)S(1)} %constant_dynamic-update-slice_fusion), channel_id=1, source_target_pairs={{0,48},{1,49},{2,50},{3,51},{4,52},{5,53},{6,54},{7,55},{8,76},{9,... | collective-permute-start | bytes 3244040 | tf_op jit(solution)/shard_map/ppermute | solution.py:40
  22.6 0.5 collective-permute-start.7
  23.2 1.0 collective-permute-done.6.refs_7_.refs_5_
  24.6 0.4 collective-permute-done.8.refs_9_.refs_7_
  25.0 0.8 collective-permute-done.9.refs_10_.refs_8_
  25.7 6.7 %early.1.refs_5_ = f32[6,128,256]{2,1,0:T(8,128)S(1)} custom-call(bf16[544,128]{1,0:T(8,128)(2,1)S(1)} %collective-permute-done.refs_0_, bf16[544,128]{1,0:T(8,128)(2,1)S(1)} %collective-permute-done.1.refs_1_, bf16[544,128]{1,0:T(8,128)(2,1)S(1)} %collective-permute-done.2.refs_2_, bf16[528,256]{1,0:T(8,128)(2,1)S(1)} %get-tuple-element.26.refs_3_.refs_1_, ...), custom_call_target="tpu_custom_call" | custom-call | flops 4831838208 | bytes 5767168 | tf_op jit(solution)/shard_map/early/pallas_call | solution.py:205
  32.4 3.4 %collective-permute-done.11.refs_4_.refs_10_ = bf16[2112,256]{1,0:T(8,128)(2,1)S(1)} collective-permute-done((bf16[2112,256]{1,0:T(8,128)(2,1)S(1)}, bf16[2112,256]{1,0:T(8,128)(2,1)S(1)}, u32[]{:S(2)}, u32[]{:S(2)}) %collective-permute-start.11) | collective-permute-done | bytes 1081376 | tf_op jit(solution)/shard_map/ppermute | solution.py:40
  35.8 0.4 collective-permute-done.10.refs_3_.refs_9_
  36.1 2.9 %collective-permute-start.12 = (bf16[2112,256]{1,0:T(8,128)(2,1)S(1)}, bf16[2112,256]{1,0:T(8,128)(2,1)S(1)}, u32[]{:S(2)}, u32[]{:S(2)}) collective-permute-start(bf16[2112,256]{1,0:T(8,128)(2,1)S(1)} %constant_dynamic-update-slice_fusion), channel_id=1, source_target_pairs={{0,32},{1,33},{2,34},{3,35},{4,36},{5,37},{6,38},{7,39},{8,72},{9,... | collective-permute-start | bytes 3244040 | tf_op jit(solution)/shard_map/ppermute | solution.py:40
  39.0 0.5 collective-permute-start.15
  39.5 7.1 %away_own.1.refs_5_ = f32[6,128,256]{2,1,0:T(8,128)S(1)} custom-call(bf16[544,128]{1,0:T(8,128)(2,1)S(1)} %collective-permute-done.refs_0_, bf16[544,128]{1,0:T(8,128)(2,1)S(1)} %collective-permute-done.1.refs_1_, bf16[544,128]{1,0:T(8,128)(2,1)S(1)} %collective-permute-done.2.refs_2_, bf16[2112,256]{1,0:T(8,128)(2,1)S(1)} %collective-permute-done.10.refs_3_.refs_9_, ...), custom_call_target="tpu_custom_call" | custom-call | flops 4831838208 | bytes 5767168 | tf_op jit(solution)/shard_map/away_own/pallas_call | solution.py:205
  46.6 6.1 %collective-permute-done.12.refs_3_.refs_13_ = bf16[2112,256]{1,0:T(8,128)(2,1)S(1)} collective-permute-done((bf16[2112,256]{1,0:T(8,128)(2,1)S(1)}, bf16[2112,256]{1,0:T(8,128)(2,1)S(1)}, u32[]{:S(2)}, u32[]{:S(2)}) %collective-permute-start.12) | collective-permute-done | bytes 1081376 | tf_op jit(solution)/shard_map/ppermute | solution.py:40
  52.8 7.1 %away_other.1.refs_5_ = f32[6,128,256]{2,1,0:T(8,128)S(1)} custom-call(bf16[544,128]{1,0:T(8,128)(2,1)S(1)} %collective-permute-done.refs_0_, bf16[544,128]{1,0:T(8,128)(2,1)S(1)} %collective-permute-done.1.refs_1_, bf16[544,128]{1,0:T(8,128)(2,1)S(1)} %collective-permute-done.2.refs_2_, bf16[2112,256]{1,0:T(8,128)(2,1)S(1)} %collective-permute-done.14.refs_3_.refs_11_, ...), custom_call_target="tpu_custom_call" | custom-call | flops 4831838208 | bytes 5767168 | tf_op jit(solution)/shard_map/away_other/pallas_call | solution.py:205
  59.9 6.8 %away_last.1 = (f32[512,128]{1,0:T(8,128)S(1)}, f32[512,128]{1,0:T(8,128)S(1)}, f32[512,128]{1,0:T(8,128)S(1)}) custom-call(bf16[544,128]{1,0:T(8,128)(2,1)S(1)} %collective-permute-done.refs_0_, bf16[544,128]{1,0:T(8,128)(2,1)S(1)} %collective-permute-done.1.refs_1_, bf16[544,128]{1,0:T(8,128)(2,1)S(1)} %collective-permute-done.2.refs_2_, ...), custom_call_target="tpu_custom_call" | custom-call | flops 4831838208 | bytes 5767168 | tf_op jit(solution)/shard_map/away_last/pallas_call | solution.py:205
  66.8 3.3 %collective-permute-start.17 = (f32[512,128]{1,0:T(8,128)S(1)}, f32[512,128]{1,0:T(8,128)S(1)}, u32[]{:S(2)}, u32[]{:S(2)}) collective-permute-start(f32[512,128]{1,0:T(8,128)S(1)} %get-tuple-element.44), channel_id=1, source_target_pairs={{0,3},{1,0},{2,1},{3,2},{4,7},{5,4},{6,5},{7,6},{8,11},{9,8},{10,9... | collective-permute-start | bytes 786440 | tf_op jit(solution)/shard_map/ppermute | solution.py:40
  70.1 1.4 %collective-permute-start.18 = (f32[512,128]{1,0:T(8,128)S(1)}, f32[512,128]{1,0:T(8,128)S(1)}, u32[]{:S(2)}, u32[]{:S(2)}) collective-permute-start(f32[512,128]{1,0:T(8,128)S(1)} %get-tuple-element.45), channel_id=1, source_target_pairs={{0,2},{1,3},{2,0},{3,1},{4,6},{5,7},{6,4},{7,5},{8,10},{9,11},{10,... | collective-permute-start | bytes 786440 | tf_op jit(solution)/shard_map/ppermute | solution.py:40
  71.5 8.4 %home.1.home_ref = f32[512,128]{1,0:T(8,128)S(1)} custom-call(bf16[544,128]{1,0:T(8,128)(2,1)S(1)} %get-tuple-element.42.refs_0_, bf16[528,256]{1,0:T(8,128)(2,1)S(1)} %get-tuple-element.26.refs_3_.refs_1_, bf16[528,256]{1,0:T(8,128)(2,1)S(1)} %collective-permute-done.3.refs_4_.refs_2_, bf16[528,256]{1,0:T(8,128)(2,1)S(1)} %collective-permute-done.4.refs_5_.refs_3_, ...), custom_call_target="tpu_custom_call" | custom-call | flops 6442450944 | bytes 17301504 | tf_op jit(solution)/shard_map/home/pallas_call | solution.py:205
  80.0 2.0 %collective-permute-done.17.b_ref = f32[512,128]{1,0:T(8,128)S(1)} collective-permute-done((f32[512,128]{1,0:T(8,128)S(1)}, f32[512,128]{1,0:T(8,128)S(1)}, u32[]{:S(2)}, u32[]{:S(2)}) %collective-permute-start.17) | collective-permute-done | bytes 262176 | tf_op jit(solution)/shard_map/ppermute | solution.py:40
  82.0 1.8 %collective-permute-done.18.c_ref = f32[512,128]{1,0:T(8,128)S(1)} collective-permute-done((f32[512,128]{1,0:T(8,128)S(1)}, f32[512,128]{1,0:T(8,128)S(1)}, u32[]{:S(2)}, u32[]{:S(2)}) %collective-permute-start.18) | collective-permute-done | bytes 262176 | tf_op jit(solution)/shard_map/ppermute | solution.py:40
  83.8 0.4 finish_rows.1
  84.3 1.2 %collective-permute-done.19 = f32[128,128]{1,0:T(8,128)S(1)} collective-permute-done((f32[128,128]{1,0:T(8,128)S(1)}, f32[128,128]{1,0:T(8,128)S(1)}, u32[]{:S(2)}, u32[]{:S(2)}) %collective-permute-start.19) | collective-permute-done | bytes 65568 | tf_op jit(solution)/shard_map/ppermute | solution.py:40
  85.6 1.2 %collective-permute-start.22 = (f32[128,128]{1,0:T(8,128)S(1)}, f32[128,128]{1,0:T(8,128)S(1)}, u32[]{:S(2)}, u32[]{:S(2)}) collective-permute-start(f32[128,128]{1,0:T(8,128)S(1)} %add.21), channel_id=1, source_target_pairs={{0,1},{1,2},{2,3},{3,0},{4,5},{5,6},{6,7},{7,4},{8,9},{9,10},{10,1... | collective-permute-start | bytes 196616 | tf_op jit(solution)/shard_map/ppermute | solution.py:40
  86.8 2.1 %collective-permute-start.21 = (f32[128,128]{1,0:T(8,128)S(1)}, f32[128,128]{1,0:T(8,128)S(1)}, u32[]{:S(2)}, u32[]{:S(2)}) collective-permute-start(f32[128,128]{1,0:T(8,128)S(1)} %add.21), channel_id=1, source_target_pairs={{0,3},{1,0},{2,1},{3,2},{4,7},{5,4},{6,5},{7,6},{8,11},{9,8},{10,9... | collective-permute-start | bytes 196616 | tf_op jit(solution)/shard_map/ppermute | solution.py:40
  89.0 2.2 %collective-permute-done.22 = f32[128,128]{1,0:T(8,128)S(1)} collective-permute-done((f32[128,128]{1,0:T(8,128)S(1)}, f32[128,128]{1,0:T(8,128)S(1)}, u32[]{:S(2)}, u32[]{:S(2)}) %collective-permute-start.22) | collective-permute-done | bytes 65568 | tf_op jit(solution)/shard_map/ppermute | solution.py:40
  91.1 0.8 collective-permute-done.21
  91.9 2.8 %collective-permute-done.20 = f32[128,128]{1,0:T(8,128)S(1)} collective-permute-done((f32[128,128]{1,0:T(8,128)S(1)}, f32[128,128]{1,0:T(8,128)S(1)}, u32[]{:S(2)}, u32[]{:S(2)}) %collective-permute-start.20) | collective-permute-done | bytes 65568 | tf_op jit(solution)/shard_map/ppermute | solution.py:40
  94.7 1.6 %collective-permute-start.25 = (f32[128,128]{1,0:T(8,128)S(1)}, f32[128,128]{1,0:T(8,128)S(1)}, u32[]{:S(2)}, u32[]{:S(2)}) collective-permute-start(f32[128,128]{1,0:T(8,128)S(1)} %add_add_fusion.1), channel_id=1, source_target_pairs={{0,16},{1,17},{2,18},{3,19},{4,20},{5,21},{6,22},{7,23},{8,24},{9,... | collective-permute-start | bytes 196616 | tf_op jit(solution)/shard_map/ppermute | solution.py:40
  96.3 1.7 %collective-permute-start.24 = (f32[128,128]{1,0:T(8,128)S(1)}, f32[128,128]{1,0:T(8,128)S(1)}, u32[]{:S(2)}, u32[]{:S(2)}) collective-permute-start(f32[128,128]{1,0:T(8,128)S(1)} %add_add_fusion.1), channel_id=1, source_target_pairs={{0,48},{1,49},{2,50},{3,51},{4,52},{5,53},{6,54},{7,55},{8,56},{9,... | collective-permute-start | bytes 196616 | tf_op jit(solution)/shard_map/ppermute | solution.py:40
  98.0 1.7 %collective-permute-start.23 = (f32[128,128]{1,0:T(8,128)S(1)}, f32[128,128]{1,0:T(8,128)S(1)}, u32[]{:S(2)}, u32[]{:S(2)}) collective-permute-start(f32[128,128]{1,0:T(8,128)S(1)} %add_add_fusion.1), channel_id=1, source_target_pairs={{0,32},{1,33},{2,34},{3,35},{4,36},{5,37},{6,38},{7,39},{8,40},{9,... | collective-permute-start | bytes 196616 | tf_op jit(solution)/shard_map/ppermute | solution.py:40
  99.7 1.3 %collective-permute-done.25 = f32[128,128]{1,0:T(8,128)S(1)} collective-permute-done((f32[128,128]{1,0:T(8,128)S(1)}, f32[128,128]{1,0:T(8,128)S(1)}, u32[]{:S(2)}, u32[]{:S(2)}) %collective-permute-start.25) | collective-permute-done | bytes 65568 | tf_op jit(solution)/shard_map/ppermute | solution.py:40
  100.9 2.8 %collective-permute-done.23 = f32[128,128]{1,0:T(8,128)S(1)} collective-permute-done((f32[128,128]{1,0:T(8,128)S(1)}, f32[128,128]{1,0:T(8,128)S(1)}, u32[]{:S(2)}, u32[]{:S(2)}) %collective-permute-start.23) | collective-permute-done | bytes 65568 | tf_op jit(solution)/shard_map/ppermute | solution.py:40
  103.8 0.4 collective-permute-start.28
  104.2 2.9 %collective-permute-start.27 = (f32[128,128]{1,0:T(8,128)S(1)}, f32[128,128]{1,0:T(8,128)S(1)}, u32[]{:S(2)}, u32[]{:S(2)}) collective-permute-start(f32[128,128]{1,0:T(8,128)S(1)} %add_add_fusion.g_ref), channel_id=1, source_target_pairs={{0,68},{1,69},{2,70},{3,71},{4,0},{5,1},{6,2},{7,3},{8,76},{9,77},... | collective-permute-start | bytes 196616 | tf_op jit(solution)/shard_map/ppermute | solution.py:40
  107.1 0.5 collective-permute-start.26
  107.6 0.7 copy.7
  108.3 1.0 collective-permute-done.28.c_ref
  109.3 3.5 %collective-permute-done.26.a_ref = f32[128,128]{1,0:T(8,128)S(1)} collective-permute-done((f32[128,128]{1,0:T(8,128)S(1)}, f32[128,128]{1,0:T(8,128)S(1)}, u32[]{:S(2)}, u32[]{:S(2)}) %collective-permute-start.26) | collective-permute-done | bytes 65568 | tf_op jit(solution)/shard_map/ppermute | solution.py:40
  112.9 6.7 %make_basis.1 = f32[512,128]{1,0:T(8,128)} custom-call(f32[128,128]{1,0:T(8,128)S(1)} %add_add_fusion.g_ref, f32[128,128]{1,0:T(8,128)S(1)} %collective-permute-done.26.a_ref, f32[128,128]{1,0:T(8,128)S(1)} %collective-permute-done.27.b_ref, f32[128,128]{1,0:T(8,128)S(1)} %collective-permute-done.28.c_ref, f32[512,128]{1,0:T(8,128)S(1)} %get-tuple-element.48.rows_ref), custom_call_target="tpu_custom_call" | custom-call | tf_op jit(solution)/shard_map/make_basis/pallas_call | solution.py:286
  (30 shorter events, 1.0 us)
Async XLA Ops:
  0.6 0.9 copy-start
  1.5 0.9 copy-start.1
  2.7 11.3 %collective-permute-start.2 = (bf16[544,128]{1,0:T(8,128)(2,1)S(1)}, bf16[544,128]{1,0:T(8,128)(2,1)S(1)}, u32[]{:S(2)}, u32[]{:S(2)}) collective-permute-start(bf16[544,128]{1,0:T(8,128)(2,1)S(1)} %get-tuple-element.42.refs_0_), channel_id=1, source_target_pairs={{0,2},{1,3},{2,0},{3,1},{4,6},{5,7},{6,4},{7,5},{8,10},{9,11},{10,... | collective-permute-start | bytes 417800 | tf_op jit(solution)/shard_map/ppermute | solution.py:40
  6.7 12.5 %collective-permute-start.5 = (bf16[528,256]{1,0:T(8,128)(2,1)S(1)}, bf16[528,256]{1,0:T(8,128)(2,1)S(1)}, u32[]{:S(2)}, u32[]{:S(2)}) collective-permute-start(bf16[528,256]{1,0:T(8,128)(2,1)S(1)} %get-tuple-element.26.refs_3_.refs_1_), channel_id=1, source_target_pairs={{0,64},{1,65},{2,66},{3,67},{4,68},{5,69},{6,70},{7,71},{8,40},{9,... | collective-permute-start | bytes 811016 | tf_op jit(solution)/shard_map/ppermute | solution.py:40
  9.7 9.5 %collective-permute-start.4 = (bf16[528,256]{1,0:T(8,128)(2,1)S(1)}, bf16[528,256]{1,0:T(8,128)(2,1)S(1)}, u32[]{:S(2)}, u32[]{:S(2)}) collective-permute-start(bf16[528,256]{1,0:T(8,128)(2,1)S(1)} %get-tuple-element.26.refs_3_.refs_1_), channel_id=1, source_target_pairs={{0,4},{1,5},{2,6},{3,7},{4,64},{5,65},{6,66},{7,67},{8,24},{9,25},... | collective-permute-start | bytes 811016 | tf_op jit(solution)/shard_map/ppermute | solution.py:40
  10.3 8.9 %collective-permute-start.3 = (bf16[528,256]{1,0:T(8,128)(2,1)S(1)}, bf16[528,256]{1,0:T(8,128)(2,1)S(1)}, u32[]{:S(2)}, u32[]{:S(2)}) collective-permute-start(bf16[528,256]{1,0:T(8,128)(2,1)S(1)} %get-tuple-element.26.refs_3_.refs_1_), channel_id=1, source_target_pairs={{0,68},{1,69},{2,70},{3,71},{4,0},{5,1},{6,2},{7,3},{8,56},{9,57},... | collective-permute-start | bytes 811016 | tf_op jit(solution)/shard_map/ppermute | solution.py:40
  13.0 6.3 %collective-permute-start.1 = (bf16[544,128]{1,0:T(8,128)(2,1)S(1)}, bf16[544,128]{1,0:T(8,128)(2,1)S(1)}, u32[]{:S(2)}, u32[]{:S(2)}) collective-permute-start(bf16[544,128]{1,0:T(8,128)(2,1)S(1)} %get-tuple-element.42.refs_0_), channel_id=1, source_target_pairs={{0,1},{1,2},{2,3},{3,0},{4,5},{5,6},{6,7},{7,4},{8,9},{9,10},{10,1... | collective-permute-start | bytes 417800 | tf_op jit(solution)/shard_map/ppermute | solution.py:40
  14.0 5.2 %collective-permute-start = (bf16[544,128]{1,0:T(8,128)(2,1)S(1)}, bf16[544,128]{1,0:T(8,128)(2,1)S(1)}, u32[]{:S(2)}, u32[]{:S(2)}) collective-permute-start(bf16[544,128]{1,0:T(8,128)(2,1)S(1)} %get-tuple-element.42.refs_0_), channel_id=1, source_target_pairs={{0,3},{1,0},{2,1},{3,2},{4,7},{5,4},{6,5},{7,6},{8,11},{9,8},{10,9... | collective-permute-start | bytes 417800 | tf_op jit(solution)/shard_map/ppermute | solution.py:40
  19.3 16.4 %collective-permute-start.11 = (bf16[2112,256]{1,0:T(8,128)(2,1)S(1)}, bf16[2112,256]{1,0:T(8,128)(2,1)S(1)}, u32[]{:S(2)}, u32[]{:S(2)}) collective-permute-start(bf16[2112,256]{1,0:T(8,128)(2,1)S(1)} %constant_dynamic-update-slice_fusion), channel_id=1, source_target_pairs={{0,16},{1,17},{2,18},{3,19},{4,20},{5,21},{6,22},{7,23},{8,12},{9,... | collective-permute-start | bytes 3244040 | tf_op jit(solution)/shard_map/ppermute | solution.py:40
  21.0 15.2 %collective-permute-start.10 = (bf16[2112,256]{1,0:T(8,128)(2,1)S(1)}, bf16[2112,256]{1,0:T(8,128)(2,1)S(1)}, u32[]{:S(2)}, u32[]{:S(2)}) collective-permute-start(bf16[2112,256]{1,0:T(8,128)(2,1)S(1)} %constant_dynamic-update-slice_fusion), channel_id=1, source_target_pairs={{0,48},{1,49},{2,50},{3,51},{4,52},{5,53},{6,54},{7,55},{8,76},{9,... | collective-permute-start | bytes 3244040 | tf_op jit(solution)/shard_map/ppermute | solution.py:40
  22.6 1.5 %collective-permute-start.6 = (bf16[528,256]{1,0:T(8,128)(2,1)S(1)}, bf16[528,256]{1,0:T(8,128)(2,1)S(1)}, u32[]{:S(2)}, u32[]{:S(2)}) collective-permute-start(bf16[528,256]{1,0:T(8,128)(2,1)S(1)} %get-tuple-element.26.refs_3_.refs_1_), channel_id=1, source_target_pairs={{0,8},{1,9},{2,10},{3,11},{4,12},{5,13},{6,14},{7,15},{8,0},{9,1},... | collective-permute-start | bytes 811016 | tf_op jit(solution)/shard_map/ppermute | solution.py:40
  22.6 1.9 %collective-permute-start.7 = (bf16[528,256]{1,0:T(8,128)(2,1)S(1)}, bf16[528,256]{1,0:T(8,128)(2,1)S(1)}, u32[]{:S(2)}, u32[]{:S(2)}) collective-permute-start(bf16[528,256]{1,0:T(8,128)(2,1)S(1)} %collective-permute-done.3.refs_4_.refs_2_), channel_id=1, source_target_pairs={{0,8},{1,9},{2,10},{3,11},{4,12},{5,13},{6,14},{7,15},{8,0},{9,1},... | collective-permute-start | bytes 811016 | tf_op jit(solution)/shard_map/ppermute | solution.py:40
  23.2 1.8 %collective-permute-start.8 = (bf16[528,256]{1,0:T(8,128)(2,1)S(1)}, bf16[528,256]{1,0:T(8,128)(2,1)S(1)}, u32[]{:S(2)}, u32[]{:S(2)}) collective-permute-start(bf16[528,256]{1,0:T(8,128)(2,1)S(1)} %collective-permute-done.4.refs_5_.refs_3_), channel_id=1, source_target_pairs={{0,8},{1,9},{2,10},{3,11},{4,12},{5,13},{6,14},{7,15},{8,0},{9,1},... | collective-permute-start | bytes 811016 | tf_op jit(solution)/shard_map/ppermute | solution.py:40
  24.2 1.5 %collective-permute-start.9 = (bf16[528,256]{1,0:T(8,128)(2,1)S(1)}, bf16[528,256]{1,0:T(8,128)(2,1)S(1)}, u32[]{:S(2)}, u32[]{:S(2)}) collective-permute-start(bf16[528,256]{1,0:T(8,128)(2,1)S(1)} %collective-permute-done.5.refs_6_.refs_4_), channel_id=1, source_target_pairs={{0,8},{1,9},{2,10},{3,11},{4,12},{5,13},{6,14},{7,15},{8,0},{9,1},... | collective-permute-start | bytes 811016 | tf_op jit(solution)/shard_map/ppermute | solution.py:40
  36.1 16.7 %collective-permute-start.12 = (bf16[2112,256]{1,0:T(8,128)(2,1)S(1)}, bf16[2112,256]{1,0:T(8,128)(2,1)S(1)}, u32[]{:S(2)}, u32[]{:S(2)}) collective-permute-start(bf16[2112,256]{1,0:T(8,128)(2,1)S(1)} %constant_dynamic-update-slice_fusion), channel_id=1, source_target_pairs={{0,32},{1,33},{2,34},{3,35},{4,36},{5,37},{6,38},{7,39},{8,72},{9,... | collective-permute-start | bytes 3244040 | tf_op jit(solution)/shard_map/ppermute | solution.py:40
  39.0 13.8 %collective-permute-start.14 = (bf16[2112,256]{1,0:T(8,128)(2,1)S(1)}, bf16[2112,256]{1,0:T(8,128)(2,1)S(1)}, u32[]{:S(2)}, u32[]{:S(2)}) collective-permute-start(bf16[2112,256]{1,0:T(8,128)(2,1)S(1)} %collective-permute-done.10.refs_3_.refs_9_), channel_id=1, source_target_pairs={{0,8},{1,9},{2,10},{3,11},{4,12},{5,13},{6,14},{7,15},{8,0},{9,1},... | collective-permute-start | bytes 3244040 | tf_op jit(solution)/shard_map/ppermute | solution.py:40
  39.0 13.8 %collective-permute-start.15 = (bf16[2112,256]{1,0:T(8,128)(2,1)S(1)}, bf16[2112,256]{1,0:T(8,128)(2,1)S(1)}, u32[]{:S(2)}, u32[]{:S(2)}) collective-permute-start(bf16[2112,256]{1,0:T(8,128)(2,1)S(1)} %collective-permute-done.11.refs_4_.refs_10_), channel_id=1, source_target_pairs={{0,8},{1,9},{2,10},{3,11},{4,12},{5,13},{6,14},{7,15},{8,0},{9,1},... | collective-permute-start | bytes 3244040 | tf_op jit(solution)/shard_map/ppermute | solution.py:40
  52.8 7.1 %collective-permute-start.13 = (bf16[2112,256]{1,0:T(8,128)(2,1)S(1)}, bf16[2112,256]{1,0:T(8,128)(2,1)S(1)}, u32[]{:S(2)}, u32[]{:S(2)}) collective-permute-start(bf16[2112,256]{1,0:T(8,128)(2,1)S(1)} %collective-permute-done.12.refs_3_.refs_13_), channel_id=1, source_target_pairs={{0,8},{1,9},{2,10},{3,11},{4,12},{5,13},{6,14},{7,15},{8,0},{9,1},... | collective-permute-start | bytes 3244040 | tf_op jit(solution)/shard_map/ppermute | solution.py:40
  66.7 13.2 %collective-permute-start.16 = (f32[512,128]{1,0:T(8,128)S(1)}, f32[512,128]{1,0:T(8,128)S(1)}, u32[]{:S(2)}, u32[]{:S(2)}) collective-permute-start(f32[512,128]{1,0:T(8,128)S(1)} %get-tuple-element.43), channel_id=1, source_target_pairs={{0,1},{1,2},{2,3},{3,0},{4,5},{5,6},{6,7},{7,4},{8,9},{9,10},{10,1... | collective-permute-start | bytes 786440 | tf_op jit(solution)/shard_map/ppermute | solution.py:40
  66.8 15.1 %collective-permute-start.17 = (f32[512,128]{1,0:T(8,128)S(1)}, f32[512,128]{1,0:T(8,128)S(1)}, u32[]{:S(2)}, u32[]{:S(2)}) collective-permute-start(f32[512,128]{1,0:T(8,128)S(1)} %get-tuple-element.44), channel_id=1, source_target_pairs={{0,3},{1,0},{2,1},{3,2},{4,7},{5,4},{6,5},{7,6},{8,11},{9,8},{10,9... | collective-permute-start | bytes 786440 | tf_op jit(solution)/shard_map/ppermute | solution.py:40
  70.1 13.7 %collective-permute-start.18 = (f32[512,128]{1,0:T(8,128)S(1)}, f32[512,128]{1,0:T(8,128)S(1)}, u32[]{:S(2)}, u32[]{:S(2)}) collective-permute-start(f32[512,128]{1,0:T(8,128)S(1)} %get-tuple-element.45), channel_id=1, source_target_pairs={{0,2},{1,3},{2,0},{3,1},{4,6},{5,7},{6,4},{7,5},{8,10},{9,11},{10,... | collective-permute-start | bytes 786440 | tf_op jit(solution)/shard_map/ppermute | solution.py:40
  84.3 1.3 %collective-permute-start.19 = (f32[128,128]{1,0:T(8,128)S(1)}, f32[128,128]{1,0:T(8,128)S(1)}, u32[]{:S(2)}, u32[]{:S(2)}) collective-permute-start(f32[128,128]{1,0:T(8,128)S(1)} %get-tuple-element.47), channel_id=1, source_target_pairs={{0,8},{1,9},{2,10},{3,11},{4,12},{5,13},{6,14},{7,15},{8,0},{9,1},... | collective-permute-start | bytes 196616 | tf_op jit(solution)/shard_map/ppermute | solution.py:40
  85.6 5.5 %collective-permute-start.22 = (f32[128,128]{1,0:T(8,128)S(1)}, f32[128,128]{1,0:T(8,128)S(1)}, u32[]{:S(2)}, u32[]{:S(2)}) collective-permute-start(f32[128,128]{1,0:T(8,128)S(1)} %add.21), channel_id=1, source_target_pairs={{0,1},{1,2},{2,3},{3,0},{4,5},{5,6},{6,7},{7,4},{8,9},{9,10},{10,1... | collective-permute-start | bytes 196616 | tf_op jit(solution)/shard_map/ppermute | solution.py:40
  86.8 5.1 %collective-permute-start.21 = (f32[128,128]{1,0:T(8,128)S(1)}, f32[128,128]{1,0:T(8,128)S(1)}, u32[]{:S(2)}, u32[]{:S(2)}) collective-permute-start(f32[128,128]{1,0:T(8,128)S(1)} %add.21), channel_id=1, source_target_pairs={{0,3},{1,0},{2,1},{3,2},{4,7},{5,4},{6,5},{7,6},{8,11},{9,8},{10,9... | collective-permute-start | bytes 196616 | tf_op jit(solution)/shard_map/ppermute | solution.py:40
  88.9 5.8 %collective-permute-start.20 = (f32[128,128]{1,0:T(8,128)S(1)}, f32[128,128]{1,0:T(8,128)S(1)}, u32[]{:S(2)}, u32[]{:S(2)}) collective-permute-start(f32[128,128]{1,0:T(8,128)S(1)} %add.21), channel_id=1, source_target_pairs={{0,2},{1,3},{2,0},{3,1},{4,6},{5,7},{6,4},{7,5},{8,10},{9,11},{10,... | collective-permute-start | bytes 196616 | tf_op jit(solution)/shard_map/ppermute | solution.py:40
  94.7 6.2 %collective-permute-start.25 = (f32[128,128]{1,0:T(8,128)S(1)}, f32[128,128]{1,0:T(8,128)S(1)}, u32[]{:S(2)}, u32[]{:S(2)}) collective-permute-start(f32[128,128]{1,0:T(8,128)S(1)} %add_add_fusion.1), channel_id=1, source_target_pairs={{0,16},{1,17},{2,18},{3,19},{4,20},{5,21},{6,22},{7,23},{8,24},{9,... | collective-permute-start | bytes 196616 | tf_op jit(solution)/shard_map/ppermute | solution.py:40
  96.3 4.6 %collective-permute-start.24 = (f32[128,128]{1,0:T(8,128)S(1)}, f32[128,128]{1,0:T(8,128)S(1)}, u32[]{:S(2)}, u32[]{:S(2)}) collective-permute-start(f32[128,128]{1,0:T(8,128)S(1)} %add_add_fusion.1), channel_id=1, source_target_pairs={{0,48},{1,49},{2,50},{3,51},{4,52},{5,53},{6,54},{7,55},{8,56},{9,... | collective-permute-start | bytes 196616 | tf_op jit(solution)/shard_map/ppermute | solution.py:40
  98.0 5.8 %collective-permute-start.23 = (f32[128,128]{1,0:T(8,128)S(1)}, f32[128,128]{1,0:T(8,128)S(1)}, u32[]{:S(2)}, u32[]{:S(2)}) collective-permute-start(f32[128,128]{1,0:T(8,128)S(1)} %add_add_fusion.1), channel_id=1, source_target_pairs={{0,32},{1,33},{2,34},{3,35},{4,36},{5,37},{6,38},{7,39},{8,40},{9,... | collective-permute-start | bytes 196616 | tf_op jit(solution)/shard_map/ppermute | solution.py:40
  103.8 5.5 %collective-permute-start.28 = (f32[128,128]{1,0:T(8,128)S(1)}, f32[128,128]{1,0:T(8,128)S(1)}, u32[]{:S(2)}, u32[]{:S(2)}) collective-permute-start(f32[128,128]{1,0:T(8,128)S(1)} %add_add_fusion.g_ref), channel_id=1, source_target_pairs={{0,4},{1,5},{2,6},{3,7},{4,64},{5,65},{6,66},{7,67},{8,12},{9,13},... | collective-permute-start | bytes 196616 | tf_op jit(solution)/shard_map/ppermute | solution.py:40
  104.2 5.2 %collective-permute-start.27 = (f32[128,128]{1,0:T(8,128)S(1)}, f32[128,128]{1,0:T(8,128)S(1)}, u32[]{:S(2)}, u32[]{:S(2)}) collective-permute-start(f32[128,128]{1,0:T(8,128)S(1)} %add_add_fusion.g_ref), channel_id=1, source_target_pairs={{0,68},{1,69},{2,70},{3,71},{4,0},{5,1},{6,2},{7,3},{8,76},{9,77},... | collective-permute-start | bytes 196616 | tf_op jit(solution)/shard_map/ppermute | solution.py:40
  107.1 5.8 %collective-permute-start.26 = (f32[128,128]{1,0:T(8,128)S(1)}, f32[128,128]{1,0:T(8,128)S(1)}, u32[]{:S(2)}, u32[]{:S(2)}) collective-permute-start(f32[128,128]{1,0:T(8,128)S(1)} %add_add_fusion.g_ref), channel_id=1, source_target_pairs={{0,64},{1,65},{2,66},{3,67},{4,68},{5,69},{6,70},{7,71},{8,72},{9,... | collective-permute-start | bytes 196616 | tf_op jit(solution)/shard_map/ppermute | solution.py:40

commit v2 on v1

--- a/solution.py
+++ b/solution.py
@@ -315,17 +315,18 @@
     rest = [second_leg(leg, d) for d in (1, -1)]
 
     acc = sketch_part(near, early, None, False, True, "early")
-    acc, leg, *rest = lax.optimization_barrier([acc, leg] + rest)
-    across = second_leg(leg, 2)
+    acc, *rest = lax.optimization_barrier([acc] + rest)
+    mid = 2 * COLS
+    across = [second_leg(rest[0][:mid], 1), second_leg(rest[1][mid:], -1)]
     other = [swap(v) for v in rest]
     acc = sketch_part(near, rest, acc, False, True, "away_own")
-    acc, across = lax.optimization_barrier([acc, across])
-    far = swap(across)
+    acc, *across = lax.optimization_barrier([acc] + across)
+    far = [swap(v) for v in across]
     acc = sketch_part(near, other, acc, False, True, "away_other")
-    away = sketch_part(near, [across, far], acc, True, True, "away_last")
+    away = sketch_part(near, across + far, acc, True, True, "away_last")
     held = lax.optimization_barrier(list(away) + [mine])
     back = [from_z(v, -d) for v, d in zip(held[:3], order)]
-    home, = sketch_part(held[3:], early + rest + other + [across, far], None, True, False, "home")
+    home, = sketch_part(held[3:], early + rest + other + across + far, None, True, False, "home")
     rows, gram = finish_rows(home, *back)
     gram = gram + swap(gram)
     gram = ring_sum(ring_parts(gram, from_z))

time: 120 us -> 114 us (0.950)
  waiting for transfers between devices: 34.7 us -> 29.4 us
    ppermute x29 -> x31, waiting for transfers between devices: 34.7 us -> 29.4 us  [fetch(): return lax.ppermute(value, AXES, sorted(pairs))]
    pallas_call x5, Pallas kernels: 36.1 us -> 34.9 us  [sketch_part(): pl.pallas_call(body, out_shape=[pltpu.VMEM(shape, jnp.float32)] * nout if...]
    ppermute x29 -> x31, starting transfers between devices: 37.9 us -> 38.5 us  [fetch(): return lax.ppermute(value, AXES, sorted(pairs))]
  transfers between devices with their start and end apart: 29 -> 31, of which waited for: 18 -> 19; matrix products, arithmetic and copies ran while one was open for 1% -> 1% of each run, Pallas kernels for 25% -> 25%
where the time goes in v2:
time: 114 us
  Pallas kernels  42.2 us (37%)
  starting transfers between devices  38.5 us (34%)
  waiting for transfers between devices  29.4 us (26%)
  local copies, waits for them, and re-layouts  2.65 us (2%)
    ppermute x31, starting transfers between devices, fetch(): return lax.ppermute(value, AXES, sorted(pairs))  38.5 us
    pallas_call x5, Pallas kernels, sketch_part(): pl.pallas_call(body, out_shape=[pltpu.VMEM(shape, jnp.float32)] * nout if...  34.9 us
    ppermute x31, waiting for transfers between devices, fetch(): return lax.ppermute(value, AXES, sorted(pairs))  29.4 us
    pallas_call x1, Pallas kernels, make_basis(): pl.pallas_call(basis_body, out_shape=jax.ShapeDtypeStruct((BLK, DIM), jnp...  6.66 us
    unnamed x8, local copies, waits for them, and re-layouts  2.56 us
  transfers between devices with their start and end apart: 31, of which 19 were waited for; matrix products, arithmetic and copies ran while one was open for 1% of the time, Pallas kernels for 25%

profile of v2, /device:TPU:0, one launch (start us, length us, event | category | flops | bytes accessed | tf_op | source)
XLA Modules:
  0.0 113.6 jit_solution(7650911205982885075)
XLA Ops:
  0.6 0.9 copy-done
  1.5 0.9 copy-done.1
  2.7 4.0 %collective-permute-start.2 = (bf16[544,128]{1,0:T(8,128)(2,1)S(1)}, bf16[544,128]{1,0:T(8,128)(2,1)S(1)}, u32[]{:S(2)}, u32[]{:S(2)}) collective-permute-start(bf16[544,128]{1,0:T(8,128)(2,1)S(1)} %get-tuple-element.42.refs_0_), channel_id=1, source_target_pairs={{0,2},{1,3},{2,0},{3,1},{4,6},{5,7},{6,4},{7,5},{8,10},{9,11},{10,... | collective-permute-start | bytes 417800 | tf_op jit(solution)/shard_map/ppermute | solution.py:40
  6.7 3.0 %collective-permute-start.5 = (bf16[528,256]{1,0:T(8,128)(2,1)S(1)}, bf16[528,256]{1,0:T(8,128)(2,1)S(1)}, u32[]{:S(2)}, u32[]{:S(2)}) collective-permute-start(bf16[528,256]{1,0:T(8,128)(2,1)S(1)} %get-tuple-element.26.refs_3_.refs_1_), channel_id=1, source_target_pairs={{0,64},{1,65},{2,66},{3,67},{4,68},{5,69},{6,70},{7,71},{8,40},{9,... | collective-permute-start | bytes 811016 | tf_op jit(solution)/shard_map/ppermute | solution.py:40
  9.7 0.6 collective-permute-start.4
  10.3 2.6 %collective-permute-start.3 = (bf16[528,256]{1,0:T(8,128)(2,1)S(1)}, bf16[528,256]{1,0:T(8,128)(2,1)S(1)}, u32[]{:S(2)}, u32[]{:S(2)}) collective-permute-start(bf16[528,256]{1,0:T(8,128)(2,1)S(1)} %get-tuple-element.26.refs_3_.refs_1_), channel_id=1, source_target_pairs={{0,68},{1,69},{2,70},{3,71},{4,0},{5,1},{6,2},{7,3},{8,56},{9,57},... | collective-permute-start | bytes 811016 | tf_op jit(solution)/shard_map/ppermute | solution.py:40
  13.0 1.0 collective-permute-start.1
  14.0 2.2 %collective-permute-start = (bf16[544,128]{1,0:T(8,128)(2,1)S(1)}, bf16[544,128]{1,0:T(8,128)(2,1)S(1)}, u32[]{:S(2)}, u32[]{:S(2)}) collective-permute-start(bf16[544,128]{1,0:T(8,128)(2,1)S(1)} %get-tuple-element.42.refs_0_), channel_id=1, source_target_pairs={{0,3},{1,0},{2,1},{3,2},{4,7},{5,4},{6,5},{7,6},{8,11},{9,8},{10,9... | collective-permute-start | bytes 417800 | tf_op jit(solution)/shard_map/ppermute | solution.py:40
  16.2 3.0 %collective-permute-done.1.refs_1_ = bf16[544,128]{1,0:T(8,128)(2,1)S(1)} collective-permute-done((bf16[544,128]{1,0:T(8,128)(2,1)S(1)}, bf16[544,128]{1,0:T(8,128)(2,1)S(1)}, u32[]{:S(2)}, u32[]{:S(2)}) %collective-permute-start.1) | collective-permute-done | bytes 139296 | tf_op jit(solution)/shard_map/ppermute | solution.py:40
  19.3 1.6 %collective-permute-start.11 = (bf16[2112,256]{1,0:T(8,128)(2,1)S(1)}, bf16[2112,256]{1,0:T(8,128)(2,1)S(1)}, u32[]{:S(2)}, u32[]{:S(2)}) collective-permute-start(bf16[2112,256]{1,0:T(8,128)(2,1)S(1)} %constant_dynamic-update-slice_fusion), channel_id=1, source_target_pairs={{0,16},{1,17},{2,18},{3,19},{4,20},{5,21},{6,22},{7,23},{8,12},{9,... | collective-permute-start | bytes 3244040 | tf_op jit(solution)/shard_map/ppermute | solution.py:40
  21.0 1.7 %collective-permute-start.10 = (bf16[2112,256]{1,0:T(8,128)(2,1)S(1)}, bf16[2112,256]{1,0:T(8,128)(2,1)S(1)}, u32[]{:S(2)}, u32[]{:S(2)}) collective-permute-start(bf16[2112,256]{1,0:T(8,128)(2,1)S(1)} %constant_dynamic-update-slice_fusion), channel_id=1, source_target_pairs={{0,48},{1,49},{2,50},{3,51},{4,52},{5,53},{6,54},{7,55},{8,76},{9,... | collective-permute-start | bytes 3244040 | tf_op jit(solution)/shard_map/ppermute | solution.py:40
  22.6 0.5 collective-permute-start.7
  23.2 1.0 collective-permute-done.6.refs_7_.refs_5_
  24.6 0.4 collective-permute-done.8.refs_9_.refs_7_
  25.0 0.8 collective-permute-done.9.refs_10_.refs_8_
  25.7 6.6 %early.1.refs_5_ = f32[6,128,256]{2,1,0:T(8,128)S(1)} custom-call(bf16[544,128]{1,0:T(8,128)(2,1)S(1)} %collective-permute-done.refs_0_, bf16[544,128]{1,0:T(8,128)(2,1)S(1)} %collective-permute-done.1.refs_1_, bf16[544,128]{1,0:T(8,128)(2,1)S(1)} %collective-permute-done.2.refs_2_, bf16[528,256]{1,0:T(8,128)(2,1)S(1)} %get-tuple-element.26.refs_3_.refs_1_, ...), custom_call_target="tpu_custom_call" | custom-call | flops 4831838208 | bytes 5767168 | tf_op jit(solution)/shard_map/early/pallas_call | solution.py:205
  32.4 3.4 %collective-permute-done.11.refs_4_.refs_10_ = bf16[2112,256]{1,0:T(8,128)(2,1)S(1)} collective-permute-done((bf16[2112,256]{1,0:T(8,128)(2,1)S(1)}, bf16[2112,256]{1,0:T(8,128)(2,1)S(1)}, u32[]{:S(2)}, u32[]{:S(2)}) %collective-permute-start.11) | collective-permute-done | bytes 1081376 | tf_op jit(solution)/shard_map/ppermute | solution.py:40
  35.8 0.4 collective-permute-done.10.refs_3_.refs_9_
  36.1 0.5 collective-permute-start.17
  36.7 1.6 %collective-permute-start.13 = (bf16[1056,256]{1,0:T(8,128)(2,1)S(1)}, bf16[1056,256]{1,0:T(8,128)(2,1)S(1)}, u32[]{:S(2)}, u32[]{:S(2)}) collective-permute-start(bf16[1056,256]{1,0:T(8,128)(2,1)S(1)} %slice.7), channel_id=1, source_target_pairs={{0,16},{1,17},{2,18},{3,19},{4,20},{5,21},{6,22},{7,23},{8,12},{9,... | collective-permute-start | bytes 1622024 | tf_op jit(solution)/shard_map/ppermute | solution.py:40
  38.4 1.7 %collective-permute-start.12 = (bf16[1056,256]{1,0:T(8,128)(2,1)S(1)}, bf16[1056,256]{1,0:T(8,128)(2,1)S(1)}, u32[]{:S(2)}, u32[]{:S(2)}) collective-permute-start(bf16[1056,256]{1,0:T(8,128)(2,1)S(1)} %slice.6), channel_id=1, source_target_pairs={{0,48},{1,49},{2,50},{3,51},{4,52},{5,53},{6,54},{7,55},{8,76},{9,... | collective-permute-start | bytes 1622024 | tf_op jit(solution)/shard_map/ppermute | solution.py:40
  40.0 7.1 %away_own.1.refs_5_ = f32[6,128,256]{2,1,0:T(8,128)S(1)} custom-call(bf16[544,128]{1,0:T(8,128)(2,1)S(1)} %collective-permute-done.refs_0_, bf16[544,128]{1,0:T(8,128)(2,1)S(1)} %collective-permute-done.1.refs_1_, bf16[544,128]{1,0:T(8,128)(2,1)S(1)} %collective-permute-done.2.refs_2_, bf16[2112,256]{1,0:T(8,128)(2,1)S(1)} %collective-permute-done.10.refs_3_.refs_9_, ...), custom_call_target="tpu_custom_call" | custom-call | flops 4831838208 | bytes 5767168 | tf_op jit(solution)/shard_map/away_own/pallas_call | solution.py:205
  47.4 0.4 collective-permute-done.12.refs_3_.refs_13_
  47.7 0.5 collective-permute-start.15
  48.2 6.4 %away_other.1.refs_7_ = f32[6,128,256]{2,1,0:T(8,128)S(1)} custom-call(bf16[544,128]{1,0:T(8,128)(2,1)S(1)} %collective-permute-done.refs_0_, bf16[544,128]{1,0:T(8,128)(2,1)S(1)} %collective-permute-done.1.refs_1_, bf16[544,128]{1,0:T(8,128)(2,1)S(1)} %collective-permute-done.2.refs_2_, bf16[2112,256]{1,0:T(8,128)(2,1)S(1)} %collective-permute-done.16.refs_3_.refs_11_, ...), custom_call_target="tpu_custom_call" | custom-call | flops 4831838208 | bytes 5767168 | tf_op jit(solution)/shard_map/away_other/pallas_call | solution.py:205
  54.7 6.6 %away_last.1 = (f32[512,128]{1,0:T(8,128)S(1)}, f32[512,128]{1,0:T(8,128)S(1)}, f32[512,128]{1,0:T(8,128)S(1)}) custom-call(bf16[544,128]{1,0:T(8,128)(2,1)S(1)} %collective-permute-done.refs_0_, bf16[544,128]{1,0:T(8,128)(2,1)S(1)} %collective-permute-done.1.refs_1_, bf16[544,128]{1,0:T(8,128)(2,1)S(1)} %collective-permute-done.2.refs_2_, ...), custom_call_target="tpu_custom_call" | custom-call | flops 4831838208 | bytes 5767168 | tf_op jit(solution)/shard_map/away_last/pallas_call | solution.py:205
  61.4 3.3 %collective-permute-start.19 = (f32[512,128]{1,0:T(8,128)S(1)}, f32[512,128]{1,0:T(8,128)S(1)}, u32[]{:S(2)}, u32[]{:S(2)}) collective-permute-start(f32[512,128]{1,0:T(8,128)S(1)} %get-tuple-element.44), channel_id=1, source_target_pairs={{0,3},{1,0},{2,1},{3,2},{4,7},{5,4},{6,5},{7,6},{8,11},{9,8},{10,9... | collective-permute-start | bytes 786440 | tf_op jit(solution)/shard_map/ppermute | solution.py:40
  64.7 1.4 %collective-permute-start.20 = (f32[512,128]{1,0:T(8,128)S(1)}, f32[512,128]{1,0:T(8,128)S(1)}, u32[]{:S(2)}, u32[]{:S(2)}) collective-permute-start(f32[512,128]{1,0:T(8,128)S(1)} %get-tuple-element.45), channel_id=1, source_target_pairs={{0,2},{1,3},{2,0},{3,1},{4,6},{5,7},{6,4},{7,5},{8,10},{9,11},{10,... | collective-permute-start | bytes 786440 | tf_op jit(solution)/shard_map/ppermute | solution.py:40
  66.1 8.2 %home.1.home_ref = f32[512,128]{1,0:T(8,128)S(1)} custom-call(bf16[544,128]{1,0:T(8,128)(2,1)S(1)} %get-tuple-element.42.refs_0_, bf16[528,256]{1,0:T(8,128)(2,1)S(1)} %get-tuple-element.26.refs_3_.refs_1_, bf16[528,256]{1,0:T(8,128)(2,1)S(1)} %collective-permute-done.3.refs_4_.refs_2_, bf16[528,256]{1,0:T(8,128)(2,1)S(1)} %collective-permute-done.4.refs_5_.refs_3_, ...), custom_call_target="tpu_custom_call" | custom-call | flops 6442450944 | bytes 17301504 | tf_op jit(solution)/shard_map/home/pallas_call | solution.py:205
  74.3 1.8 %collective-permute-done.19.b_ref = f32[512,128]{1,0:T(8,128)S(1)} collective-permute-done((f32[512,128]{1,0:T(8,128)S(1)}, f32[512,128]{1,0:T(8,128)S(1)}, u32[]{:S(2)}, u32[]{:S(2)}) %collective-permute-start.19) | collective-permute-done | bytes 262176 | tf_op jit(solution)/shard_map/ppermute | solution.py:40
  76.1 1.8 %collective-permute-done.20.c_ref = f32[512,128]{1,0:T(8,128)S(1)} collective-permute-done((f32[512,128]{1,0:T(8,128)S(1)}, f32[512,128]{1,0:T(8,128)S(1)}, u32[]{:S(2)}, u32[]{:S(2)}) %collective-permute-start.20) | collective-permute-done | bytes 262176 | tf_op jit(solution)/shard_map/ppermute | solution.py:40
  77.9 0.4 finish_rows.1
  78.5 1.2 %collective-permute-done.21 = f32[128,128]{1,0:T(8,128)S(1)} collective-permute-done((f32[128,128]{1,0:T(8,128)S(1)}, f32[128,128]{1,0:T(8,128)S(1)}, u32[]{:S(2)}, u32[]{:S(2)}) %collective-permute-start.21) | collective-permute-done | bytes 65568 | tf_op jit(solution)/shard_map/ppermute | solution.py:40
  79.7 1.2 %collective-permute-start.24 = (f32[128,128]{1,0:T(8,128)S(1)}, f32[128,128]{1,0:T(8,128)S(1)}, u32[]{:S(2)}, u32[]{:S(2)}) collective-permute-start(f32[128,128]{1,0:T(8,128)S(1)} %add.21), channel_id=1, source_target_pairs={{0,1},{1,2},{2,3},{3,0},{4,5},{5,6},{6,7},{7,4},{8,9},{9,10},{10,1... | collective-permute-start | bytes 196616 | tf_op jit(solution)/shard_map/ppermute | solution.py:40
  80.9 2.1 %collective-permute-start.23 = (f32[128,128]{1,0:T(8,128)S(1)}, f32[128,128]{1,0:T(8,128)S(1)}, u32[]{:S(2)}, u32[]{:S(2)}) collective-permute-start(f32[128,128]{1,0:T(8,128)S(1)} %add.21), channel_id=1, source_target_pairs={{0,3},{1,0},{2,1},{3,2},{4,7},{5,4},{6,5},{7,6},{8,11},{9,8},{10,9... | collective-permute-start | bytes 196616 | tf_op jit(solution)/shard_map/ppermute | solution.py:40
  83.1 2.2 %collective-permute-done.24 = f32[128,128]{1,0:T(8,128)S(1)} collective-permute-done((f32[128,128]{1,0:T(8,128)S(1)}, f32[128,128]{1,0:T(8,128)S(1)}, u32[]{:S(2)}, u32[]{:S(2)}) %collective-permute-start.24) | collective-permute-done | bytes 65568 | tf_op jit(solution)/shard_map/ppermute | solution.py:40
  85.3 0.8 collective-permute-done.23
  86.0 2.8 %collective-permute-done.22 = f32[128,128]{1,0:T(8,128)S(1)} collective-permute-done((f32[128,128]{1,0:T(8,128)S(1)}, f32[128,128]{1,0:T(8,128)S(1)}, u32[]{:S(2)}, u32[]{:S(2)}) %collective-permute-start.22) | collective-permute-done | bytes 65568 | tf_op jit(solution)/shard_map/ppermute | solution.py:40
  88.8 1.4 %collective-permute-start.27 = (f32[128,128]{1,0:T(8,128)S(1)}, f32[128,128]{1,0:T(8,128)S(1)}, u32[]{:S(2)}, u32[]{:S(2)}) collective-permute-start(f32[128,128]{1,0:T(8,128)S(1)} %add_add_fusion.1), channel_id=1, source_target_pairs={{0,16},{1,17},{2,18},{3,19},{4,20},{5,21},{6,22},{7,23},{8,24},{9,... | collective-permute-start | bytes 196616 | tf_op jit(solution)/shard_map/ppermute | solution.py:40
  90.2 2.0 %collective-permute-start.26 = (f32[128,128]{1,0:T(8,128)S(1)}, f32[128,128]{1,0:T(8,128)S(1)}, u32[]{:S(2)}, u32[]{:S(2)}) collective-permute-start(f32[128,128]{1,0:T(8,128)S(1)} %add_add_fusion.1), channel_id=1, source_target_pairs={{0,48},{1,49},{2,50},{3,51},{4,52},{5,53},{6,54},{7,55},{8,56},{9,... | collective-permute-start | bytes 196616 | tf_op jit(solution)/shard_map/ppermute | solution.py:40
  92.1 1.5 %collective-permute-start.25 = (f32[128,128]{1,0:T(8,128)S(1)}, f32[128,128]{1,0:T(8,128)S(1)}, u32[]{:S(2)}, u32[]{:S(2)}) collective-permute-start(f32[128,128]{1,0:T(8,128)S(1)} %add_add_fusion.1), channel_id=1, source_target_pairs={{0,32},{1,33},{2,34},{3,35},{4,36},{5,37},{6,38},{7,39},{8,40},{9,... | collective-permute-start | bytes 196616 | tf_op jit(solution)/shard_map/ppermute | solution.py:40
  93.6 1.4 %collective-permute-done.27 = f32[128,128]{1,0:T(8,128)S(1)} collective-permute-done((f32[128,128]{1,0:T(8,128)S(1)}, f32[128,128]{1,0:T(8,128)S(1)}, u32[]{:S(2)}, u32[]{:S(2)}) %collective-permute-start.27) | collective-permute-done | bytes 65568 | tf_op jit(solution)/shard_map/ppermute | solution.py:40
  95.1 2.8 %collective-permute-done.25 = f32[128,128]{1,0:T(8,128)S(1)} collective-permute-done((f32[128,128]{1,0:T(8,128)S(1)}, f32[128,128]{1,0:T(8,128)S(1)}, u32[]{:S(2)}, u32[]{:S(2)}) %collective-permute-start.25) | collective-permute-done | bytes 65568 | tf_op jit(solution)/shard_map/ppermute | solution.py:40
  98.1 3.1 %collective-permute-start.29 = (f32[128,128]{1,0:T(8,128)S(1)}, f32[128,128]{1,0:T(8,128)S(1)}, u32[]{:S(2)}, u32[]{:S(2)}) collective-permute-start(f32[128,128]{1,0:T(8,128)S(1)} %add_add_fusion.g_ref), channel_id=1, source_target_pairs={{0,68},{1,69},{2,70},{3,71},{4,0},{5,1},{6,2},{7,3},{8,76},{9,77},... | collective-permute-start | bytes 196616 | tf_op jit(solution)/shard_map/ppermute | solution.py:40
  101.5 0.7 copy.7
  102.2 1.2 %collective-permute-done.30.c_ref = f32[128,128]{1,0:T(8,128)S(1)} collective-permute-done((f32[128,128]{1,0:T(8,128)S(1)}, f32[128,128]{1,0:T(8,128)S(1)}, u32[]{:S(2)}, u32[]{:S(2)}) %collective-permute-start.30) | collective-permute-done | bytes 65568 | tf_op jit(solution)/shard_map/ppermute | solution.py:40
  103.4 3.5 %collective-permute-done.28.a_ref = f32[128,128]{1,0:T(8,128)S(1)} collective-permute-done((f32[128,128]{1,0:T(8,128)S(1)}, f32[128,128]{1,0:T(8,128)S(1)}, u32[]{:S(2)}, u32[]{:S(2)}) %collective-permute-start.28) | collective-permute-done | bytes 65568 | tf_op jit(solution)/shard_map/ppermute | solution.py:40
  107.0 6.7 %make_basis.1 = f32[512,128]{1,0:T(8,128)} custom-call(f32[128,128]{1,0:T(8,128)S(1)} %add_add_fusion.g_ref, f32[128,128]{1,0:T(8,128)S(1)} %collective-permute-done.28.a_ref, f32[128,128]{1,0:T(8,128)S(1)} %collective-permute-done.29.b_ref, f32[128,128]{1,0:T(8,128)S(1)} %collective-permute-done.30.c_ref, f32[512,128]{1,0:T(8,128)S(1)} %get-tuple-element.48.rows_ref), custom_call_target="tpu_custom_call" | custom-call | tf_op jit(solution)/shard_map/make_basis/pallas_call | solution.py:286
  (36 shorter events, 1.8 us)
Async XLA Ops:
  0.6 0.9 copy-start
  1.5 0.9 copy-start.1
  2.7 11.3 %collective-permute-start.2 = (bf16[544,128]{1,0:T(8,128)(2,1)S(1)}, bf16[544,128]{1,0:T(8,128)(2,1)S(1)}, u32[]{:S(2)}, u32[]{:S(2)}) collective-permute-start(bf16[544,128]{1,0:T(8,128)(2,1)S(1)} %get-tuple-element.42.refs_0_), channel_id=1, source_target_pairs={{0,2},{1,3},{2,0},{3,1},{4,6},{5,7},{6,4},{7,5},{8,10},{9,11},{10,... | collective-permute-start | bytes 417800 | tf_op jit(solution)/shard_map/ppermute | solution.py:40
  6.7 12.5 %collective-permute-start.5 = (bf16[528,256]{1,0:T(8,128)(2,1)S(1)}, bf16[528,256]{1,0:T(8,128)(2,1)S(1)}, u32[]{:S(2)}, u32[]{:S(2)}) collective-permute-start(bf16[528,256]{1,0:T(8,128)(2,1)S(1)} %get-tuple-element.26.refs_3_.refs_1_), channel_id=1, source_target_pairs={{0,64},{1,65},{2,66},{3,67},{4,68},{5,69},{6,70},{7,71},{8,40},{9,... | collective-permute-start | bytes 811016 | tf_op jit(solution)/shard_map/ppermute | solution.py:40
  9.7 9.5 %collective-permute-start.4 = (bf16[528,256]{1,0:T(8,128)(2,1)S(1)}, bf16[528,256]{1,0:T(8,128)(2,1)S(1)}, u32[]{:S(2)}, u32[]{:S(2)}) collective-permute-start(bf16[528,256]{1,0:T(8,128)(2,1)S(1)} %get-tuple-element.26.refs_3_.refs_1_), channel_id=1, source_target_pairs={{0,4},{1,5},{2,6},{3,7},{4,64},{5,65},{6,66},{7,67},{8,24},{9,25},... | collective-permute-start | bytes 811016 | tf_op jit(solution)/shard_map/ppermute | solution.py:40
  10.3 8.9 %collective-permute-start.3 = (bf16[528,256]{1,0:T(8,128)(2,1)S(1)}, bf16[528,256]{1,0:T(8,128)(2,1)S(1)}, u32[]{:S(2)}, u32[]{:S(2)}) collective-permute-start(bf16[528,256]{1,0:T(8,128)(2,1)S(1)} %get-tuple-element.26.refs_3_.refs_1_), channel_id=1, source_target_pairs={{0,68},{1,69},{2,70},{3,71},{4,0},{5,1},{6,2},{7,3},{8,56},{9,57},... | collective-permute-start | bytes 811016 | tf_op jit(solution)/shard_map/ppermute | solution.py:40
  13.0 6.3 %collective-permute-start.1 = (bf16[544,128]{1,0:T(8,128)(2,1)S(1)}, bf16[544,128]{1,0:T(8,128)(2,1)S(1)}, u32[]{:S(2)}, u32[]{:S(2)}) collective-permute-start(bf16[544,128]{1,0:T(8,128)(2,1)S(1)} %get-tuple-element.42.refs_0_), channel_id=1, source_target_pairs={{0,1},{1,2},{2,3},{3,0},{4,5},{5,6},{6,7},{7,4},{8,9},{9,10},{10,1... | collective-permute-start | bytes 417800 | tf_op jit(solution)/shard_map/ppermute | solution.py:40
  14.0 5.2 %collective-permute-start = (bf16[544,128]{1,0:T(8,128)(2,1)S(1)}, bf16[544,128]{1,0:T(8,128)(2,1)S(1)}, u32[]{:S(2)}, u32[]{:S(2)}) collective-permute-start(bf16[544,128]{1,0:T(8,128)(2,1)S(1)} %get-tuple-element.42.refs_0_), channel_id=1, source_target_pairs={{0,3},{1,0},{2,1},{3,2},{4,7},{5,4},{6,5},{7,6},{8,11},{9,8},{10,9... | collective-permute-start | bytes 417800 | tf_op jit(solution)/shard_map/ppermute | solution.py:40
  19.3 16.4 %collective-permute-start.11 = (bf16[2112,256]{1,0:T(8,128)(2,1)S(1)}, bf16[2112,256]{1,0:T(8,128)(2,1)S(1)}, u32[]{:S(2)}, u32[]{:S(2)}) collective-permute-start(bf16[2112,256]{1,0:T(8,128)(2,1)S(1)} %constant_dynamic-update-slice_fusion), channel_id=1, source_target_pairs={{0,16},{1,17},{2,18},{3,19},{4,20},{5,21},{6,22},{7,23},{8,12},{9,... | collective-permute-start | bytes 3244040 | tf_op jit(solution)/shard_map/ppermute | solution.py:40
  21.0 15.2 %collective-permute-start.10 = (bf16[2112,256]{1,0:T(8,128)(2,1)S(1)}, bf16[2112,256]{1,0:T(8,128)(2,1)S(1)}, u32[]{:S(2)}, u32[]{:S(2)}) collective-permute-start(bf16[2112,256]{1,0:T(8,128)(2,1)S(1)} %constant_dynamic-update-slice_fusion), channel_id=1, source_target_pairs={{0,48},{1,49},{2,50},{3,51},{4,52},{5,53},{6,54},{7,55},{8,76},{9,... | collective-permute-start | bytes 3244040 | tf_op jit(solution)/shard_map/ppermute | solution.py:40
  22.6 1.5 %collective-permute-start.6 = (bf16[528,256]{1,0:T(8,128)(2,1)S(1)}, bf16[528,256]{1,0:T(8,128)(2,1)S(1)}, u32[]{:S(2)}, u32[]{:S(2)}) collective-permute-start(bf16[528,256]{1,0:T(8,128)(2,1)S(1)} %get-tuple-element.26.refs_3_.refs_1_), channel_id=1, source_target_pairs={{0,8},{1,9},{2,10},{3,11},{4,12},{5,13},{6,14},{7,15},{8,0},{9,1},... | collective-permute-start | bytes 811016 | tf_op jit(solution)/shard_map/ppermute | solution.py:40
  22.6 1.9 %collective-permute-start.7 = (bf16[528,256]{1,0:T(8,128)(2,1)S(1)}, bf16[528,256]{1,0:T(8,128)(2,1)S(1)}, u32[]{:S(2)}, u32[]{:S(2)}) collective-permute-start(bf16[528,256]{1,0:T(8,128)(2,1)S(1)} %collective-permute-done.3.refs_4_.refs_2_), channel_id=1, source_target_pairs={{0,8},{1,9},{2,10},{3,11},{4,12},{5,13},{6,14},{7,15},{8,0},{9,1},... | collective-permute-start | bytes 811016 | tf_op jit(solution)/shard_map/ppermute | solution.py:40
  23.2 1.8 %collective-permute-start.8 = (bf16[528,256]{1,0:T(8,128)(2,1)S(1)}, bf16[528,256]{1,0:T(8,128)(2,1)S(1)}, u32[]{:S(2)}, u32[]{:S(2)}) collective-permute-start(bf16[528,256]{1,0:T(8,128)(2,1)S(1)} %collective-permute-done.4.refs_5_.refs_3_), channel_id=1, source_target_pairs={{0,8},{1,9},{2,10},{3,11},{4,12},{5,13},{6,14},{7,15},{8,0},{9,1},... | collective-permute-start | bytes 811016 | tf_op jit(solution)/shard_map/ppermute | solution.py:40
  24.2 1.5 %collective-permute-start.9 = (bf16[528,256]{1,0:T(8,128)(2,1)S(1)}, bf16[528,256]{1,0:T(8,128)(2,1)S(1)}, u32[]{:S(2)}, u32[]{:S(2)}) collective-permute-start(bf16[528,256]{1,0:T(8,128)(2,1)S(1)} %collective-permute-done.5.refs_6_.refs_4_), channel_id=1, source_target_pairs={{0,8},{1,9},{2,10},{3,11},{4,12},{5,13},{6,14},{7,15},{8,0},{9,1},... | collective-permute-start | bytes 811016 | tf_op jit(solution)/shard_map/ppermute | solution.py:40
  36.1 12.1 %collective-permute-start.16 = (bf16[2112,256]{1,0:T(8,128)(2,1)S(1)}, bf16[2112,256]{1,0:T(8,128)(2,1)S(1)}, u32[]{:S(2)}, u32[]{:S(2)}) collective-permute-start(bf16[2112,256]{1,0:T(8,128)(2,1)S(1)} %collective-permute-done.10.refs_3_.refs_9_), channel_id=1, source_target_pairs={{0,8},{1,9},{2,10},{3,11},{4,12},{5,13},{6,14},{7,15},{8,0},{9,1},... | collective-permute-start | bytes 3244040 | tf_op jit(solution)/shard_map/ppermute | solution.py:40
  36.1 12.1 %collective-permute-start.17 = (bf16[2112,256]{1,0:T(8,128)(2,1)S(1)}, bf16[2112,256]{1,0:T(8,128)(2,1)S(1)}, u32[]{:S(2)}, u32[]{:S(2)}) collective-permute-start(bf16[2112,256]{1,0:T(8,128)(2,1)S(1)} %collective-permute-done.11.refs_4_.refs_10_), channel_id=1, source_target_pairs={{0,8},{1,9},{2,10},{3,11},{4,12},{5,13},{6,14},{7,15},{8,0},{9,1},... | collective-permute-start | bytes 3244040 | tf_op jit(solution)/shard_map/ppermute | solution.py:40
  36.7 10.6 %collective-permute-start.13 = (bf16[1056,256]{1,0:T(8,128)(2,1)S(1)}, bf16[1056,256]{1,0:T(8,128)(2,1)S(1)}, u32[]{:S(2)}, u32[]{:S(2)}) collective-permute-start(bf16[1056,256]{1,0:T(8,128)(2,1)S(1)} %slice.7), channel_id=1, source_target_pairs={{0,16},{1,17},{2,18},{3,19},{4,20},{5,21},{6,22},{7,23},{8,12},{9,... | collective-permute-start | bytes 1622024 | tf_op jit(solution)/shard_map/ppermute | solution.py:40
  38.4 9.4 %collective-permute-start.12 = (bf16[1056,256]{1,0:T(8,128)(2,1)S(1)}, bf16[1056,256]{1,0:T(8,128)(2,1)S(1)}, u32[]{:S(2)}, u32[]{:S(2)}) collective-permute-start(bf16[1056,256]{1,0:T(8,128)(2,1)S(1)} %slice.6), channel_id=1, source_target_pairs={{0,48},{1,49},{2,50},{3,51},{4,52},{5,53},{6,54},{7,55},{8,76},{9,... | collective-permute-start | bytes 1622024 | tf_op jit(solution)/shard_map/ppermute | solution.py:40
  47.7 7.0 %collective-permute-start.14 = (bf16[1056,256]{1,0:T(8,128)(2,1)S(1)}, bf16[1056,256]{1,0:T(8,128)(2,1)S(1)}, u32[]{:S(2)}, u32[]{:S(2)}) collective-permute-start(bf16[1056,256]{1,0:T(8,128)(2,1)S(1)} %collective-permute-done.12.refs_3_.refs_13_), channel_id=1, source_target_pairs={{0,8},{1,9},{2,10},{3,11},{4,12},{5,13},{6,14},{7,15},{8,0},{9,1},... | collective-permute-start | bytes 1622024 | tf_op jit(solution)/shard_map/ppermute | solution.py:40
  47.7 7.0 %collective-permute-start.15 = (bf16[1056,256]{1,0:T(8,128)(2,1)S(1)}, bf16[1056,256]{1,0:T(8,128)(2,1)S(1)}, u32[]{:S(2)}, u32[]{:S(2)}) collective-permute-start(bf16[1056,256]{1,0:T(8,128)(2,1)S(1)} %collective-permute-done.13.refs_4_.refs_14_), channel_id=1, source_target_pairs={{0,8},{1,9},{2,10},{3,11},{4,12},{5,13},{6,14},{7,15},{8,0},{9,1},... | collective-permute-start | bytes 1622024 | tf_op jit(solution)/shard_map/ppermute | solution.py:40
  61.3 12.9 %collective-permute-start.18 = (f32[512,128]{1,0:T(8,128)S(1)}, f32[512,128]{1,0:T(8,128)S(1)}, u32[]{:S(2)}, u32[]{:S(2)}) collective-permute-start(f32[512,128]{1,0:T(8,128)S(1)} %get-tuple-element.43), channel_id=1, source_target_pairs={{0,1},{1,2},{2,3},{3,0},{4,5},{5,6},{6,7},{7,4},{8,9},{9,10},{10,1... | collective-permute-start | bytes 786440 | tf_op jit(solution)/shard_map/ppermute | solution.py:40
  61.4 14.7 %collective-permute-start.19 = (f32[512,128]{1,0:T(8,128)S(1)}, f32[512,128]{1,0:T(8,128)S(1)}, u32[]{:S(2)}, u32[]{:S(2)}) collective-permute-start(f32[512,128]{1,0:T(8,128)S(1)} %get-tuple-element.44), channel_id=1, source_target_pairs={{0,3},{1,0},{2,1},{3,2},{4,7},{5,4},{6,5},{7,6},{8,11},{9,8},{10,9... | collective-permute-start | bytes 786440 | tf_op jit(solution)/shard_map/ppermute | solution.py:40
  64.7 13.2 %collective-permute-start.20 = (f32[512,128]{1,0:T(8,128)S(1)}, f32[512,128]{1,0:T(8,128)S(1)}, u32[]{:S(2)}, u32[]{:S(2)}) collective-permute-start(f32[512,128]{1,0:T(8,128)S(1)} %get-tuple-element.45), channel_id=1, source_target_pairs={{0,2},{1,3},{2,0},{3,1},{4,6},{5,7},{6,4},{7,5},{8,10},{9,11},{10,... | collective-permute-start | bytes 786440 | tf_op jit(solution)/shard_map/ppermute | solution.py:40
  78.4 1.3 %collective-permute-start.21 = (f32[128,128]{1,0:T(8,128)S(1)}, f32[128,128]{1,0:T(8,128)S(1)}, u32[]{:S(2)}, u32[]{:S(2)}) collective-permute-start(f32[128,128]{1,0:T(8,128)S(1)} %get-tuple-element.47), channel_id=1, source_target_pairs={{0,8},{1,9},{2,10},{3,11},{4,12},{5,13},{6,14},{7,15},{8,0},{9,1},... | collective-permute-start | bytes 196616 | tf_op jit(solution)/shard_map/ppermute | solution.py:40
  79.7 5.5 %collective-permute-start.24 = (f32[128,128]{1,0:T(8,128)S(1)}, f32[128,128]{1,0:T(8,128)S(1)}, u32[]{:S(2)}, u32[]{:S(2)}) collective-permute-start(f32[128,128]{1,0:T(8,128)S(1)} %add.21), channel_id=1, source_target_pairs={{0,1},{1,2},{2,3},{3,0},{4,5},{5,6},{6,7},{7,4},{8,9},{9,10},{10,1... | collective-permute-start | bytes 196616 | tf_op jit(solution)/shard_map/ppermute | solution.py:40
  80.9 5.1 %collective-permute-start.23 = (f32[128,128]{1,0:T(8,128)S(1)}, f32[128,128]{1,0:T(8,128)S(1)}, u32[]{:S(2)}, u32[]{:S(2)}) collective-permute-start(f32[128,128]{1,0:T(8,128)S(1)} %add.21), channel_id=1, source_target_pairs={{0,3},{1,0},{2,1},{3,2},{4,7},{5,4},{6,5},{7,6},{8,11},{9,8},{10,9... | collective-permute-start | bytes 196616 | tf_op jit(solution)/shard_map/ppermute | solution.py:40
  83.0 5.8 %collective-permute-start.22 = (f32[128,128]{1,0:T(8,128)S(1)}, f32[128,128]{1,0:T(8,128)S(1)}, u32[]{:S(2)}, u32[]{:S(2)}) collective-permute-start(f32[128,128]{1,0:T(8,128)S(1)} %add.21), channel_id=1, source_target_pairs={{0,2},{1,3},{2,0},{3,1},{4,6},{5,7},{6,4},{7,5},{8,10},{9,11},{10,... | collective-permute-start | bytes 196616 | tf_op jit(solution)/shard_map/ppermute | solution.py:40
  88.8 6.2 %collective-permute-start.27 = (f32[128,128]{1,0:T(8,128)S(1)}, f32[128,128]{1,0:T(8,128)S(1)}, u32[]{:S(2)}, u32[]{:S(2)}) collective-permute-start(f32[128,128]{1,0:T(8,128)S(1)} %add_add_fusion.1), channel_id=1, source_target_pairs={{0,16},{1,17},{2,18},{3,19},{4,20},{5,21},{6,22},{7,23},{8,24},{9,... | collective-permute-start | bytes 196616 | tf_op jit(solution)/shard_map/ppermute | solution.py:40
  90.2 4.9 %collective-permute-start.26 = (f32[128,128]{1,0:T(8,128)S(1)}, f32[128,128]{1,0:T(8,128)S(1)}, u32[]{:S(2)}, u32[]{:S(2)}) collective-permute-start(f32[128,128]{1,0:T(8,128)S(1)} %add_add_fusion.1), channel_id=1, source_target_pairs={{0,48},{1,49},{2,50},{3,51},{4,52},{5,53},{6,54},{7,55},{8,56},{9,... | collective-permute-start | bytes 196616 | tf_op jit(solution)/shard_map/ppermute | solution.py:40
  92.1 5.8 %collective-permute-start.25 = (f32[128,128]{1,0:T(8,128)S(1)}, f32[128,128]{1,0:T(8,128)S(1)}, u32[]{:S(2)}, u32[]{:S(2)}) collective-permute-start(f32[128,128]{1,0:T(8,128)S(1)} %add_add_fusion.1), channel_id=1, source_target_pairs={{0,32},{1,33},{2,34},{3,35},{4,36},{5,37},{6,38},{7,39},{8,40},{9,... | collective-permute-start | bytes 196616 | tf_op jit(solution)/shard_map/ppermute | solution.py:40
  97.9 5.5 %collective-permute-start.30 = (f32[128,128]{1,0:T(8,128)S(1)}, f32[128,128]{1,0:T(8,128)S(1)}, u32[]{:S(2)}, u32[]{:S(2)}) collective-permute-start(f32[128,128]{1,0:T(8,128)S(1)} %add_add_fusion.g_ref), channel_id=1, source_target_pairs={{0,4},{1,5},{2,6},{3,7},{4,64},{5,65},{6,66},{7,67},{8,12},{9,13},... | collective-permute-start | bytes 196616 | tf_op jit(solution)/shard_map/ppermute | solution.py:40
  98.1 5.4 %collective-permute-start.29 = (f32[128,128]{1,0:T(8,128)S(1)}, f32[128,128]{1,0:T(8,128)S(1)}, u32[]{:S(2)}, u32[]{:S(2)}) collective-permute-start(f32[128,128]{1,0:T(8,128)S(1)} %add_add_fusion.g_ref), channel_id=1, source_target_pairs={{0,68},{1,69},{2,70},{3,71},{4,0},{5,1},{6,2},{7,3},{8,76},{9,77},... | collective-permute-start | bytes 196616 | tf_op jit(solution)/shard_map/ppermute | solution.py:40
  101.2 5.8 %collective-permute-start.28 = (f32[128,128]{1,0:T(8,128)S(1)}, f32[128,128]{1,0:T(8,128)S(1)}, u32[]{:S(2)}, u32[]{:S(2)}) collective-permute-start(f32[128,128]{1,0:T(8,128)S(1)} %add_add_fusion.g_ref), channel_id=1, source_target_pairs={{0,64},{1,65},{2,66},{3,67},{4,68},{5,69},{6,70},{7,71},{8,72},{9,... | collective-permute-start | bytes 196616 | tf_op jit(solution)/shard_map/ppermute | solution.py:40

commit v3 on v2

--- a/solution.py
+++ b/solution.py
@@ -64,8 +64,7 @@
     return fetch(value, lambda x, y, z, k: (x + step * k, y + step * (1 - k), z, k))
 
 
-def pack_body(pts_ref, prb_ref, block_ref, rows_ref):
-    pts = pts_ref[...].astype(jnp.float32)
+def split_norms(pts, at_col, one_col):
     square = pts * pts
     major = square.astype(jnp.bfloat16)
     minor = (square - major.astype(jnp.float32)).astype(jnp.bfloat16)
@@ -80,37 +79,49 @@
     mid = rest.astype(jnp.bfloat16).astype(jnp.float32)
     low = rest - mid
     sub = lax.broadcasted_iota(jnp.int32, (8, BLK), 0)
-
-    def place(at, one):
-        v = jnp.where((sub >= one) & (sub < one + 3), 1.0, 0.0)
-        v = jnp.where(sub == at, high, v)
-        v = jnp.where(sub == at + 1, mid, v)
-        return jnp.where(sub == at + 2, low, v)
-
-    col = place(0, 3)
-    row = place(3, 0)
+    v = jnp.where((sub >= one_col) & (sub < one_col + 3), 1.0, 0.0)
+    v = jnp.where(sub == at_col, high, v)
+    v = jnp.where(sub == at_col + 1, mid, v)
+    return jnp.where(sub == at_col + 2, low, v)
+
+
+def row_block_body(pts_ref, rows_ref):
+    pts = pts_ref[...].astype(jnp.float32)
+    row = split_norms(pts, 3, 0)
+    rows_ref[BLK:, :] = jnp.concatenate(
+        [row[:, c:c + DIM] for c in range(0, BLK, DIM)], axis=0).astype(jnp.bfloat16)
+    rows_ref[:BLK, :] = (pts * -2.0).astype(jnp.bfloat16)
+
+
+def col_block_body(pts_ref, prb_ref, block_ref):
+    col = split_norms(pts_ref[...].astype(jnp.float32), 0, 3)
     half = BLK // 2
     block_ref[BLK:, :] = jnp.concatenate([col[:, :half], col[:, half:]], axis=0).astype(jnp.bfloat16)
-    rows_ref[BLK:, :] = jnp.concatenate(
-        [row[:, c:c + DIM] for c in range(0, BLK, DIM)], axis=0).astype(jnp.bfloat16)
     block_ref[:BLK, :DIM] = pts_ref[...]
-    rows_ref[:BLK, :] = (pts * -2.0).astype(jnp.bfloat16)
     for c in range(0, BLK, DIM):
         block_ref[c:c + DIM, DIM:] = prb_ref[c:c + DIM, :].astype(jnp.float32).T.astype(jnp.bfloat16)
 
 
-def pack(points, probes):
-    return pl.pallas_call(
-        pack_body,
-        out_shape=[
-            pltpu.VMEM((COLS, 2 * DIM), jnp.bfloat16),
-            pltpu.VMEM((ROWS, DIM), jnp.bfloat16),
-        ],
+def row_block(points):
+    return pl.pallas_call(
+        row_block_body,
+        out_shape=pltpu.VMEM((ROWS, DIM), jnp.bfloat16),
+        in_specs=[VMEM],
+        out_specs=VMEM,
+        compiler_params=PARAMS,
+        name="row_block",
+    )(*local([points]))
+
+
+def col_block(points, probes):
+    return pl.pallas_call(
+        col_block_body,
+        out_shape=pltpu.VMEM((COLS, 2 * DIM), jnp.bfloat16),
         in_specs=[VMEM, VMEM],
-        out_specs=[VMEM, VMEM],
-        compiler_params=PARAMS,
-        name="pack",
-    )(points, probes)
+        out_specs=VMEM,
+        compiler_params=PARAMS,
+        name="col_block",
+    )(*local([points, probes]))
 
 
 def upright(v):
@@ -122,7 +133,7 @@
     first = acc is None
     slots = [(r, lo) for r, v in enumerate(islots) for lo in range(0, v.shape[0], ROWS)]
     irows = len(slots) * BLK
-    nout = len(slots) if last else 1
+    nout = 1
     where = [(r, lo) for r, v in enumerate(jblocks) for lo in range(0, v.shape[0], COLS)]
     count = len(where)
     ntile = irows // TI
@@ -186,27 +197,24 @@
                 if not final:
                     now = ahead
             if last:
-                out_ref[at * TI:(at + 1) * TI, :] = total.T
+                out_ref[pl.ds(pl.multiple_of(t * TI, TI), TI), :] = total.T
             else:
                 out_ref[t] = total
 
-        if last:
-            for t in range(ntile):
-                step(t, outs[t // 2], t % 2)
-        else:
-            def turn(i, carry):
-                step(2 * i, outs[0], 0)
-                step(2 * i + 1, outs[0], 0)
-                return carry
-            lax.fori_loop(0, ntile // 2, turn, 0)
-
-    shape = (BLK, DIM) if last else (ntile, DIM, TI)
+        def turn(i, carry):
+            step(2 * i, outs[0], 0)
+            step(2 * i + 1, outs[0], 1)
+            return carry
+
+        lax.fori_loop(0, ntile // 2, turn, 0)
+
+    shape = (irows, DIM) if last else (ntile, DIM, TI)
     ops = list(islots) + list(jblocks) + ([] if first else [acc])
     return pl.pallas_call(
         body,
-        out_shape=[pltpu.VMEM(shape, jnp.float32)] * nout if last else pltpu.VMEM(shape, jnp.float32),
+        out_shape=pltpu.VMEM(shape, jnp.float32),
         in_specs=[VMEM] * len(ops),
-        out_specs=[VMEM] * nout if last else VMEM,
+        out_specs=VMEM,
         scratch_shapes=[
             pltpu.VMEM((irows, 2 * DIM), jnp.bfloat16),
             pltpu.VMEM((count * BLK, DIM), jnp.bfloat16),
@@ -304,29 +312,37 @@
 
 def shards(points, probes):
     order = (1, -1, 2)
-    block, mine = pack(points, probes)
+    mine = row_block(points)
+    block = col_block(points, probes)
     near = [from_z(mine, d) for d in order]
     legs = [first_leg(block, d) for d in order]
     held = lax.optimization_barrier(near + legs)
     near, legs = held[:3], held[3:]
-    early = [block] + legs
-    early += [swap(v) for v in early]
-    leg = jnp.concatenate([block] + legs)
-    rest = [second_leg(leg, d) for d in (1, -1)]
-
-    acc = sketch_part(near, early, None, False, True, "early")
-    acc, *rest = lax.optimization_barrier([acc] + rest)
-    mid = 2 * COLS
-    across = [second_leg(rest[0][:mid], 1), second_leg(rest[1][mid:], -1)]
-    other = [swap(v) for v in rest]
-    acc = sketch_part(near, rest, acc, False, True, "away_own")
-    acc, *across = lax.optimization_barrier([acc] + across)
+    leg_a = jnp.concatenate([block, legs[0]])
+    leg_b = jnp.concatenate([legs[1], legs[2]])
+    partner = [swap(jnp.concatenate([leg_a, leg_b]))]
+    rest_a = [second_leg(leg_a, d) for d in (1, -1)]
+    rest_b = [second_leg(leg_b, d) for d in (1, -1)]
+
+    early = [leg_a, leg_b]
+    acc = sketch_part(near, early + partner, None, False, True, "early")
+
+    acc, *rest_a = lax.optimization_barrier([acc] + rest_a)
+    across_a = second_leg(rest_a[0], 1)
+    other_a = [swap(v) for v in rest_a]
+    acc = sketch_part(near, rest_a, acc, False, True, "a_own")
+    acc, *rest_b = lax.optimization_barrier([acc] + rest_b)
+    across_b = second_leg(rest_b[1], -1)
+    other_b = [swap(v) for v in rest_b]
+    acc = sketch_part(near, other_a + rest_b, acc, False, True, "a_other_b_own")
+    acc, *across = lax.optimization_barrier([acc, across_a, across_b])
     far = [swap(v) for v in across]
-    acc = sketch_part(near, other, acc, False, True, "away_other")
+    acc = sketch_part(near, other_b, acc, False, True, "b_other")
     away = sketch_part(near, across + far, acc, True, True, "away_last")
-    held = lax.optimization_barrier(list(away) + [mine])
+    blocks = early + partner + rest_a + other_a + rest_b + other_b + across + far
+    held = lax.optimization_barrier([away[i * BLK:(i + 1) * BLK] for i in range(3)] + [mine])
     back = [from_z(v, -d) for v, d in zip(held[:3], order)]
-    home, = sketch_part(held[3:], early + rest + other + across + far, None, True, False, "home")
+    home = sketch_part(held[3:], blocks, None, True, False, "home")
     rows, gram = finish_rows(home, *back)
     gram = gram + swap(gram)
     gram = ring_sum(ring_parts(gram, from_z))

time: 114 us -> 112 us (0.982)
  waiting for transfers between devices: 29.4 us -> 23.3 us
  starting transfers between devices: 38.5 us -> 41.4 us
  Pallas kernels: 42.2 us -> 43.7 us
    ppermute x31 -> x32, waiting for transfers between devices: 29.4 us -> 23.3 us  [fetch(): return lax.ppermute(value, AXES, sorted(pairs))]
    ppermute x31 -> x32, starting transfers between devices: 38.5 us -> 41.4 us  [fetch(): return lax.ppermute(value, AXES, sorted(pairs))]
    pallas_call x6 -> x8, Pallas kernels: 35.1 us -> 36.6 us  [the longest x6 36.2 us: sketch_part(): pl.pallas_call(body, out_shape=pltpu.VMEM(shape, jnp.float32), in_specs=[...]
    unnamed x8 -> x6, local copies, waits for them, and re-layouts: 2.56 us -> 2.52 us
  transfers between devices with their start and end apart: 31 -> 32, of which waited for: 19 -> 13; matrix products, arithmetic and copies ran while one was open for 1% -> 1% of each run, Pallas kernels for 25% -> 26%
where the time goes in v3:
time: 112 us
  Pallas kernels  43.7 us (39%)
  starting transfers between devices  41.4 us (37%)
  waiting for transfers between devices  23.3 us (21%)
  local copies, waits for them, and re-layouts  2.6 us (2%)
    ppermute x32, starting transfers between devices, fetch(): return lax.ppermute(value, AXES, sorted(pairs))  41.4 us
    pallas_call x6, Pallas kernels, sketch_part(): pl.pallas_call(body, out_shape=pltpu.VMEM(shape, jnp.float32), in_specs=[...  36.2 us
    ppermute x32, waiting for transfers between devices, fetch(): return lax.ppermute(value, AXES, sorted(pairs))  23.3 us
    pallas_call x1, Pallas kernels, make_basis(): pl.pallas_call(basis_body, out_shape=jax.ShapeDtypeStruct((BLK, DIM), jnp...  6.66 us
    unnamed x6, local copies, waits for them, and re-layouts  2.52 us
  transfers between devices with their start and end apart: 32, of which 13 were waited for; matrix products, arithmetic and copies ran while one was open for 1% of the time, Pallas kernels for 26%

profile of v3, /device:TPU:0, one launch (start us, length us, event | category | flops | bytes accessed | tf_op | source)
XLA Modules:
  0.0 112.1 jit_solution(2336295974400902422)
XLA Ops:
  0.6 0.9 copy-done
  1.5 0.2 row_block.1.refs_0_
  1.8 4.0 %collective-permute-start.2 = (bf16[544,128]{1,0:T(8,128)(2,1)S(1)}, bf16[544,128]{1,0:T(8,128)(2,1)S(1)}, u32[]{:S(2)}, u32[]{:S(2)}) collective-permute-start(bf16[544,128]{1,0:T(8,128)(2,1)S(1)} %row_block.1.refs_0_), channel_id=1, source_target_pairs={{0,2},{1,3},{2,0},{3,1},{4,6},{5,7},{6,4},{7,5},{8,10},{9,11},{10,... | collective-permute-start | bytes 417800 | tf_op jit(solution)/shard_map/ppermute | solution.py:40
  5.8 0.9 copy-done.1
  6.7 0.2 col_block.1
  6.9 3.1 %collective-permute-start.5 = (bf16[528,256]{1,0:T(8,128)(2,1)S(1)}, bf16[528,256]{1,0:T(8,128)(2,1)S(1)}, u32[]{:S(2)}, u32[]{:S(2)}) collective-permute-start(bf16[528,256]{1,0:T(8,128)(2,1)S(1)} %col_block.1), channel_id=1, source_target_pairs={{0,64},{1,65},{2,66},{3,67},{4,68},{5,69},{6,70},{7,71},{8,40},{9,... | collective-permute-start | bytes 811016 | tf_op jit(solution)/shard_map/ppermute | solution.py:40
  10.0 0.6 collective-permute-start.4
  10.6 2.6 %collective-permute-start.3 = (bf16[528,256]{1,0:T(8,128)(2,1)S(1)}, bf16[528,256]{1,0:T(8,128)(2,1)S(1)}, u32[]{:S(2)}, u32[]{:S(2)}) collective-permute-start(bf16[528,256]{1,0:T(8,128)(2,1)S(1)} %col_block.1), channel_id=1, source_target_pairs={{0,68},{1,69},{2,70},{3,71},{4,0},{5,1},{6,2},{7,3},{8,56},{9,57},... | collective-permute-start | bytes 811016 | tf_op jit(solution)/shard_map/ppermute | solution.py:40
  13.2 1.0 collective-permute-start.1
  14.3 2.2 %collective-permute-start = (bf16[544,128]{1,0:T(8,128)(2,1)S(1)}, bf16[544,128]{1,0:T(8,128)(2,1)S(1)}, u32[]{:S(2)}, u32[]{:S(2)}) collective-permute-start(bf16[544,128]{1,0:T(8,128)(2,1)S(1)} %row_block.1.refs_0_), channel_id=1, source_target_pairs={{0,3},{1,0},{2,1},{3,2},{4,7},{5,4},{6,5},{7,6},{8,11},{9,8},{10,9... | collective-permute-start | bytes 417800 | tf_op jit(solution)/shard_map/ppermute | solution.py:40
  16.5 3.0 %collective-permute-done.1.refs_1_ = bf16[544,128]{1,0:T(8,128)(2,1)S(1)} collective-permute-done((bf16[544,128]{1,0:T(8,128)(2,1)S(1)}, bf16[544,128]{1,0:T(8,128)(2,1)S(1)}, u32[]{:S(2)}, u32[]{:S(2)}) %collective-permute-start.1) | collective-permute-done | bytes 139296 | tf_op jit(solution)/shard_map/ppermute | solution.py:40
  19.8 1.6 %collective-permute-start.8 = (bf16[1056,256]{1,0:T(8,128)(2,1)S(1)}, bf16[1056,256]{1,0:T(8,128)(2,1)S(1)}, u32[]{:S(2)}, u32[]{:S(2)}) collective-permute-start(bf16[1056,256]{1,0:T(8,128)(2,1)S(1)} %pad_maximum_fusion.1.refs_3_.refs_1_), channel_id=1, source_target_pairs={{0,16},{1,17},{2,18},{3,19},{4,20},{5,21},{6,22},{7,23},{8,12},{9,... | collective-permute-start | bytes 1622024 | tf_op jit(solution)/shard_map/ppermute | solution.py:40
  21.4 1.7 %collective-permute-start.7 = (bf16[1056,256]{1,0:T(8,128)(2,1)S(1)}, bf16[1056,256]{1,0:T(8,128)(2,1)S(1)}, u32[]{:S(2)}, u32[]{:S(2)}) collective-permute-start(bf16[1056,256]{1,0:T(8,128)(2,1)S(1)} %pad_maximum_fusion.1.refs_3_.refs_1_), channel_id=1, source_target_pairs={{0,48},{1,49},{2,50},{3,51},{4,52},{5,53},{6,54},{7,55},{8,76},{9,... | collective-permute-start | bytes 1622024 | tf_op jit(solution)/shard_map/ppermute | solution.py:40
  23.1 0.4 collective-permute-start.12
  23.5 2.9 %collective-permute-start.11 = (bf16[1056,256]{1,0:T(8,128)(2,1)S(1)}, bf16[1056,256]{1,0:T(8,128)(2,1)S(1)}, u32[]{:S(2)}, u32[]{:S(2)}) collective-permute-start(bf16[1056,256]{1,0:T(8,128)(2,1)S(1)} %constant_dynamic-update-slice_fusion.refs_4_.refs_2_), channel_id=1, source_target_pairs={{0,48},{1,49},{2,50},{3,51},{4,52},{5,53},{6,54},{7,55},{8,76},{9,... | collective-permute-start | bytes 1622024 | tf_op jit(solution)/shard_map/ppermute | solution.py:40
  26.4 6.5 %early.1.refs_5_ = f32[6,128,256]{2,1,0:T(8,128)S(1)} custom-call(bf16[544,128]{1,0:T(8,128)(2,1)S(1)} %collective-permute-done.refs_0_, bf16[544,128]{1,0:T(8,128)(2,1)S(1)} %collective-permute-done.1.refs_1_, bf16[544,128]{1,0:T(8,128)(2,1)S(1)} %collective-permute-done.2.refs_2_, bf16[1056,256]{1,0:T(8,128)(2,1)S(1)} %pad_maximum_fusion.1.refs_3_.refs_1_, ...), custom_call_target="tpu_custom_call" | custom-call | flops 4831838208 | bytes 5767168 | tf_op jit(solution)/shard_map/early/pallas_call | solution.py:213
  33.1 0.5 collective-permute-start.9
  33.6 3.8 %a_own.1.refs_7_ = f32[6,128,256]{2,1,0:T(8,128)S(1)} custom-call(bf16[544,128]{1,0:T(8,128)(2,1)S(1)} %collective-permute-done.refs_0_, bf16[544,128]{1,0:T(8,128)(2,1)S(1)} %collective-permute-done.1.refs_1_, bf16[544,128]{1,0:T(8,128)(2,1)S(1)} %collective-permute-done.2.refs_2_, bf16[1056,256]{1,0:T(8,128)(2,1)S(1)} %collective-permute-done.7.refs_3_.refs_4_, ...), custom_call_target="tpu_custom_call" | custom-call | flops 2415919104 | bytes 3670016 | tf_op jit(solution)/shard_map/a_own/pallas_call | solution.py:213
  37.4 0.7 collective-permute-start.14
  38.1 2.6 %collective-permute-start.13 = (bf16[1056,256]{1,0:T(8,128)(2,1)S(1)}, bf16[1056,256]{1,0:T(8,128)(2,1)S(1)}, u32[]{:S(2)}, u32[]{:S(2)}) collective-permute-start(bf16[1056,256]{1,0:T(8,128)(2,1)S(1)} %collective-permute-done.7.refs_3_.refs_4_), channel_id=1, source_target_pairs={{0,48},{1,49},{2,50},{3,51},{4,52},{5,53},{6,54},{7,55},{8,76},{9,... | collective-permute-start | bytes 1622024 | tf_op jit(solution)/shard_map/ppermute | solution.py:40
  40.7 0.5 collective-permute-start.17
  41.2 6.8 %a_other_b_own.1.refs_5_ = f32[6,128,256]{2,1,0:T(8,128)S(1)} custom-call(bf16[544,128]{1,0:T(8,128)(2,1)S(1)} %collective-permute-done.refs_0_, bf16[544,128]{1,0:T(8,128)(2,1)S(1)} %collective-permute-done.1.refs_1_, bf16[544,128]{1,0:T(8,128)(2,1)S(1)} %collective-permute-done.2.refs_2_, bf16[1056,256]{1,0:T(8,128)(2,1)S(1)} %collective-permute-done.9.refs_3_.refs_6_, ...), custom_call_target="tpu_custom_call" | custom-call | flops 4831838208 | bytes 5767168 | tf_op jit(solution)/shard_map/a_other_b_own/pallas_call | solution.py:213
  48.1 0.5 collective-permute-start.16
  48.6 3.9 %b_other.1.refs_7_ = f32[6,128,256]{2,1,0:T(8,128)S(1)} custom-call(bf16[544,128]{1,0:T(8,128)(2,1)S(1)} %collective-permute-done.refs_0_, bf16[544,128]{1,0:T(8,128)(2,1)S(1)} %collective-permute-done.1.refs_1_, bf16[544,128]{1,0:T(8,128)(2,1)S(1)} %collective-permute-done.2.refs_2_, bf16[1056,256]{1,0:T(8,128)(2,1)S(1)} %collective-permute-done.17.refs_3_.refs_10_, ...), custom_call_target="tpu_custom_call" | custom-call | flops 2415919104 | bytes 3670016 | tf_op jit(solution)/shard_map/b_other/pallas_call | solution.py:213
  52.6 7.1 %away_last.1 = f32[1536,128]{1,0:T(8,128)S(1)} custom-call(bf16[544,128]{1,0:T(8,128)(2,1)S(1)} %collective-permute-done.refs_0_, bf16[544,128]{1,0:T(8,128)(2,1)S(1)} %collective-permute-done.1.refs_1_, bf16[544,128]{1,0:T(8,128)(2,1)S(1)} %collective-permute-done.2.refs_2_, bf16[1056,256]{1,0:T(8,128)(2,1)S(1)} %collective-permute-done.13.refs_3_.refs_12_, ...), custom_call_target="tpu_custom_call" | custom-call | flops 4831838208 | bytes 5767168 | tf_op jit(solution)/shard_map/away_last/pallas_call | solution.py:213
  59.8 3.3 %collective-permute-start.20 = (f32[512,128]{1,0:T(8,128)S(1)}, f32[512,128]{1,0:T(8,128)S(1)}, u32[]{:S(2)}, u32[]{:S(2)}) collective-permute-start(f32[512,128]{1,0:T(8,128)S(1)} %get-tuple-element.40), channel_id=1, source_target_pairs={{0,3},{1,0},{2,1},{3,2},{4,7},{5,4},{6,5},{7,6},{8,11},{9,8},{10,9... | collective-permute-start | bytes 786440 | tf_op jit(solution)/shard_map/ppermute | solution.py:40
  63.1 1.4 %collective-permute-start.21 = (f32[512,128]{1,0:T(8,128)S(1)}, f32[512,128]{1,0:T(8,128)S(1)}, u32[]{:S(2)}, u32[]{:S(2)}) collective-permute-start(f32[512,128]{1,0:T(8,128)S(1)} %get-tuple-element.41), channel_id=1, source_target_pairs={{0,2},{1,3},{2,0},{3,1},{4,6},{5,7},{6,4},{7,5},{8,10},{9,11},{10,... | collective-permute-start | bytes 786440 | tf_op jit(solution)/shard_map/ppermute | solution.py:40
  64.5 8.1 %home.1.home_ref = f32[512,128]{1,0:T(8,128)S(1)} custom-call(bf16[544,128]{1,0:T(8,128)(2,1)S(1)} %row_block.1.refs_0_, bf16[1056,256]{1,0:T(8,128)(2,1)S(1)} %pad_maximum_fusion.1.refs_3_.refs_1_, bf16[1056,256]{1,0:T(8,128)(2,1)S(1)} %constant_dynamic-update-slice_fusion.refs_4_.refs_2_, bf16[2112,256]{1,0:T(8,128)(2,1)S(1)} %collective-permute-done.6.refs_5_.refs_3_, ...), custom_call_target="tpu_custom_call" | custom-call | flops 6442450944 | bytes 17301504 | tf_op jit(solution)/shard_map/home/pallas_call | solution.py:213
  72.6 1.9 %collective-permute-done.20.b_ref = f32[512,128]{1,0:T(8,128)S(1)} collective-permute-done((f32[512,128]{1,0:T(8,128)S(1)}, f32[512,128]{1,0:T(8,128)S(1)}, u32[]{:S(2)}, u32[]{:S(2)}) %collective-permute-start.20) | collective-permute-done | bytes 262176 | tf_op jit(solution)/shard_map/ppermute | solution.py:40
  74.5 1.8 %collective-permute-done.21.c_ref = f32[512,128]{1,0:T(8,128)S(1)} collective-permute-done((f32[512,128]{1,0:T(8,128)S(1)}, f32[512,128]{1,0:T(8,128)S(1)}, u32[]{:S(2)}, u32[]{:S(2)}) %collective-permute-start.21) | collective-permute-done | bytes 262176 | tf_op jit(solution)/shard_map/ppermute | solution.py:40
  76.4 0.4 finish_rows.1
  76.9 1.2 %collective-permute-done.22 = f32[128,128]{1,0:T(8,128)S(1)} collective-permute-done((f32[128,128]{1,0:T(8,128)S(1)}, f32[128,128]{1,0:T(8,128)S(1)}, u32[]{:S(2)}, u32[]{:S(2)}) %collective-permute-start.22) | collective-permute-done | bytes 65568 | tf_op jit(solution)/shard_map/ppermute | solution.py:40
  78.1 1.2 %collective-permute-start.25 = (f32[128,128]{1,0:T(8,128)S(1)}, f32[128,128]{1,0:T(8,128)S(1)}, u32[]{:S(2)}, u32[]{:S(2)}) collective-permute-start(f32[128,128]{1,0:T(8,128)S(1)} %add.21), channel_id=1, source_target_pairs={{0,1},{1,2},{2,3},{3,0},{4,5},{5,6},{6,7},{7,4},{8,9},{9,10},{10,1... | collective-permute-start | bytes 196616 | tf_op jit(solution)/shard_map/ppermute | solution.py:40
  79.4 2.1 %collective-permute-start.24 = (f32[128,128]{1,0:T(8,128)S(1)}, f32[128,128]{1,0:T(8,128)S(1)}, u32[]{:S(2)}, u32[]{:S(2)}) collective-permute-start(f32[128,128]{1,0:T(8,128)S(1)} %add.21), channel_id=1, source_target_pairs={{0,3},{1,0},{2,1},{3,2},{4,7},{5,4},{6,5},{7,6},{8,11},{9,8},{10,9... | collective-permute-start | bytes 196616 | tf_op jit(solution)/shard_map/ppermute | solution.py:40
  81.5 2.2 %collective-permute-done.25 = f32[128,128]{1,0:T(8,128)S(1)} collective-permute-done((f32[128,128]{1,0:T(8,128)S(1)}, f32[128,128]{1,0:T(8,128)S(1)}, u32[]{:S(2)}, u32[]{:S(2)}) %collective-permute-start.25) | collective-permute-done | bytes 65568 | tf_op jit(solution)/shard_map/ppermute | solution.py:40
  83.7 0.8 collective-permute-done.24
  84.5 2.8 %collective-permute-done.23 = f32[128,128]{1,0:T(8,128)S(1)} collective-permute-done((f32[128,128]{1,0:T(8,128)S(1)}, f32[128,128]{1,0:T(8,128)S(1)}, u32[]{:S(2)}, u32[]{:S(2)}) %collective-permute-start.23) | collective-permute-done | bytes 65568 | tf_op jit(solution)/shard_map/ppermute | solution.py:40
  87.2 0.8 collective-permute-start.28
  88.1 2.5 %collective-permute-start.27 = (f32[128,128]{1,0:T(8,128)S(1)}, f32[128,128]{1,0:T(8,128)S(1)}, u32[]{:S(2)}, u32[]{:S(2)}) collective-permute-start(f32[128,128]{1,0:T(8,128)S(1)} %add_add_fusion.1), channel_id=1, source_target_pairs={{0,48},{1,49},{2,50},{3,51},{4,52},{5,53},{6,54},{7,55},{8,56},{9,... | collective-permute-start | bytes 196616 | tf_op jit(solution)/shard_map/ppermute | solution.py:40
  90.6 1.3 %collective-permute-start.26 = (f32[128,128]{1,0:T(8,128)S(1)}, f32[128,128]{1,0:T(8,128)S(1)}, u32[]{:S(2)}, u32[]{:S(2)}) collective-permute-start(f32[128,128]{1,0:T(8,128)S(1)} %add_add_fusion.1), channel_id=1, source_target_pairs={{0,32},{1,33},{2,34},{3,35},{4,36},{5,37},{6,38},{7,39},{8,40},{9,... | collective-permute-start | bytes 196616 | tf_op jit(solution)/shard_map/ppermute | solution.py:40
  91.9 0.9 collective-permute-done.28
  92.9 3.4 %collective-permute-done.26 = f32[128,128]{1,0:T(8,128)S(1)} collective-permute-done((f32[128,128]{1,0:T(8,128)S(1)}, f32[128,128]{1,0:T(8,128)S(1)}, u32[]{:S(2)}, u32[]{:S(2)}) %collective-permute-start.26) | collective-permute-done | bytes 65568 | tf_op jit(solution)/shard_map/ppermute | solution.py:40
  96.3 0.7 collective-permute-start.31
  97.0 2.6 %collective-permute-start.30 = (f32[128,128]{1,0:T(8,128)S(1)}, f32[128,128]{1,0:T(8,128)S(1)}, u32[]{:S(2)}, u32[]{:S(2)}) collective-permute-start(f32[128,128]{1,0:T(8,128)S(1)} %add_add_fusion.g_ref), channel_id=1, source_target_pairs={{0,68},{1,69},{2,70},{3,71},{4,0},{5,1},{6,2},{7,3},{8,76},{9,77},... | collective-permute-start | bytes 196616 | tf_op jit(solution)/shard_map/ppermute | solution.py:40
  99.7 0.7 copy.5
  100.4 1.5 %collective-permute-done.31.c_ref = f32[128,128]{1,0:T(8,128)S(1)} collective-permute-done((f32[128,128]{1,0:T(8,128)S(1)}, f32[128,128]{1,0:T(8,128)S(1)}, u32[]{:S(2)}, u32[]{:S(2)}) %collective-permute-start.31) | collective-permute-done | bytes 65568 | tf_op jit(solution)/shard_map/ppermute | solution.py:40
  101.9 3.5 %collective-permute-done.29.a_ref = f32[128,128]{1,0:T(8,128)S(1)} collective-permute-done((f32[128,128]{1,0:T(8,128)S(1)}, f32[128,128]{1,0:T(8,128)S(1)}, u32[]{:S(2)}, u32[]{:S(2)}) %collective-permute-start.29) | collective-permute-done | bytes 65568 | tf_op jit(solution)/shard_map/ppermute | solution.py:40
  105.4 6.7 %make_basis.1 = f32[512,128]{1,0:T(8,128)} custom-call(f32[128,128]{1,0:T(8,128)S(1)} %add_add_fusion.g_ref, f32[128,128]{1,0:T(8,128)S(1)} %collective-permute-done.29.a_ref, f32[128,128]{1,0:T(8,128)S(1)} %collective-permute-done.30.b_ref, f32[128,128]{1,0:T(8,128)S(1)} %collective-permute-done.31.c_ref, f32[512,128]{1,0:T(8,128)S(1)} %get-tuple-element.47.rows_ref), custom_call_target="tpu_custom_call" | custom-call | tf_op jit(solution)/shard_map/make_basis/pallas_call | solution.py:294
  (39 shorter events, 1.0 us)
Async XLA Ops:
  0.6 0.9 copy-start
  1.8 12.5 %collective-permute-start.2 = (bf16[544,128]{1,0:T(8,128)(2,1)S(1)}, bf16[544,128]{1,0:T(8,128)(2,1)S(1)}, u32[]{:S(2)}, u32[]{:S(2)}) collective-permute-start(bf16[544,128]{1,0:T(8,128)(2,1)S(1)} %row_block.1.refs_0_), channel_id=1, source_target_pairs={{0,2},{1,3},{2,0},{3,1},{4,6},{5,7},{6,4},{7,5},{8,10},{9,11},{10,... | collective-permute-start | bytes 417800 | tf_op jit(solution)/shard_map/ppermute | solution.py:40
  5.8 0.9 copy-start.1
  6.9 12.6 %collective-permute-start.5 = (bf16[528,256]{1,0:T(8,128)(2,1)S(1)}, bf16[528,256]{1,0:T(8,128)(2,1)S(1)}, u32[]{:S(2)}, u32[]{:S(2)}) collective-permute-start(bf16[528,256]{1,0:T(8,128)(2,1)S(1)} %col_block.1), channel_id=1, source_target_pairs={{0,64},{1,65},{2,66},{3,67},{4,68},{5,69},{6,70},{7,71},{8,40},{9,... | collective-permute-start | bytes 811016 | tf_op jit(solution)/shard_map/ppermute | solution.py:40
  10.0 9.5 %collective-permute-start.4 = (bf16[528,256]{1,0:T(8,128)(2,1)S(1)}, bf16[528,256]{1,0:T(8,128)(2,1)S(1)}, u32[]{:S(2)}, u32[]{:S(2)}) collective-permute-start(bf16[528,256]{1,0:T(8,128)(2,1)S(1)} %col_block.1), channel_id=1, source_target_pairs={{0,4},{1,5},{2,6},{3,7},{4,64},{5,65},{6,66},{7,67},{8,24},{9,25},... | collective-permute-start | bytes 811016 | tf_op jit(solution)/shard_map/ppermute | solution.py:40
  10.6 8.9 %collective-permute-start.3 = (bf16[528,256]{1,0:T(8,128)(2,1)S(1)}, bf16[528,256]{1,0:T(8,128)(2,1)S(1)}, u32[]{:S(2)}, u32[]{:S(2)}) collective-permute-start(bf16[528,256]{1,0:T(8,128)(2,1)S(1)} %col_block.1), channel_id=1, source_target_pairs={{0,68},{1,69},{2,70},{3,71},{4,0},{5,1},{6,2},{7,3},{8,56},{9,57},... | collective-permute-start | bytes 811016 | tf_op jit(solution)/shard_map/ppermute | solution.py:40
  13.2 6.3 %collective-permute-start.1 = (bf16[544,128]{1,0:T(8,128)(2,1)S(1)}, bf16[544,128]{1,0:T(8,128)(2,1)S(1)}, u32[]{:S(2)}, u32[]{:S(2)}) collective-permute-start(bf16[544,128]{1,0:T(8,128)(2,1)S(1)} %row_block.1.refs_0_), channel_id=1, source_target_pairs={{0,1},{1,2},{2,3},{3,0},{4,5},{5,6},{6,7},{7,4},{8,9},{9,10},{10,1... | collective-permute-start | bytes 417800 | tf_op jit(solution)/shard_map/ppermute | solution.py:40
  14.3 5.2 %collective-permute-start = (bf16[544,128]{1,0:T(8,128)(2,1)S(1)}, bf16[544,128]{1,0:T(8,128)(2,1)S(1)}, u32[]{:S(2)}, u32[]{:S(2)}) collective-permute-start(bf16[544,128]{1,0:T(8,128)(2,1)S(1)} %row_block.1.refs_0_), channel_id=1, source_target_pairs={{0,3},{1,0},{2,1},{3,2},{4,7},{5,4},{6,5},{7,6},{8,11},{9,8},{10,9... | collective-permute-start | bytes 417800 | tf_op jit(solution)/shard_map/ppermute | solution.py:40
  19.6 6.8 %collective-permute-start.6 = (bf16[2112,256]{1,0:T(8,128)(2,1)S(1)}, bf16[2112,256]{1,0:T(8,128)(2,1)S(1)}, u32[]{:S(2)}, u32[]{:S(2)}) collective-permute-start(bf16[2112,256]{1,0:T(8,128)(2,1)S(1)} %pad_maximum_fusion), channel_id=1, source_target_pairs={{0,8},{1,9},{2,10},{3,11},{4,12},{5,13},{6,14},{7,15},{8,0},{9,1},... | collective-permute-start | bytes 3244040 | tf_op jit(solution)/shard_map/ppermute | solution.py:40
  19.8 13.2 %collective-permute-start.8 = (bf16[1056,256]{1,0:T(8,128)(2,1)S(1)}, bf16[1056,256]{1,0:T(8,128)(2,1)S(1)}, u32[]{:S(2)}, u32[]{:S(2)}) collective-permute-start(bf16[1056,256]{1,0:T(8,128)(2,1)S(1)} %pad_maximum_fusion.1.refs_3_.refs_1_), channel_id=1, source_target_pairs={{0,16},{1,17},{2,18},{3,19},{4,20},{5,21},{6,22},{7,23},{8,12},{9,... | collective-permute-start | bytes 1622024 | tf_op jit(solution)/shard_map/ppermute | solution.py:40
  21.4 11.6 %collective-permute-start.7 = (bf16[1056,256]{1,0:T(8,128)(2,1)S(1)}, bf16[1056,256]{1,0:T(8,128)(2,1)S(1)}, u32[]{:S(2)}, u32[]{:S(2)}) collective-permute-start(bf16[1056,256]{1,0:T(8,128)(2,1)S(1)} %pad_maximum_fusion.1.refs_3_.refs_1_), channel_id=1, source_target_pairs={{0,48},{1,49},{2,50},{3,51},{4,52},{5,53},{6,54},{7,55},{8,76},{9,... | collective-permute-start | bytes 1622024 | tf_op jit(solution)/shard_map/ppermute | solution.py:40
  23.1 14.3 %collective-permute-start.12 = (bf16[1056,256]{1,0:T(8,128)(2,1)S(1)}, bf16[1056,256]{1,0:T(8,128)(2,1)S(1)}, u32[]{:S(2)}, u32[]{:S(2)}) collective-permute-start(bf16[1056,256]{1,0:T(8,128)(2,1)S(1)} %constant_dynamic-update-slice_fusion.refs_4_.refs_2_), channel_id=1, source_target_pairs={{0,16},{1,17},{2,18},{3,19},{4,20},{5,21},{6,22},{7,23},{8,12},{9,... | collective-permute-start | bytes 1622024 | tf_op jit(solution)/shard_map/ppermute | solution.py:40
  23.5 13.9 %collective-permute-start.11 = (bf16[1056,256]{1,0:T(8,128)(2,1)S(1)}, bf16[1056,256]{1,0:T(8,128)(2,1)S(1)}, u32[]{:S(2)}, u32[]{:S(2)}) collective-permute-start(bf16[1056,256]{1,0:T(8,128)(2,1)S(1)} %constant_dynamic-update-slice_fusion.refs_4_.refs_2_), channel_id=1, source_target_pairs={{0,48},{1,49},{2,50},{3,51},{4,52},{5,53},{6,54},{7,55},{8,76},{9,... | collective-permute-start | bytes 1622024 | tf_op jit(solution)/shard_map/ppermute | solution.py:40
  33.0 7.7 %collective-permute-start.10 = (bf16[1056,256]{1,0:T(8,128)(2,1)S(1)}, bf16[1056,256]{1,0:T(8,128)(2,1)S(1)}, u32[]{:S(2)}, u32[]{:S(2)}) collective-permute-start(bf16[1056,256]{1,0:T(8,128)(2,1)S(1)} %collective-permute-done.8.refs_4_.refs_5_), channel_id=1, source_target_pairs={{0,8},{1,9},{2,10},{3,11},{4,12},{5,13},{6,14},{7,15},{8,0},{9,1},... | collective-permute-start | bytes 1622024 | tf_op jit(solution)/shard_map/ppermute | solution.py:40
  33.1 8.2 %collective-permute-start.9 = (bf16[1056,256]{1,0:T(8,128)(2,1)S(1)}, bf16[1056,256]{1,0:T(8,128)(2,1)S(1)}, u32[]{:S(2)}, u32[]{:S(2)}) collective-permute-start(bf16[1056,256]{1,0:T(8,128)(2,1)S(1)} %collective-permute-done.7.refs_3_.refs_4_), channel_id=1, source_target_pairs={{0,8},{1,9},{2,10},{3,11},{4,12},{5,13},{6,14},{7,15},{8,0},{9,1},... | collective-permute-start | bytes 1622024 | tf_op jit(solution)/shard_map/ppermute | solution.py:40
  37.4 10.6 %collective-permute-start.14 = (bf16[1056,256]{1,0:T(8,128)(2,1)S(1)}, bf16[1056,256]{1,0:T(8,128)(2,1)S(1)}, u32[]{:S(2)}, u32[]{:S(2)}) collective-permute-start(bf16[1056,256]{1,0:T(8,128)(2,1)S(1)} %collective-permute-done.12.refs_6_.refs_9_), channel_id=1, source_target_pairs={{0,16},{1,17},{2,18},{3,19},{4,20},{5,21},{6,22},{7,23},{8,12},{9,... | collective-permute-start | bytes 1622024 | tf_op jit(solution)/shard_map/ppermute | solution.py:40
  38.1 9.9 %collective-permute-start.13 = (bf16[1056,256]{1,0:T(8,128)(2,1)S(1)}, bf16[1056,256]{1,0:T(8,128)(2,1)S(1)}, u32[]{:S(2)}, u32[]{:S(2)}) collective-permute-start(bf16[1056,256]{1,0:T(8,128)(2,1)S(1)} %collective-permute-done.7.refs_3_.refs_4_), channel_id=1, source_target_pairs={{0,48},{1,49},{2,50},{3,51},{4,52},{5,53},{6,54},{7,55},{8,76},{9,... | collective-permute-start | bytes 1622024 | tf_op jit(solution)/shard_map/ppermute | solution.py:40
  40.7 7.9 %collective-permute-start.18 = (bf16[1056,256]{1,0:T(8,128)(2,1)S(1)}, bf16[1056,256]{1,0:T(8,128)(2,1)S(1)}, u32[]{:S(2)}, u32[]{:S(2)}) collective-permute-start(bf16[1056,256]{1,0:T(8,128)(2,1)S(1)} %collective-permute-done.12.refs_6_.refs_9_), channel_id=1, source_target_pairs={{0,8},{1,9},{2,10},{3,11},{4,12},{5,13},{6,14},{7,15},{8,0},{9,1},... | collective-permute-start | bytes 1622024 | tf_op jit(solution)/shard_map/ppermute | solution.py:40
  40.7 7.9 %collective-permute-start.17 = (bf16[1056,256]{1,0:T(8,128)(2,1)S(1)}, bf16[1056,256]{1,0:T(8,128)(2,1)S(1)}, u32[]{:S(2)}, u32[]{:S(2)}) collective-permute-start(bf16[1056,256]{1,0:T(8,128)(2,1)S(1)} %collective-permute-done.11.refs_5_.refs_8_), channel_id=1, source_target_pairs={{0,8},{1,9},{2,10},{3,11},{4,12},{5,13},{6,14},{7,15},{8,0},{9,1},... | collective-permute-start | bytes 1622024 | tf_op jit(solution)/shard_map/ppermute | solution.py:40
  48.1 4.5 %collective-permute-start.15 = (bf16[1056,256]{1,0:T(8,128)(2,1)S(1)}, bf16[1056,256]{1,0:T(8,128)(2,1)S(1)}, u32[]{:S(2)}, u32[]{:S(2)}) collective-permute-start(bf16[1056,256]{1,0:T(8,128)(2,1)S(1)} %collective-permute-done.13.refs_3_.refs_12_), channel_id=1, source_target_pairs={{0,8},{1,9},{2,10},{3,11},{4,12},{5,13},{6,14},{7,15},{8,0},{9,1},... | collective-permute-start | bytes 1622024 | tf_op jit(solution)/shard_map/ppermute | solution.py:40
  48.1 4.4 %collective-permute-start.16 = (bf16[1056,256]{1,0:T(8,128)(2,1)S(1)}, bf16[1056,256]{1,0:T(8,128)(2,1)S(1)}, u32[]{:S(2)}, u32[]{:S(2)}) collective-permute-start(bf16[1056,256]{1,0:T(8,128)(2,1)S(1)} %collective-permute-done.14.refs_4_.refs_13_), channel_id=1, source_target_pairs={{0,8},{1,9},{2,10},{3,11},{4,12},{5,13},{6,14},{7,15},{8,0},{9,1},... | collective-permute-start | bytes 1622024 | tf_op jit(solution)/shard_map/ppermute | solution.py:40
  59.7 12.9 %collective-permute-start.19 = (f32[512,128]{1,0:T(8,128)S(1)}, f32[512,128]{1,0:T(8,128)S(1)}, u32[]{:S(2)}, u32[]{:S(2)}) collective-permute-start(f32[512,128]{1,0:T(8,128)S(1)} %get-tuple-element.39), channel_id=1, source_target_pairs={{0,1},{1,2},{2,3},{3,0},{4,5},{5,6},{6,7},{7,4},{8,9},{9,10},{10,1... | collective-permute-start | bytes 786440 | tf_op jit(solution)/shard_map/ppermute | solution.py:40
  59.8 14.7 %collective-permute-start.20 = (f32[512,128]{1,0:T(8,128)S(1)}, f32[512,128]{1,0:T(8,128)S(1)}, u32[]{:S(2)}, u32[]{:S(2)}) collective-permute-start(f32[512,128]{1,0:T(8,128)S(1)} %get-tuple-element.40), channel_id=1, source_target_pairs={{0,3},{1,0},{2,1},{3,2},{4,7},{5,4},{6,5},{7,6},{8,11},{9,8},{10,9... | collective-permute-start | bytes 786440 | tf_op jit(solution)/shard_map/ppermute | solution.py:40
  63.1 13.3 %collective-permute-start.21 = (f32[512,128]{1,0:T(8,128)S(1)}, f32[512,128]{1,0:T(8,128)S(1)}, u32[]{:S(2)}, u32[]{:S(2)}) collective-permute-start(f32[512,128]{1,0:T(8,128)S(1)} %get-tuple-element.41), channel_id=1, source_target_pairs={{0,2},{1,3},{2,0},{3,1},{4,6},{5,7},{6,4},{7,5},{8,10},{9,11},{10,... | collective-permute-start | bytes 786440 | tf_op jit(solution)/shard_map/ppermute | solution.py:40
  76.8 1.3 %collective-permute-start.22 = (f32[128,128]{1,0:T(8,128)S(1)}, f32[128,128]{1,0:T(8,128)S(1)}, u32[]{:S(2)}, u32[]{:S(2)}) collective-permute-start(f32[128,128]{1,0:T(8,128)S(1)} %get-tuple-element.43), channel_id=1, source_target_pairs={{0,8},{1,9},{2,10},{3,11},{4,12},{5,13},{6,14},{7,15},{8,0},{9,1},... | collective-permute-start | bytes 196616 | tf_op jit(solution)/shard_map/ppermute | solution.py:40
  78.1 5.5 %collective-permute-start.25 = (f32[128,128]{1,0:T(8,128)S(1)}, f32[128,128]{1,0:T(8,128)S(1)}, u32[]{:S(2)}, u32[]{:S(2)}) collective-permute-start(f32[128,128]{1,0:T(8,128)S(1)} %add.21), channel_id=1, source_target_pairs={{0,1},{1,2},{2,3},{3,0},{4,5},{5,6},{6,7},{7,4},{8,9},{9,10},{10,1... | collective-permute-start | bytes 196616 | tf_op jit(solution)/shard_map/ppermute | solution.py:40
  79.4 5.1 %collective-permute-start.24 = (f32[128,128]{1,0:T(8,128)S(1)}, f32[128,128]{1,0:T(8,128)S(1)}, u32[]{:S(2)}, u32[]{:S(2)}) collective-permute-start(f32[128,128]{1,0:T(8,128)S(1)} %add.21), channel_id=1, source_target_pairs={{0,3},{1,0},{2,1},{3,2},{4,7},{5,4},{6,5},{7,6},{8,11},{9,8},{10,9... | collective-permute-start | bytes 196616 | tf_op jit(solution)/shard_map/ppermute | solution.py:40
  81.5 5.8 %collective-permute-start.23 = (f32[128,128]{1,0:T(8,128)S(1)}, f32[128,128]{1,0:T(8,128)S(1)}, u32[]{:S(2)}, u32[]{:S(2)}) collective-permute-start(f32[128,128]{1,0:T(8,128)S(1)} %add.21), channel_id=1, source_target_pairs={{0,2},{1,3},{2,0},{3,1},{4,6},{5,7},{6,4},{7,5},{8,10},{9,11},{10,... | collective-permute-start | bytes 196616 | tf_op jit(solution)/shard_map/ppermute | solution.py:40
  87.2 5.6 %collective-permute-start.28 = (f32[128,128]{1,0:T(8,128)S(1)}, f32[128,128]{1,0:T(8,128)S(1)}, u32[]{:S(2)}, u32[]{:S(2)}) collective-permute-start(f32[128,128]{1,0:T(8,128)S(1)} %add_add_fusion.1), channel_id=1, source_target_pairs={{0,16},{1,17},{2,18},{3,19},{4,20},{5,21},{6,22},{7,23},{8,24},{9,... | collective-permute-start | bytes 196616 | tf_op jit(solution)/shard_map/ppermute | solution.py:40
  88.1 4.9 %collective-permute-start.27 = (f32[128,128]{1,0:T(8,128)S(1)}, f32[128,128]{1,0:T(8,128)S(1)}, u32[]{:S(2)}, u32[]{:S(2)}) collective-permute-start(f32[128,128]{1,0:T(8,128)S(1)} %add_add_fusion.1), channel_id=1, source_target_pairs={{0,48},{1,49},{2,50},{3,51},{4,52},{5,53},{6,54},{7,55},{8,56},{9,... | collective-permute-start | bytes 196616 | tf_op jit(solution)/shard_map/ppermute | solution.py:40
  90.6 5.8 %collective-permute-start.26 = (f32[128,128]{1,0:T(8,128)S(1)}, f32[128,128]{1,0:T(8,128)S(1)}, u32[]{:S(2)}, u32[]{:S(2)}) collective-permute-start(f32[128,128]{1,0:T(8,128)S(1)} %add_add_fusion.1), channel_id=1, source_target_pairs={{0,32},{1,33},{2,34},{3,35},{4,36},{5,37},{6,38},{7,39},{8,40},{9,... | collective-permute-start | bytes 196616 | tf_op jit(solution)/shard_map/ppermute | solution.py:40
  96.3 5.5 %collective-permute-start.31 = (f32[128,128]{1,0:T(8,128)S(1)}, f32[128,128]{1,0:T(8,128)S(1)}, u32[]{:S(2)}, u32[]{:S(2)}) collective-permute-start(f32[128,128]{1,0:T(8,128)S(1)} %add_add_fusion.g_ref), channel_id=1, source_target_pairs={{0,4},{1,5},{2,6},{3,7},{4,64},{5,65},{6,66},{7,67},{8,12},{9,13},... | collective-permute-start | bytes 196616 | tf_op jit(solution)/shard_map/ppermute | solution.py:40
  97.0 4.9 %collective-permute-start.30 = (f32[128,128]{1,0:T(8,128)S(1)}, f32[128,128]{1,0:T(8,128)S(1)}, u32[]{:S(2)}, u32[]{:S(2)}) collective-permute-start(f32[128,128]{1,0:T(8,128)S(1)} %add_add_fusion.g_ref), channel_id=1, source_target_pairs={{0,68},{1,69},{2,70},{3,71},{4,0},{5,1},{6,2},{7,3},{8,76},{9,77},... | collective-permute-start | bytes 196616 | tf_op jit(solution)/shard_map/ppermute | solution.py:40
  99.6 5.8 %collective-permute-start.29 = (f32[128,128]{1,0:T(8,128)S(1)}, f32[128,128]{1,0:T(8,128)S(1)}, u32[]{:S(2)}, u32[]{:S(2)}) collective-permute-start(f32[128,128]{1,0:T(8,128)S(1)} %add_add_fusion.g_ref), channel_id=1, source_target_pairs={{0,64},{1,65},{2,66},{3,67},{4,68},{5,69},{6,70},{7,71},{8,72},{9,... | collective-permute-start | bytes 196616 | tf_op jit(solution)/shard_map/ppermute | solution.py:40

commit v4 on v3

--- a/solution.py
+++ b/solution.py
@@ -314,7 +314,8 @@
     order = (1, -1, 2)
     mine = row_block(points)
     block = col_block(points, probes)
-    near = [from_z(mine, d) for d in order]
+    turns = (2, 1, -1)
+    near = [from_z(mine, d) for d in turns]
     legs = [first_leg(block, d) for d in order]
     held = lax.optimization_barrier(near + legs)
     near, legs = held[:3], held[3:]
@@ -341,7 +342,7 @@
     away = sketch_part(near, across + far, acc, True, True, "away_last")
     blocks = early + partner + rest_a + other_a + rest_b + other_b + across + far
     held = lax.optimization_barrier([away[i * BLK:(i + 1) * BLK] for i in range(3)] + [mine])
-    back = [from_z(v, -d) for v, d in zip(held[:3], order)]
+    back = [from_z(v, -d) for v, d in zip(held[:3], turns)]
     home = sketch_part(held[3:], blocks, None, True, False, "home")
     rows, gram = finish_rows(home, *back)
     gram = gram + swap(gram)

time: 112 us -> 112 us (level)
  no operation moved by 1% of the time
where the time goes in v4:
time: 112 us; the launch traced here: 111 us
  Pallas kernels  43.7 us (39%)
  starting transfers between devices  41.7 us (37%)
  waiting for transfers between devices  22.3 us (20%)
  local copies, waits for them, and re-layouts  2.6 us (2%)
    ppermute x32, starting transfers between devices, fetch(): return lax.ppermute(value, AXES, sorted(pairs))  41.7 us
    pallas_call x6, Pallas kernels, sketch_part(): pl.pallas_call(body, out_shape=pltpu.VMEM(shape, jnp.float32), in_specs=[...  36.2 us
    ppermute x32, waiting for transfers between devices, fetch(): return lax.ppermute(value, AXES, sorted(pairs))  22.3 us
    pallas_call x1, Pallas kernels, make_basis(): pl.pallas_call(basis_body, out_shape=jax.ShapeDtypeStruct((BLK, DIM), jnp...  6.66 us
    unnamed x6, local copies, waits for them, and re-layouts  2.52 us
  transfers between devices with their start and end apart: 32, of which 13 were waited for; matrix products, arithmetic and copies ran while one was open for 1% of the time, Pallas kernels for 26%

profile of v4, /device:TPU:0, one launch (start us, length us, event | category | flops | bytes accessed | tf_op | source)
XLA Modules:
  0.0 111.4 jit_solution(10421667175702408992)
XLA Ops:
  0.6 0.9 copy-done
  1.8 2.1 %collective-permute-start.2 = (bf16[544,128]{1,0:T(8,128)(2,1)S(1)}, bf16[544,128]{1,0:T(8,128)(2,1)S(1)}, u32[]{:S(2)}, u32[]{:S(2)}) collective-permute-start(bf16[544,128]{1,0:T(8,128)(2,1)S(1)} %row_block.1.refs_0_), channel_id=1, source_target_pairs={{0,1},{1,2},{2,3},{3,0},{4,5},{5,6},{6,7},{7,4},{8,9},{9,10},{10,1... | collective-permute-start | bytes 417800 | tf_op jit(solution)/shard_map/ppermute | solution.py:40
  3.8 0.9 copy-done.1
  4.9 3.1 %collective-permute-start.5 = (bf16[528,256]{1,0:T(8,128)(2,1)S(1)}, bf16[528,256]{1,0:T(8,128)(2,1)S(1)}, u32[]{:S(2)}, u32[]{:S(2)}) collective-permute-start(bf16[528,256]{1,0:T(8,128)(2,1)S(1)} %col_block.1), channel_id=1, source_target_pairs={{0,64},{1,65},{2,66},{3,67},{4,68},{5,69},{6,70},{7,71},{8,40},{9,... | collective-permute-start | bytes 811016 | tf_op jit(solution)/shard_map/ppermute | solution.py:40
  8.0 0.6 collective-permute-start.4
  8.6 2.6 %collective-permute-start.3 = (bf16[528,256]{1,0:T(8,128)(2,1)S(1)}, bf16[528,256]{1,0:T(8,128)(2,1)S(1)}, u32[]{:S(2)}, u32[]{:S(2)}) collective-permute-start(bf16[528,256]{1,0:T(8,128)(2,1)S(1)} %col_block.1), channel_id=1, source_target_pairs={{0,68},{1,69},{2,70},{3,71},{4,0},{5,1},{6,2},{7,3},{8,56},{9,57},... | collective-permute-start | bytes 811016 | tf_op jit(solution)/shard_map/ppermute | solution.py:40
  11.3 2.1 %collective-permute-start.1 = (bf16[544,128]{1,0:T(8,128)(2,1)S(1)}, bf16[544,128]{1,0:T(8,128)(2,1)S(1)}, u32[]{:S(2)}, u32[]{:S(2)}) collective-permute-start(bf16[544,128]{1,0:T(8,128)(2,1)S(1)} %row_block.1.refs_0_), channel_id=1, source_target_pairs={{0,3},{1,0},{2,1},{3,2},{4,7},{5,4},{6,5},{7,6},{8,11},{9,8},{10,9... | collective-permute-start | bytes 417800 | tf_op jit(solution)/shard_map/ppermute | solution.py:40
  13.4 1.9 %collective-permute-start = (bf16[544,128]{1,0:T(8,128)(2,1)S(1)}, bf16[544,128]{1,0:T(8,128)(2,1)S(1)}, u32[]{:S(2)}, u32[]{:S(2)}) collective-permute-start(bf16[544,128]{1,0:T(8,128)(2,1)S(1)} %row_block.1.refs_0_), channel_id=1, source_target_pairs={{0,2},{1,3},{2,0},{3,1},{4,6},{5,7},{6,4},{7,5},{8,10},{9,11},{10,... | collective-permute-start | bytes 417800 | tf_op jit(solution)/shard_map/ppermute | solution.py:40
  15.3 3.7 %collective-permute-done.1.refs_1_ = bf16[544,128]{1,0:T(8,128)(2,1)S(1)} collective-permute-done((bf16[544,128]{1,0:T(8,128)(2,1)S(1)}, bf16[544,128]{1,0:T(8,128)(2,1)S(1)}, u32[]{:S(2)}, u32[]{:S(2)}) %collective-permute-start.1) | collective-permute-done | bytes 139296 | tf_op jit(solution)/shard_map/ppermute | solution.py:40
  19.0 1.0 collective-permute-done.refs_0_
  20.2 1.6 %collective-permute-start.8 = (bf16[1056,256]{1,0:T(8,128)(2,1)S(1)}, bf16[1056,256]{1,0:T(8,128)(2,1)S(1)}, u32[]{:S(2)}, u32[]{:S(2)}) collective-permute-start(bf16[1056,256]{1,0:T(8,128)(2,1)S(1)} %pad_maximum_fusion.1.refs_3_.refs_1_), channel_id=1, source_target_pairs={{0,16},{1,17},{2,18},{3,19},{4,20},{5,21},{6,22},{7,23},{8,12},{9,... | collective-permute-start | bytes 1622024 | tf_op jit(solution)/shard_map/ppermute | solution.py:40
  21.9 1.7 %collective-permute-start.7 = (bf16[1056,256]{1,0:T(8,128)(2,1)S(1)}, bf16[1056,256]{1,0:T(8,128)(2,1)S(1)}, u32[]{:S(2)}, u32[]{:S(2)}) collective-permute-start(bf16[1056,256]{1,0:T(8,128)(2,1)S(1)} %pad_maximum_fusion.1.refs_3_.refs_1_), channel_id=1, source_target_pairs={{0,48},{1,49},{2,50},{3,51},{4,52},{5,53},{6,54},{7,55},{8,76},{9,... | collective-permute-start | bytes 1622024 | tf_op jit(solution)/shard_map/ppermute | solution.py:40
  23.6 0.4 collective-permute-start.12
  24.0 2.9 %collective-permute-start.11 = (bf16[1056,256]{1,0:T(8,128)(2,1)S(1)}, bf16[1056,256]{1,0:T(8,128)(2,1)S(1)}, u32[]{:S(2)}, u32[]{:S(2)}) collective-permute-start(bf16[1056,256]{1,0:T(8,128)(2,1)S(1)} %constant_dynamic-update-slice_fusion.refs_4_.refs_2_), channel_id=1, source_target_pairs={{0,48},{1,49},{2,50},{3,51},{4,52},{5,53},{6,54},{7,55},{8,76},{9,... | collective-permute-start | bytes 1622024 | tf_op jit(solution)/shard_map/ppermute | solution.py:40
  26.9 6.5 %early.1.refs_5_ = f32[6,128,256]{2,1,0:T(8,128)S(1)} custom-call(bf16[544,128]{1,0:T(8,128)(2,1)S(1)} %collective-permute-done.refs_0_, bf16[544,128]{1,0:T(8,128)(2,1)S(1)} %collective-permute-done.1.refs_1_, bf16[544,128]{1,0:T(8,128)(2,1)S(1)} %collective-permute-done.2.refs_2_, bf16[1056,256]{1,0:T(8,128)(2,1)S(1)} %pad_maximum_fusion.1.refs_3_.refs_1_, ...), custom_call_target="tpu_custom_call" | custom-call | flops 4831838208 | bytes 5767168 | tf_op jit(solution)/shard_map/early/pallas_call | solution.py:213
  33.5 0.5 collective-permute-start.9
  34.0 3.8 %a_own.1.refs_7_ = f32[6,128,256]{2,1,0:T(8,128)S(1)} custom-call(bf16[544,128]{1,0:T(8,128)(2,1)S(1)} %collective-permute-done.refs_0_, bf16[544,128]{1,0:T(8,128)(2,1)S(1)} %collective-permute-done.1.refs_1_, bf16[544,128]{1,0:T(8,128)(2,1)S(1)} %collective-permute-done.2.refs_2_, bf16[1056,256]{1,0:T(8,128)(2,1)S(1)} %collective-permute-done.7.refs_3_.refs_4_, ...), custom_call_target="tpu_custom_call" | custom-call | flops 2415919104 | bytes 3670016 | tf_op jit(solution)/shard_map/a_own/pallas_call | solution.py:213
  37.9 0.7 collective-permute-start.14
  38.6 2.6 %collective-permute-start.13 = (bf16[1056,256]{1,0:T(8,128)(2,1)S(1)}, bf16[1056,256]{1,0:T(8,128)(2,1)S(1)}, u32[]{:S(2)}, u32[]{:S(2)}) collective-permute-start(bf16[1056,256]{1,0:T(8,128)(2,1)S(1)} %collective-permute-done.7.refs_3_.refs_4_), channel_id=1, source_target_pairs={{0,48},{1,49},{2,50},{3,51},{4,52},{5,53},{6,54},{7,55},{8,76},{9,... | collective-permute-start | bytes 1622024 | tf_op jit(solution)/shard_map/ppermute | solution.py:40
  41.2 0.5 collective-permute-start.17
  41.7 6.8 %a_other_b_own.1.refs_5_ = f32[6,128,256]{2,1,0:T(8,128)S(1)} custom-call(bf16[544,128]{1,0:T(8,128)(2,1)S(1)} %collective-permute-done.refs_0_, bf16[544,128]{1,0:T(8,128)(2,1)S(1)} %collective-permute-done.1.refs_1_, bf16[544,128]{1,0:T(8,128)(2,1)S(1)} %collective-permute-done.2.refs_2_, bf16[1056,256]{1,0:T(8,128)(2,1)S(1)} %collective-permute-done.9.refs_3_.refs_6_, ...), custom_call_target="tpu_custom_call" | custom-call | flops 4831838208 | bytes 5767168 | tf_op jit(solution)/shard_map/a_other_b_own/pallas_call | solution.py:213
  48.6 0.5 collective-permute-start.16
  49.1 3.9 %b_other.1.refs_7_ = f32[6,128,256]{2,1,0:T(8,128)S(1)} custom-call(bf16[544,128]{1,0:T(8,128)(2,1)S(1)} %collective-permute-done.refs_0_, bf16[544,128]{1,0:T(8,128)(2,1)S(1)} %collective-permute-done.1.refs_1_, bf16[544,128]{1,0:T(8,128)(2,1)S(1)} %collective-permute-done.2.refs_2_, bf16[1056,256]{1,0:T(8,128)(2,1)S(1)} %collective-permute-done.17.refs_3_.refs_10_, ...), custom_call_target="tpu_custom_call" | custom-call | flops 2415919104 | bytes 3670016 | tf_op jit(solution)/shard_map/b_other/pallas_call | solution.py:213
  53.0 7.1 %away_last.1 = f32[1536,128]{1,0:T(8,128)S(1)} custom-call(bf16[544,128]{1,0:T(8,128)(2,1)S(1)} %collective-permute-done.refs_0_, bf16[544,128]{1,0:T(8,128)(2,1)S(1)} %collective-permute-done.1.refs_1_, bf16[544,128]{1,0:T(8,128)(2,1)S(1)} %collective-permute-done.2.refs_2_, bf16[1056,256]{1,0:T(8,128)(2,1)S(1)} %collective-permute-done.13.refs_3_.refs_12_, ...), custom_call_target="tpu_custom_call" | custom-call | flops 4831838208 | bytes 5767168 | tf_op jit(solution)/shard_map/away_last/pallas_call | solution.py:213
  60.1 2.0 %collective-permute-start.19 = (f32[512,128]{1,0:T(8,128)S(1)}, f32[512,128]{1,0:T(8,128)S(1)}, u32[]{:S(2)}, u32[]{:S(2)}) collective-permute-start(f32[512,128]{1,0:T(8,128)S(1)} %get-tuple-element.39), channel_id=1, source_target_pairs={{0,2},{1,3},{2,0},{3,1},{4,6},{5,7},{6,4},{7,5},{8,10},{9,11},{10,... | collective-permute-start | bytes 786440 | tf_op jit(solution)/shard_map/ppermute | solution.py:40
  62.1 1.6 %collective-permute-start.20 = (f32[512,128]{1,0:T(8,128)S(1)}, f32[512,128]{1,0:T(8,128)S(1)}, u32[]{:S(2)}, u32[]{:S(2)}) collective-permute-start(f32[512,128]{1,0:T(8,128)S(1)} %get-tuple-element.40), channel_id=1, source_target_pairs={{0,1},{1,2},{2,3},{3,0},{4,5},{5,6},{6,7},{7,4},{8,9},{9,10},{10,1... | collective-permute-start | bytes 786440 | tf_op jit(solution)/shard_map/ppermute | solution.py:40
  63.7 1.6 %collective-permute-start.21 = (f32[512,128]{1,0:T(8,128)S(1)}, f32[512,128]{1,0:T(8,128)S(1)}, u32[]{:S(2)}, u32[]{:S(2)}) collective-permute-start(f32[512,128]{1,0:T(8,128)S(1)} %get-tuple-element.41), channel_id=1, source_target_pairs={{0,3},{1,0},{2,1},{3,2},{4,7},{5,4},{6,5},{7,6},{8,11},{9,8},{10,9... | collective-permute-start | bytes 786440 | tf_op jit(solution)/shard_map/ppermute | solution.py:40
  65.3 8.1 %home.1.home_ref = f32[512,128]{1,0:T(8,128)S(1)} custom-call(bf16[544,128]{1,0:T(8,128)(2,1)S(1)} %row_block.1.refs_0_, bf16[1056,256]{1,0:T(8,128)(2,1)S(1)} %pad_maximum_fusion.1.refs_3_.refs_1_, bf16[1056,256]{1,0:T(8,128)(2,1)S(1)} %constant_dynamic-update-slice_fusion.refs_4_.refs_2_, bf16[2112,256]{1,0:T(8,128)(2,1)S(1)} %collective-permute-done.6.refs_5_.refs_3_, ...), custom_call_target="tpu_custom_call" | custom-call | flops 6442450944 | bytes 17301504 | tf_op jit(solution)/shard_map/home/pallas_call | solution.py:213
  73.5 2.2 %collective-permute-done.20.b_ref = f32[512,128]{1,0:T(8,128)S(1)} collective-permute-done((f32[512,128]{1,0:T(8,128)S(1)}, f32[512,128]{1,0:T(8,128)S(1)}, u32[]{:S(2)}, u32[]{:S(2)}) %collective-permute-start.20) | collective-permute-done | bytes 262176 | tf_op jit(solution)/shard_map/ppermute | solution.py:40
  75.7 0.4 finish_rows.1
  76.2 1.2 %collective-permute-done.22 = f32[128,128]{1,0:T(8,128)S(1)} collective-permute-done((f32[128,128]{1,0:T(8,128)S(1)}, f32[128,128]{1,0:T(8,128)S(1)}, u32[]{:S(2)}, u32[]{:S(2)}) %collective-permute-start.22) | collective-permute-done | bytes 65568 | tf_op jit(solution)/shard_map/ppermute | solution.py:40
  77.5 1.8 %collective-permute-start.25 = (f32[128,128]{1,0:T(8,128)S(1)}, f32[128,128]{1,0:T(8,128)S(1)}, u32[]{:S(2)}, u32[]{:S(2)}) collective-permute-start(f32[128,128]{1,0:T(8,128)S(1)} %add.21), channel_id=1, source_target_pairs={{0,1},{1,2},{2,3},{3,0},{4,5},{5,6},{6,7},{7,4},{8,9},{9,10},{10,1... | collective-permute-start | bytes 196616 | tf_op jit(solution)/shard_map/ppermute | solution.py:40
  79.2 1.5 %collective-permute-start.24 = (f32[128,128]{1,0:T(8,128)S(1)}, f32[128,128]{1,0:T(8,128)S(1)}, u32[]{:S(2)}, u32[]{:S(2)}) collective-permute-start(f32[128,128]{1,0:T(8,128)S(1)} %add.21), channel_id=1, source_target_pairs={{0,3},{1,0},{2,1},{3,2},{4,7},{5,4},{6,5},{7,6},{8,11},{9,8},{10,9... | collective-permute-start | bytes 196616 | tf_op jit(solution)/shard_map/ppermute | solution.py:40
  80.8 1.2 %collective-permute-start.23 = (f32[128,128]{1,0:T(8,128)S(1)}, f32[128,128]{1,0:T(8,128)S(1)}, u32[]{:S(2)}, u32[]{:S(2)}) collective-permute-start(f32[128,128]{1,0:T(8,128)S(1)} %add.21), channel_id=1, source_target_pairs={{0,2},{1,3},{2,0},{3,1},{4,6},{5,7},{6,4},{7,5},{8,10},{9,11},{10,... | collective-permute-start | bytes 196616 | tf_op jit(solution)/shard_map/ppermute | solution.py:40
  81.9 1.1 collective-permute-done.25
  83.0 0.9 collective-permute-done.24
  83.9 2.6 %collective-permute-done.23 = f32[128,128]{1,0:T(8,128)S(1)} collective-permute-done((f32[128,128]{1,0:T(8,128)S(1)}, f32[128,128]{1,0:T(8,128)S(1)}, u32[]{:S(2)}, u32[]{:S(2)}) %collective-permute-start.23) | collective-permute-done | bytes 65568 | tf_op jit(solution)/shard_map/ppermute | solution.py:40
  86.5 0.8 collective-permute-start.28
  87.4 2.5 %collective-permute-start.27 = (f32[128,128]{1,0:T(8,128)S(1)}, f32[128,128]{1,0:T(8,128)S(1)}, u32[]{:S(2)}, u32[]{:S(2)}) collective-permute-start(f32[128,128]{1,0:T(8,128)S(1)} %add_add_fusion.1), channel_id=1, source_target_pairs={{0,48},{1,49},{2,50},{3,51},{4,52},{5,53},{6,54},{7,55},{8,56},{9,... | collective-permute-start | bytes 196616 | tf_op jit(solution)/shard_map/ppermute | solution.py:40
  89.9 1.3 %collective-permute-start.26 = (f32[128,128]{1,0:T(8,128)S(1)}, f32[128,128]{1,0:T(8,128)S(1)}, u32[]{:S(2)}, u32[]{:S(2)}) collective-permute-start(f32[128,128]{1,0:T(8,128)S(1)} %add_add_fusion.1), channel_id=1, source_target_pairs={{0,32},{1,33},{2,34},{3,35},{4,36},{5,37},{6,38},{7,39},{8,40},{9,... | collective-permute-start | bytes 196616 | tf_op jit(solution)/shard_map/ppermute | solution.py:40
  91.2 0.9 collective-permute-done.28
  92.2 3.4 %collective-permute-done.26 = f32[128,128]{1,0:T(8,128)S(1)} collective-permute-done((f32[128,128]{1,0:T(8,128)S(1)}, f32[128,128]{1,0:T(8,128)S(1)}, u32[]{:S(2)}, u32[]{:S(2)}) %collective-permute-start.26) | collective-permute-done | bytes 65568 | tf_op jit(solution)/shard_map/ppermute | solution.py:40
  95.6 1.0 collective-permute-start.31
  96.6 2.3 %collective-permute-start.30 = (f32[128,128]{1,0:T(8,128)S(1)}, f32[128,128]{1,0:T(8,128)S(1)}, u32[]{:S(2)}, u32[]{:S(2)}) collective-permute-start(f32[128,128]{1,0:T(8,128)S(1)} %add_add_fusion.g_ref), channel_id=1, source_target_pairs={{0,68},{1,69},{2,70},{3,71},{4,0},{5,1},{6,2},{7,3},{8,76},{9,77},... | collective-permute-start | bytes 196616 | tf_op jit(solution)/shard_map/ppermute | solution.py:40
  99.0 0.7 copy.5
  99.7 1.5 %collective-permute-done.31.c_ref = f32[128,128]{1,0:T(8,128)S(1)} collective-permute-done((f32[128,128]{1,0:T(8,128)S(1)}, f32[128,128]{1,0:T(8,128)S(1)}, u32[]{:S(2)}, u32[]{:S(2)}) %collective-permute-start.31) | collective-permute-done | bytes 65568 | tf_op jit(solution)/shard_map/ppermute | solution.py:40
  101.2 3.5 %collective-permute-done.29.a_ref = f32[128,128]{1,0:T(8,128)S(1)} collective-permute-done((f32[128,128]{1,0:T(8,128)S(1)}, f32[128,128]{1,0:T(8,128)S(1)}, u32[]{:S(2)}, u32[]{:S(2)}) %collective-permute-start.29) | collective-permute-done | bytes 65568 | tf_op jit(solution)/shard_map/ppermute | solution.py:40
  104.7 6.7 %make_basis.1 = f32[512,128]{1,0:T(8,128)} custom-call(f32[128,128]{1,0:T(8,128)S(1)} %add_add_fusion.g_ref, f32[128,128]{1,0:T(8,128)S(1)} %collective-permute-done.29.a_ref, f32[128,128]{1,0:T(8,128)S(1)} %collective-permute-done.30.b_ref, f32[128,128]{1,0:T(8,128)S(1)} %collective-permute-done.31.c_ref, f32[512,128]{1,0:T(8,128)S(1)} %get-tuple-element.47.rows_ref), custom_call_target="tpu_custom_call" | custom-call | tf_op jit(solution)/shard_map/make_basis/pallas_call | solution.py:294
  (39 shorter events, 1.2 us)
Async XLA Ops:
  0.6 0.9 copy-start
  1.8 11.7 %collective-permute-start.2 = (bf16[544,128]{1,0:T(8,128)(2,1)S(1)}, bf16[544,128]{1,0:T(8,128)(2,1)S(1)}, u32[]{:S(2)}, u32[]{:S(2)}) collective-permute-start(bf16[544,128]{1,0:T(8,128)(2,1)S(1)} %row_block.1.refs_0_), channel_id=1, source_target_pairs={{0,1},{1,2},{2,3},{3,0},{4,5},{5,6},{6,7},{7,4},{8,9},{9,10},{10,1... | collective-permute-start | bytes 417800 | tf_op jit(solution)/shard_map/ppermute | solution.py:40
  3.8 0.9 copy-start.1
  4.9 15.0 %collective-permute-start.5 = (bf16[528,256]{1,0:T(8,128)(2,1)S(1)}, bf16[528,256]{1,0:T(8,128)(2,1)S(1)}, u32[]{:S(2)}, u32[]{:S(2)}) collective-permute-start(bf16[528,256]{1,0:T(8,128)(2,1)S(1)} %col_block.1), channel_id=1, source_target_pairs={{0,64},{1,65},{2,66},{3,67},{4,68},{5,69},{6,70},{7,71},{8,40},{9,... | collective-permute-start | bytes 811016 | tf_op jit(solution)/shard_map/ppermute | solution.py:40
  8.0 11.9 %collective-permute-start.4 = (bf16[528,256]{1,0:T(8,128)(2,1)S(1)}, bf16[528,256]{1,0:T(8,128)(2,1)S(1)}, u32[]{:S(2)}, u32[]{:S(2)}) collective-permute-start(bf16[528,256]{1,0:T(8,128)(2,1)S(1)} %col_block.1), channel_id=1, source_target_pairs={{0,4},{1,5},{2,6},{3,7},{4,64},{5,65},{6,66},{7,67},{8,24},{9,25},... | collective-permute-start | bytes 811016 | tf_op jit(solution)/shard_map/ppermute | solution.py:40
  8.6 11.4 %collective-permute-start.3 = (bf16[528,256]{1,0:T(8,128)(2,1)S(1)}, bf16[528,256]{1,0:T(8,128)(2,1)S(1)}, u32[]{:S(2)}, u32[]{:S(2)}) collective-permute-start(bf16[528,256]{1,0:T(8,128)(2,1)S(1)} %col_block.1), channel_id=1, source_target_pairs={{0,68},{1,69},{2,70},{3,71},{4,0},{5,1},{6,2},{7,3},{8,56},{9,57},... | collective-permute-start | bytes 811016 | tf_op jit(solution)/shard_map/ppermute | solution.py:40
  11.3 7.7 %collective-permute-start.1 = (bf16[544,128]{1,0:T(8,128)(2,1)S(1)}, bf16[544,128]{1,0:T(8,128)(2,1)S(1)}, u32[]{:S(2)}, u32[]{:S(2)}) collective-permute-start(bf16[544,128]{1,0:T(8,128)(2,1)S(1)} %row_block.1.refs_0_), channel_id=1, source_target_pairs={{0,3},{1,0},{2,1},{3,2},{4,7},{5,4},{6,5},{7,6},{8,11},{9,8},{10,9... | collective-permute-start | bytes 417800 | tf_op jit(solution)/shard_map/ppermute | solution.py:40
  13.4 6.6 %collective-permute-start = (bf16[544,128]{1,0:T(8,128)(2,1)S(1)}, bf16[544,128]{1,0:T(8,128)(2,1)S(1)}, u32[]{:S(2)}, u32[]{:S(2)}) collective-permute-start(bf16[544,128]{1,0:T(8,128)(2,1)S(1)} %row_block.1.refs_0_), channel_id=1, source_target_pairs={{0,2},{1,3},{2,0},{3,1},{4,6},{5,7},{6,4},{7,5},{8,10},{9,11},{10,... | collective-permute-start | bytes 417800 | tf_op jit(solution)/shard_map/ppermute | solution.py:40
  20.1 6.8 %collective-permute-start.6 = (bf16[2112,256]{1,0:T(8,128)(2,1)S(1)}, bf16[2112,256]{1,0:T(8,128)(2,1)S(1)}, u32[]{:S(2)}, u32[]{:S(2)}) collective-permute-start(bf16[2112,256]{1,0:T(8,128)(2,1)S(1)} %pad_maximum_fusion), channel_id=1, source_target_pairs={{0,8},{1,9},{2,10},{3,11},{4,12},{5,13},{6,14},{7,15},{8,0},{9,1},... | collective-permute-start | bytes 3244040 | tf_op jit(solution)/shard_map/ppermute | solution.py:40
  20.2 13.2 %collective-permute-start.8 = (bf16[1056,256]{1,0:T(8,128)(2,1)S(1)}, bf16[1056,256]{1,0:T(8,128)(2,1)S(1)}, u32[]{:S(2)}, u32[]{:S(2)}) collective-permute-start(bf16[1056,256]{1,0:T(8,128)(2,1)S(1)} %pad_maximum_fusion.1.refs_3_.refs_1_), channel_id=1, source_target_pairs={{0,16},{1,17},{2,18},{3,19},{4,20},{5,21},{6,22},{7,23},{8,12},{9,... | collective-permute-start | bytes 1622024 | tf_op jit(solution)/shard_map/ppermute | solution.py:40
  21.9 11.6 %collective-permute-start.7 = (bf16[1056,256]{1,0:T(8,128)(2,1)S(1)}, bf16[1056,256]{1,0:T(8,128)(2,1)S(1)}, u32[]{:S(2)}, u32[]{:S(2)}) collective-permute-start(bf16[1056,256]{1,0:T(8,128)(2,1)S(1)} %pad_maximum_fusion.1.refs_3_.refs_1_), channel_id=1, source_target_pairs={{0,48},{1,49},{2,50},{3,51},{4,52},{5,53},{6,54},{7,55},{8,76},{9,... | collective-permute-start | bytes 1622024 | tf_op jit(solution)/shard_map/ppermute | solution.py:40
  23.6 14.3 %collective-permute-start.12 = (bf16[1056,256]{1,0:T(8,128)(2,1)S(1)}, bf16[1056,256]{1,0:T(8,128)(2,1)S(1)}, u32[]{:S(2)}, u32[]{:S(2)}) collective-permute-start(bf16[1056,256]{1,0:T(8,128)(2,1)S(1)} %constant_dynamic-update-slice_fusion.refs_4_.refs_2_), channel_id=1, source_target_pairs={{0,16},{1,17},{2,18},{3,19},{4,20},{5,21},{6,22},{7,23},{8,12},{9,... | collective-permute-start | bytes 1622024 | tf_op jit(solution)/shard_map/ppermute | solution.py:40
  24.0 13.8 %collective-permute-start.11 = (bf16[1056,256]{1,0:T(8,128)(2,1)S(1)}, bf16[1056,256]{1,0:T(8,128)(2,1)S(1)}, u32[]{:S(2)}, u32[]{:S(2)}) collective-permute-start(bf16[1056,256]{1,0:T(8,128)(2,1)S(1)} %constant_dynamic-update-slice_fusion.refs_4_.refs_2_), channel_id=1, source_target_pairs={{0,48},{1,49},{2,50},{3,51},{4,52},{5,53},{6,54},{7,55},{8,76},{9,... | collective-permute-start | bytes 1622024 | tf_op jit(solution)/shard_map/ppermute | solution.py:40
  33.4 7.7 %collective-permute-start.10 = (bf16[1056,256]{1,0:T(8,128)(2,1)S(1)}, bf16[1056,256]{1,0:T(8,128)(2,1)S(1)}, u32[]{:S(2)}, u32[]{:S(2)}) collective-permute-start(bf16[1056,256]{1,0:T(8,128)(2,1)S(1)} %collective-permute-done.8.refs_4_.refs_5_), channel_id=1, source_target_pairs={{0,8},{1,9},{2,10},{3,11},{4,12},{5,13},{6,14},{7,15},{8,0},{9,1},... | collective-permute-start | bytes 1622024 | tf_op jit(solution)/shard_map/ppermute | solution.py:40
  33.5 8.2 %collective-permute-start.9 = (bf16[1056,256]{1,0:T(8,128)(2,1)S(1)}, bf16[1056,256]{1,0:T(8,128)(2,1)S(1)}, u32[]{:S(2)}, u32[]{:S(2)}) collective-permute-start(bf16[1056,256]{1,0:T(8,128)(2,1)S(1)} %collective-permute-done.7.refs_3_.refs_4_), channel_id=1, source_target_pairs={{0,8},{1,9},{2,10},{3,11},{4,12},{5,13},{6,14},{7,15},{8,0},{9,1},... | collective-permute-start | bytes 1622024 | tf_op jit(solution)/shard_map/ppermute | solution.py:40
  37.9 10.6 %collective-permute-start.14 = (bf16[1056,256]{1,0:T(8,128)(2,1)S(1)}, bf16[1056,256]{1,0:T(8,128)(2,1)S(1)}, u32[]{:S(2)}, u32[]{:S(2)}) collective-permute-start(bf16[1056,256]{1,0:T(8,128)(2,1)S(1)} %collective-permute-done.12.refs_6_.refs_9_), channel_id=1, source_target_pairs={{0,16},{1,17},{2,18},{3,19},{4,20},{5,21},{6,22},{7,23},{8,12},{9,... | collective-permute-start | bytes 1622024 | tf_op jit(solution)/shard_map/ppermute | solution.py:40
  38.6 9.9 %collective-permute-start.13 = (bf16[1056,256]{1,0:T(8,128)(2,1)S(1)}, bf16[1056,256]{1,0:T(8,128)(2,1)S(1)}, u32[]{:S(2)}, u32[]{:S(2)}) collective-permute-start(bf16[1056,256]{1,0:T(8,128)(2,1)S(1)} %collective-permute-done.7.refs_3_.refs_4_), channel_id=1, source_target_pairs={{0,48},{1,49},{2,50},{3,51},{4,52},{5,53},{6,54},{7,55},{8,76},{9,... | collective-permute-start | bytes 1622024 | tf_op jit(solution)/shard_map/ppermute | solution.py:40
  41.2 7.9 %collective-permute-start.18 = (bf16[1056,256]{1,0:T(8,128)(2,1)S(1)}, bf16[1056,256]{1,0:T(8,128)(2,1)S(1)}, u32[]{:S(2)}, u32[]{:S(2)}) collective-permute-start(bf16[1056,256]{1,0:T(8,128)(2,1)S(1)} %collective-permute-done.12.refs_6_.refs_9_), channel_id=1, source_target_pairs={{0,8},{1,9},{2,10},{3,11},{4,12},{5,13},{6,14},{7,15},{8,0},{9,1},... | collective-permute-start | bytes 1622024 | tf_op jit(solution)/shard_map/ppermute | solution.py:40
  41.2 7.9 %collective-permute-start.17 = (bf16[1056,256]{1,0:T(8,128)(2,1)S(1)}, bf16[1056,256]{1,0:T(8,128)(2,1)S(1)}, u32[]{:S(2)}, u32[]{:S(2)}) collective-permute-start(bf16[1056,256]{1,0:T(8,128)(2,1)S(1)} %collective-permute-done.11.refs_5_.refs_8_), channel_id=1, source_target_pairs={{0,8},{1,9},{2,10},{3,11},{4,12},{5,13},{6,14},{7,15},{8,0},{9,1},... | collective-permute-start | bytes 1622024 | tf_op jit(solution)/shard_map/ppermute | solution.py:40
  48.5 4.5 %collective-permute-start.15 = (bf16[1056,256]{1,0:T(8,128)(2,1)S(1)}, bf16[1056,256]{1,0:T(8,128)(2,1)S(1)}, u32[]{:S(2)}, u32[]{:S(2)}) collective-permute-start(bf16[1056,256]{1,0:T(8,128)(2,1)S(1)} %collective-permute-done.13.refs_3_.refs_12_), channel_id=1, source_target_pairs={{0,8},{1,9},{2,10},{3,11},{4,12},{5,13},{6,14},{7,15},{8,0},{9,1},... | collective-permute-start | bytes 1622024 | tf_op jit(solution)/shard_map/ppermute | solution.py:40
  48.6 4.4 %collective-permute-start.16 = (bf16[1056,256]{1,0:T(8,128)(2,1)S(1)}, bf16[1056,256]{1,0:T(8,128)(2,1)S(1)}, u32[]{:S(2)}, u32[]{:S(2)}) collective-permute-start(bf16[1056,256]{1,0:T(8,128)(2,1)S(1)} %collective-permute-done.14.refs_4_.refs_13_), channel_id=1, source_target_pairs={{0,8},{1,9},{2,10},{3,11},{4,12},{5,13},{6,14},{7,15},{8,0},{9,1},... | collective-permute-start | bytes 1622024 | tf_op jit(solution)/shard_map/ppermute | solution.py:40
  60.1 13.3 %collective-permute-start.19 = (f32[512,128]{1,0:T(8,128)S(1)}, f32[512,128]{1,0:T(8,128)S(1)}, u32[]{:S(2)}, u32[]{:S(2)}) collective-permute-start(f32[512,128]{1,0:T(8,128)S(1)} %get-tuple-element.39), channel_id=1, source_target_pairs={{0,2},{1,3},{2,0},{3,1},{4,6},{5,7},{6,4},{7,5},{8,10},{9,11},{10,... | collective-permute-start | bytes 786440 | tf_op jit(solution)/shard_map/ppermute | solution.py:40
  62.1 13.5 %collective-permute-start.20 = (f32[512,128]{1,0:T(8,128)S(1)}, f32[512,128]{1,0:T(8,128)S(1)}, u32[]{:S(2)}, u32[]{:S(2)}) collective-permute-start(f32[512,128]{1,0:T(8,128)S(1)} %get-tuple-element.40), channel_id=1, source_target_pairs={{0,1},{1,2},{2,3},{3,0},{4,5},{5,6},{6,7},{7,4},{8,9},{9,10},{10,1... | collective-permute-start | bytes 786440 | tf_op jit(solution)/shard_map/ppermute | solution.py:40
  63.7 11.9 %collective-permute-start.21 = (f32[512,128]{1,0:T(8,128)S(1)}, f32[512,128]{1,0:T(8,128)S(1)}, u32[]{:S(2)}, u32[]{:S(2)}) collective-permute-start(f32[512,128]{1,0:T(8,128)S(1)} %get-tuple-element.41), channel_id=1, source_target_pairs={{0,3},{1,0},{2,1},{3,2},{4,7},{5,4},{6,5},{7,6},{8,11},{9,8},{10,9... | collective-permute-start | bytes 786440 | tf_op jit(solution)/shard_map/ppermute | solution.py:40
  76.1 1.3 %collective-permute-start.22 = (f32[128,128]{1,0:T(8,128)S(1)}, f32[128,128]{1,0:T(8,128)S(1)}, u32[]{:S(2)}, u32[]{:S(2)}) collective-permute-start(f32[128,128]{1,0:T(8,128)S(1)} %get-tuple-element.43), channel_id=1, source_target_pairs={{0,8},{1,9},{2,10},{3,11},{4,12},{5,13},{6,14},{7,15},{8,0},{9,1},... | collective-permute-start | bytes 196616 | tf_op jit(solution)/shard_map/ppermute | solution.py:40
  77.5 5.5 %collective-permute-start.25 = (f32[128,128]{1,0:T(8,128)S(1)}, f32[128,128]{1,0:T(8,128)S(1)}, u32[]{:S(2)}, u32[]{:S(2)}) collective-permute-start(f32[128,128]{1,0:T(8,128)S(1)} %add.21), channel_id=1, source_target_pairs={{0,1},{1,2},{2,3},{3,0},{4,5},{5,6},{6,7},{7,4},{8,9},{9,10},{10,1... | collective-permute-start | bytes 196616 | tf_op jit(solution)/shard_map/ppermute | solution.py:40
  79.2 4.7 %collective-permute-start.24 = (f32[128,128]{1,0:T(8,128)S(1)}, f32[128,128]{1,0:T(8,128)S(1)}, u32[]{:S(2)}, u32[]{:S(2)}) collective-permute-start(f32[128,128]{1,0:T(8,128)S(1)} %add.21), channel_id=1, source_target_pairs={{0,3},{1,0},{2,1},{3,2},{4,7},{5,4},{6,5},{7,6},{8,11},{9,8},{10,9... | collective-permute-start | bytes 196616 | tf_op jit(solution)/shard_map/ppermute | solution.py:40
  80.8 5.8 %collective-permute-start.23 = (f32[128,128]{1,0:T(8,128)S(1)}, f32[128,128]{1,0:T(8,128)S(1)}, u32[]{:S(2)}, u32[]{:S(2)}) collective-permute-start(f32[128,128]{1,0:T(8,128)S(1)} %add.21), channel_id=1, source_target_pairs={{0,2},{1,3},{2,0},{3,1},{4,6},{5,7},{6,4},{7,5},{8,10},{9,11},{10,... | collective-permute-start | bytes 196616 | tf_op jit(solution)/shard_map/ppermute | solution.py:40
  86.5 5.6 %collective-permute-start.28 = (f32[128,128]{1,0:T(8,128)S(1)}, f32[128,128]{1,0:T(8,128)S(1)}, u32[]{:S(2)}, u32[]{:S(2)}) collective-permute-start(f32[128,128]{1,0:T(8,128)S(1)} %add_add_fusion.1), channel_id=1, source_target_pairs={{0,16},{1,17},{2,18},{3,19},{4,20},{5,21},{6,22},{7,23},{8,24},{9,... | collective-permute-start | bytes 196616 | tf_op jit(solution)/shard_map/ppermute | solution.py:40
  87.4 4.8 %collective-permute-start.27 = (f32[128,128]{1,0:T(8,128)S(1)}, f32[128,128]{1,0:T(8,128)S(1)}, u32[]{:S(2)}, u32[]{:S(2)}) collective-permute-start(f32[128,128]{1,0:T(8,128)S(1)} %add_add_fusion.1), channel_id=1, source_target_pairs={{0,48},{1,49},{2,50},{3,51},{4,52},{5,53},{6,54},{7,55},{8,56},{9,... | collective-permute-start | bytes 196616 | tf_op jit(solution)/shard_map/ppermute | solution.py:40
  89.9 5.8 %collective-permute-start.26 = (f32[128,128]{1,0:T(8,128)S(1)}, f32[128,128]{1,0:T(8,128)S(1)}, u32[]{:S(2)}, u32[]{:S(2)}) collective-permute-start(f32[128,128]{1,0:T(8,128)S(1)} %add_add_fusion.1), channel_id=1, source_target_pairs={{0,32},{1,33},{2,34},{3,35},{4,36},{5,37},{6,38},{7,39},{8,40},{9,... | collective-permute-start | bytes 196616 | tf_op jit(solution)/shard_map/ppermute | solution.py:40
  95.6 5.5 %collective-permute-start.31 = (f32[128,128]{1,0:T(8,128)S(1)}, f32[128,128]{1,0:T(8,128)S(1)}, u32[]{:S(2)}, u32[]{:S(2)}) collective-permute-start(f32[128,128]{1,0:T(8,128)S(1)} %add_add_fusion.g_ref), channel_id=1, source_target_pairs={{0,4},{1,5},{2,6},{3,7},{4,64},{5,65},{6,66},{7,67},{8,12},{9,13},... | collective-permute-start | bytes 196616 | tf_op jit(solution)/shard_map/ppermute | solution.py:40
  96.6 4.5 %collective-permute-start.30 = (f32[128,128]{1,0:T(8,128)S(1)}, f32[128,128]{1,0:T(8,128)S(1)}, u32[]{:S(2)}, u32[]{:S(2)}) collective-permute-start(f32[128,128]{1,0:T(8,128)S(1)} %add_add_fusion.g_ref), channel_id=1, source_target_pairs={{0,68},{1,69},{2,70},{3,71},{4,0},{5,1},{6,2},{7,3},{8,76},{9,77},... | collective-permute-start | bytes 196616 | tf_op jit(solution)/shard_map/ppermute | solution.py:40
  99.0 5.8 %collective-permute-start.29 = (f32[128,128]{1,0:T(8,128)S(1)}, f32[128,128]{1,0:T(8,128)S(1)}, u32[]{:S(2)}, u32[]{:S(2)}) collective-permute-start(f32[128,128]{1,0:T(8,128)S(1)} %add_add_fusion.g_ref), channel_id=1, source_target_pairs={{0,64},{1,65},{2,66},{3,67},{4,68},{5,69},{6,70},{7,71},{8,72},{9,... | collective-permute-start | bytes 196616 | tf_op jit(solution)/shard_map/ppermute | solution.py:40
